TPU v7x, 32 devices: a whole 2x2x4 slice. The times are simulated.
32 devices in a mesh: parts: 2 (over y), seq: 4 (over z), dp: 2 (over x), fsdp: 2 (over core).
Axes of the slice: x: 2, y: 2, z: 4, core: 2. Of those that a mesh axis runs over, the one named last changes fastest.
Arguments:
- inputs: bfloat16 [8, 960, 1024], P(('parts', 'dp', 'fsdp'), 'seq'), parts along dimension 0, may hold values from -6 to 6
- conv_weight: bfloat16 [4096, 128], P(('seq', 'dp', 'fsdp')), may hold values from -0.25 to 0.25
- score_weight: bfloat16 [1024], P(('seq', 'dp', 'fsdp')), may hold values from -0.375 to 0.375
- lengths: int32 [8], P(('parts', 'dp', 'fsdp')), parts along dimension 0, may hold values from 480 to 960, as said below
- offsets: int32 [8, 16], P(('parts', 'dp', 'fsdp')), parts along dimension 0, may hold values from 0 to 956, as said below
- cotangent: bfloat16 [8, 480, 1024], P(('parts', 'dp', 'fsdp'), 'seq'), parts along dimension 0, may hold values from -6 to 6
Outputs:
- x_grad: bfloat16 [8, 960, 1024], P(('parts', 'dp', 'fsdp'), 'seq'), parts along dimension 0
- conv_grad: float32 [8192, 128], P(('parts', 'seq', 'dp', 'fsdp')), parts along dimension 0
- score_grad: float32 [2048], P(('parts', 'seq', 'dp', 'fsdp')), parts along dimension 0
There are 2 independent parts, one for each index of `parts`. A program takes and returns all parts, laid end to end along the dimension named above; an argument that names none is the same for every part. Nothing has to cross between parts.
Inputs may be any that keep to these rules, and one draw needn't show every extreme that they name: `lengths`: each length is a multiple of 4; one stream in every draw uses all 960 characters. In each stream the first offset is 0, the offsets rise strictly, and each is a multiple of 4.
All inputs are finite; a program needn't handle non-finite values.
Results may differ from a plain program's by a relative error of at most 0.0049.
Values may be sent and summed in bfloat16 or wider, within the bound.
No kernel may reach another device: no remote copies, remote signals or barrier semaphores. Data moves between devices by JAX's collectives and lax.ppermute only.
A program may use at most 64 MiB of HBM per device.

v0:
```python
import jax
import jax.numpy as jnp
from jax import lax
from jax.sharding import PartitionSpec as P

GROUPS = 8
KERNEL = 4
GROUP_WIDTH = 128


precise_mode = lax.Precision.HIGHEST


def shifted(value, axis, by):
    devices = lax.axis_size(axis)
    pairs = [(i, i + by) for i in range(devices) if 0 <= i + by < devices]
    return lax.ppermute(value, axis, pairs)


def segment_of(positions, offsets):
    return jnp.sum((offsets[None, :] <= positions[:, None]).astype(jnp.int32), axis=1)


def tap_valid(positions, offsets, lag_steps):
    earlier = positions - lag_steps
    same_file = segment_of(positions, offsets) == segment_of(earlier, offsets)
    return jnp.logical_and(earlier >= 0, same_file)


def mix_backward(hidden, upstream, score_vec):
    row_count = hidden.shape[0]
    width_all = hidden.shape[1]
    pooled_list = []
    logit_list = []
    for block_size in range(1, 5):
        pooled = hidden.reshape(row_count // block_size, block_size, width_all).sum(axis=1) * (
            1.0 / block_size
        )
        pooled_list.append(pooled)
        logit_list.append(
            jnp.repeat(jnp.dot(pooled, score_vec, precision=precise_mode), block_size)
        )
    logits = jnp.stack(logit_list)
    exp_logits = jnp.exp(logits)
    choose_prob = exp_logits / jnp.sum(exp_logits, axis=0)
    mix_grad = jnp.repeat(upstream.astype(jnp.float32) * 0.5, 2, axis=0)
    inner_list = []
    for block_size in range(1, 5):
        pooled = pooled_list[block_size - 1]
        inner = jnp.sum(
            mix_grad.reshape(row_count // block_size, block_size, width_all) * pooled[:, None, :],
            axis=2,
        )
        inner_list.append(inner.reshape(row_count))
    inner_all = jnp.stack(inner_list)
    dlogit = choose_prob * (inner_all - jnp.sum(choose_prob * inner_all, axis=0))
    hidden_grad = jnp.zeros((row_count, width_all), jnp.float32)
    weight_grad = jnp.zeros((width_all,), jnp.float32)
    for block_size in range(1, 5):
        block_logit = (
            dlogit[block_size - 1].reshape(row_count // block_size, block_size).sum(axis=1)
        )
        block_mix = (
            (choose_prob[block_size - 1][:, None] * mix_grad)
            .reshape(row_count // block_size, block_size, width_all)
            .sum(axis=1)
        )
        block_term = (block_mix + block_logit[:, None] * score_vec[None, :]) * (1.0 / block_size)
        hidden_grad = hidden_grad + jnp.repeat(block_term, block_size, axis=0)
        weight_grad = weight_grad + jnp.dot(
            block_logit, pooled_list[block_size - 1], precision=precise_mode
        )
    return (hidden_grad, weight_grad)


def per_device(inputs, conv_weight, score_weight, lengths, offsets, cotangent):
    local_rows = inputs.shape[1]
    width_all = inputs.shape[2]
    kernel_flat, score_full = (
        lax.all_gather(conv_weight, ("seq", "dp", "fsdp"), axis=0, tiled=True),
        lax.all_gather(score_weight, ("seq", "dp", "fsdp"), axis=0, tiled=True),
    )
    kernel_full = kernel_flat.reshape(GROUPS, KERNEL, GROUP_WIDTH, GROUP_WIDTH)
    score_vec = score_full.astype(jnp.float32)
    start_row = lax.axis_index("seq") * local_rows
    positions = start_row + jnp.arange(local_rows, dtype=jnp.int32)
    own_rows = inputs[0]
    file_starts = offsets[0]
    valid = (positions < lengths[0]).astype(jnp.float32)
    left_rows = shifted(own_rows[local_rows - (KERNEL - 1) :], "seq", 1)
    padded = jnp.concatenate([left_rows, own_rows], axis=0)
    windows = []
    hidden = jnp.zeros((local_rows, GROUPS, GROUP_WIDTH), jnp.float32)
    for tap_index in range(KERNEL):
        window = padded[KERNEL - 1 - tap_index : KERNEL - 1 - tap_index + local_rows]
        keep = tap_valid(positions, file_starts, tap_index)
        window = jnp.where(keep[:, None], window, jnp.zeros_like(window)).reshape(
            local_rows, GROUPS, GROUP_WIDTH
        )
        windows.append(window)
        hidden = hidden + jnp.einsum(
            "ngc,gco->ngo", window, kernel_full[:, tap_index], preferred_element_type=jnp.float32
        )
    hidden = hidden.reshape(local_rows, width_all) * valid[:, None]
    hidden_grad, weight_grad = mix_backward(hidden, cotangent[0], score_vec)
    hidden_low = (hidden_grad * valid[:, None]).astype(jnp.bfloat16)
    right_rows = shifted(hidden_low[: KERNEL - 1], "seq", -1)
    grad_padded = jnp.concatenate([hidden_low, right_rows], axis=0)
    hidden_groups = hidden_low.reshape(local_rows, GROUPS, GROUP_WIDTH)
    input_grad = jnp.zeros((local_rows, GROUPS, GROUP_WIDTH), jnp.float32)
    kernel_terms = []
    for tap_index in range(KERNEL):
        window = grad_padded[tap_index : tap_index + local_rows]
        keep = tap_valid(positions + tap_index, file_starts, tap_index)
        window = jnp.where(keep[:, None], window, jnp.zeros_like(window)).reshape(
            local_rows, GROUPS, GROUP_WIDTH
        )
        input_grad = input_grad + jnp.einsum(
            "ngo,gco->ngc", window, kernel_full[:, tap_index], preferred_element_type=jnp.float32
        )
        kernel_terms.append(
            jnp.einsum(
                "ngc,ngo->gco",
                windows[tap_index],
                hidden_groups,
                preferred_element_type=jnp.float32,
            )
        )
    input_grad = input_grad.reshape(local_rows, width_all).astype(jnp.bfloat16)[None]
    kernel_part = jnp.stack(kernel_terms, axis=1).reshape(
        GROUPS * KERNEL * GROUP_WIDTH, GROUP_WIDTH
    )
    kernel_grad, score_grad = (
        lax.psum_scatter(kernel_part, ("seq", "dp", "fsdp"), scatter_dimension=0, tiled=True),
        lax.psum_scatter(weight_grad, ("seq", "dp", "fsdp"), scatter_dimension=0, tiled=True),
    )
    return (input_grad, kernel_grad, score_grad)


def solution(mesh):
    placed = (
        P(("parts", "dp", "fsdp"), "seq", None),
        P(("seq", "dp", "fsdp"), None),
        P(("seq", "dp", "fsdp")),
        P(("parts", "dp", "fsdp")),
        P(("parts", "dp", "fsdp"), None),
        P(("parts", "dp", "fsdp"), "seq", None),
    )
    return jax.shard_map(
        per_device,
        mesh=mesh,
        in_specs=placed,
        out_specs=(
            P(("parts", "dp", "fsdp"), "seq", None),
            P(("parts", "seq", "dp", "fsdp"), None),
            P(("parts", "seq", "dp", "fsdp")),
        ),
        check_vma=False,
    )
```

profile of v0, /device:TPU:0, one launch (start us, length us, event | category | flops | bytes accessed | tf_op | source)
XLA Modules:
  0.0 173.1 jit_solution(12926582862866578665)
XLA Ops:
  8.7 4.9 %collective-permute-start = (bf16[3,1024]{1,0:T(4,128)(2,1)S(1)}, bf16[3,1024]{1,0:T(4,128)(2,1)S(1)}, u32[]{:S(2)}, u32[]{:S(2)}) collective-permute-start(bf16[3,1024]{1,0:T(4,128)(2,1)S(1)} %slice_bitcast_fusion.12), channel_id=1, source_target_pairs={{0,4},{4,8},{8,12},{1,5},{5,9},{9,13},{2,6},{6,10},{10,14},{3,7},{... | collective-permute-start | bytes 18440 | tf_op jit(solution)/shard_map/ppermute | solution.py:17
  17.1 31.5 %all-reduce = bf16[1024]{0:T(1024)(128)(2,1)S(1)} all-reduce(bf16[1024]{0:T(1024)(128)(2,1)S(1)} %dynamic-update-slice), channel_id=1, replica_groups=mesh['parts'=2,'seq'=4,'dp'=2,'fsdp'=2] {'seq','dp','fsdp'}, use_global_device_ids=true, to_apply=%add | all-reduce | flops 1024 | bytes 4096
  53.2 1.7 fusion.58
  56.6 1.4 reshape.367
  59.7 1.9 %multiply_reduce_fusion.6 = f32[60,1024]{1,0:T(8,128)S(1)} fusion(f32[60,4,1024]{2,1,0:T(4,128)} %reshape.369, f32[60,4]{1,0:T(8,128)S(1)} %copy.109), kind=kLoop, calls=%fused_computation.35 | loop fusion | flops 430080 | bytes 1229760 | tf_op jit(solution)/shard_map/reduce_sum | solution.py:36
  69.0 2.0 %broadcast_in_dim.113 = f32[80,3,1024]{2,1,0:T(4,128)} reshape(f32[120,2,1024]{2,1,0:T(2,128)S(1)} %broadcast_in_dim.112) | data formatting | bytes 1966080 | tf_op jit(solution)/shard_map/broadcast_in_dim | solution.py:46
  76.2 1.4 mul.302
  77.6 4.5 %multiply_reduce_fusion.4 = (f32[120,1024]{1,0:T(8,128)}, f32[120,1024]{1,0:T(8,128)}) fusion(f32[120,2]{1,0:T(8,128)S(1)} %mul.288, f32[120,1024]{1,0:T(8,128)S(1)} %get-tuple-element.29, f32[120,2]{1,0:T(8,128)} %mul.302), kind=kLoop, calls=%fused_computation.33 | loop fusion | flops 737280 | bytes 1476480 | tf_op jit(solution)/shard_map/reduce_sum | solution.py:66
  83.4 3.3 %multiply_reduce_fusion = (f32[80,1024]{1,0:T(8,128)}, f32[80,3]{1,0:T(8,128)S(1)}) fusion(f32[80,3,1024]{2,1,0:T(4,128)} %broadcast_in_dim.113, f32[80,3]{1,0:T(8,128)S(1)} %mul.295, f32[80,1024]{1,0:T(8,128)} %broadcast_multiply_fusion), kind=kLoop, calls=%fused_computation.7 | loop fusion | flops 900880 | bytes 1640320 | tf_op jit(solution)/shard_map/reduce_sum | solution.py:66
  86.9 1.3 multiply_bitcast_fusion
  91.2 1.5 reshape.372
  93.1 1.4 reshape.373
  95.6 1.3 broadcast_in_dim.114
  96.9 2.9 %reshape.371 = f32[240,8,128]{2,1,0:T(8,128)} reshape(f32[120,2,1024]{2,1,0:T(2,128)} %broadcast_in_dim.114) | data formatting | bytes 1966080 | tf_op jit(solution)/shard_map/reshape | solution.py:69
  99.9 2.9 %fusion.8 = bf16[240,8,128]{2,0,1:T(8,128)(2,1)S(1)} fusion(f32[240,8,128]{2,1,0:T(8,128)} %reshape.373, f32[240,8,128]{2,1,0:T(8,128)} %reshape.372, f32[240,8,128]{2,1,0:T(8,128)} %reshape.371, f32[240,8,128]{2,1,0:T(8,128)} %copy-done, f32[240]{0:T(256)S(1)} %copy-done.30, f32[8,128]{1,0:T(8,128)S(1)} %copy-done.33, f32[240]{0:T(256)S(1)} %bitcast.163, ...), kind=kLoop, calls=%fused_computation.27 | loop fusion | flops 1966080 | bytes 4430656 | tf_op jit(solution)/shard_map/convert_element_type | solution.py:106
  105.6 1.5 copy.122
  107.7 1.6 reshape.374
  109.4 1.4 reshape.376
  110.8 1.5 reshape.377
  112.3 1.7 reshape.375
  114.0 2.3 %multiply_convert_fusion = bf16[240,1024]{1,0:T(8,128)(2,1)S(1)} fusion(f32[240,1024]{1,0:T(8,128)} %reshape.377, f32[240,1024]{1,0:T(8,128)} %reshape.376, f32[240,1024]{1,0:T(8,128)} %reshape.375, f32[240,1024]{1,0:T(8,128)S(1)} %copy-done.22, f32[1024]{0:T(1024)S(1)} %get-tuple-element.33, f32[240]{0:T(256)S(1)} %bitcast.164, f32[240]{0:T(256)S(1)} %bitcast.162, ...), kind=kLoop, calls=%fused_computation.31 | loop fusion | flops 1966080 | bytes 4430656 | tf_op jit(solution)/shard_map/convert_element_type | solution.py:106
  116.4 1.4 collective-permute-start.1
  119.8 30.1 %all-reduce.1 = f32[1024]{0:T(1024)S(1)} all-reduce(f32[1024]{0:T(1024)S(1)} %add_add_fusion), channel_id=3, replica_groups=mesh['parts'=2,'seq'=4,'dp'=2,'fsdp'=2] {'seq','dp','fsdp'}, use_global_device_ids=true, to_apply=%region_24.25.clone | all-reduce | flops 1024 | bytes 8192
  153.5 12.8 %reduce-scatter.2.cloned.1.call-done = f32[256,128]{1,0:T(8,128)} async-done(((f32[4096,128]{1,0:T(8,128)}), f32[256,128]{1,0:T(8,128)}) %reduce-scatter.2.cloned.1.call-update) | async-done | bytes 131088 | tf_op jit(solution)/shard_map/reduce_scatter | solution.py:134
  (188 shorter events, 37.9 us)
Async XLA Ops:
  7.2 45.5 %copy-start.23 = (bf16[1,240,1024]{2,1,0:T(8,128)(2,1)S(1)}, bf16[1,240,1024]{2,1,0:T(8,128)(2,1)}, u32[]{:S(2)}) copy-start(bf16[1,240,1024]{2,1,0:T(8,128)(2,1)} %param.6) | copy-start | bytes 1474564
  7.2 46.0 %all-gather.2.cloned.1.call-start = ((), (), s32[]{:S(2)}) async-start(), calls=%async_computation.1 | async-start | bytes 1114112 | tf_op jit(solution)/shard_map/all_gather | solution.py:80
  7.9 158.3 %reduce-scatter.2.cloned.1.call-start = ((), (), s32[]{:S(2)}) async-start(), calls=%async_computation.2 | async-start | bytes 2228224 | tf_op jit(solution)/shard_map/reduce_scatter | solution.py:134
  8.7 44.0 %collective-permute-start = (bf16[3,1024]{1,0:T(4,128)(2,1)S(1)}, bf16[3,1024]{1,0:T(4,128)(2,1)S(1)}, u32[]{:S(2)}, u32[]{:S(2)}) collective-permute-start(bf16[3,1024]{1,0:T(4,128)(2,1)S(1)} %slice_bitcast_fusion.12), channel_id=1, source_target_pairs={{0,4},{4,8},{8,12},{1,5},{5,9},{9,13},{2,6},{6,10},{10,14},{3,7},{... | collective-permute-start | bytes 18440 | tf_op jit(solution)/shard_map/ppermute | solution.py:17
  50.6 20.4 %copy-start.29 = (f32[240]{0:T(256)}, f32[240]{0:T(256)S(1)}, u32[]{:S(2)}) copy-start(f32[240]{0:T(256)S(1)} %get-tuple-element.42) | copy-start | bytes 2884
  50.6 2.6 %copy-start.37 = (pred[240]{0:T(512)(128)(4,1)}, pred[240]{0:T(512)(128)(4,1)S(1)}, u32[]{:S(2)}) copy-start(pred[240]{0:T(512)(128)(4,1)S(1)} %fusion.71) | copy-start | bytes 724
  53.2 2.7 %copy-start.14 = (bf16[30,8,8,128]{3,2,1,0:T(8,128)(2,1)}, bf16[30,8,8,128]{3,2,1,0:T(8,128)(2,1)S(1)}, u32[]{:S(2)}) copy-start(bf16[30,8,8,128]{3,2,1,0:T(8,128)(2,1)S(1)} %get-tuple-element.25) | copy-start | bytes 1474564
  64.2 2.9 %copy-start.24 = (bf16[1,120,1024]{2,1,0:T(8,128)(2,1)S(1)}, bf16[1,120,1024]{2,1,0:T(8,128)(2,1)}, u32[]{:S(2)}) copy-start(bf16[1,120,1024]{2,1,0:T(8,128)(2,1)} %param.11) | copy-start | bytes 737284
  69.0 17.8 %copy-start = (f32[240,8,128]{2,1,0:T(8,128)}, f32[240,8,128]{2,1,0:T(8,128)S(1)}, u32[]{:S(2)}) copy-start(f32[240,8,128]{2,1,0:T(8,128)S(1)} %reshape.370) | copy-start | bytes 2949124
  71.7 3.5 %copy-start.27 = (f32[1,240]{1,0:T(1,128)}, f32[1,240]{1,0:T(1,128)S(1)}, u32[]{:S(2)}) copy-start(f32[1,240]{1,0:T(1,128)S(1)} %fusion.5) | copy-start | bytes 2884
  82.1 4.8 %copy-start.30 = (f32[240]{0:T(256)S(1)}, f32[240]{0:T(256)}, u32[]{:S(2)}) copy-start(f32[240]{0:T(256)} %copy-done.29) | copy-start | bytes 2884
  82.1 4.8 %copy-start.39 = (f32[240]{0:T(256)S(1)}, f32[240]{0:T(256)}, u32[]{:S(2)}) copy-start(f32[240]{0:T(256)} %reshape.382) | copy-start | bytes 2884
  96.9 3.0 %copy-start.33 = (f32[8,128]{1,0:T(8,128)S(1)}, f32[8,128]{1,0:T(8,128)}, u32[]{:S(2)}) copy-start(f32[8,128]{1,0:T(8,128)} %get-tuple-element.32) | copy-start | bytes 12292
  96.9 3.0 %copy-start.36 = (f32[1,240]{1,0:T(1,128)S(1)}, f32[1,240]{1,0:T(1,128)}, u32[]{:S(2)}) copy-start(f32[1,240]{1,0:T(1,128)} %get-tuple-element.30) | copy-start | bytes 2884
  99.9 2.9 %copy-start.15 = (bf16[30,8,8,128]{3,2,1,0:T(8,128)(2,1)S(1)}, bf16[30,8,8,128]{3,2,1,0:T(8,128)(2,1)}, u32[]{:S(2)}) copy-start(bf16[30,8,8,128]{3,2,1,0:T(8,128)(2,1)} %copy-done.14) | copy-start | bytes 1474564
  114.0 3.8 %copy-start.17 = (f32[60,1024]{1,0:T(8,128)S(1)}, f32[60,1024]{1,0:T(8,128)}, u32[]{:S(2)}) copy-start(f32[60,1024]{1,0:T(8,128)} %copy-done.16) | copy-start | bytes 737284
  114.0 4.1 %copy-start.7 = (f32[80,1024]{1,0:T(8,128)S(1)}, f32[80,1024]{1,0:T(8,128)}, u32[]{:S(2)}) copy-start(f32[80,1024]{1,0:T(8,128)} %copy-done.6) | copy-start | bytes 983044
  114.0 4.4 %copy-start.5 = (f32[120,1024]{1,0:T(8,128)S(1)}, f32[120,1024]{1,0:T(8,128)}, u32[]{:S(2)}) copy-start(f32[120,1024]{1,0:T(8,128)} %copy-done.4) | copy-start | bytes 1474564
  114.0 4.7 %copy-start.20 = (f32[8,30,8,128]{3,2,1,0:T(8,128)S(1)}, f32[8,30,8,128]{3,2,1,0:T(8,128)}, u32[]{:S(2)}) copy-start(f32[8,30,8,128]{3,2,1,0:T(8,128)} %get-tuple-element.20) | copy-start | bytes 2949124
  116.4 3.0 %copy-start.19 = (bf16[4096,128]{1,0:T(8,128)(2,1)S(1)}, bf16[4096,128]{1,0:T(8,128)(2,1)}, u32[]{:S(2)}) copy-start(bf16[4096,128]{1,0:T(8,128)(2,1)} %all-gather.2.cloned.1.call-done) | copy-start | bytes 3145732
  116.4 34.1 %collective-permute-start.1 = (bf16[3,1024]{1,0:T(4,128)(2,1)S(1)}, bf16[3,1024]{1,0:T(4,128)(2,1)S(1)}, u32[]{:S(2)}, u32[]{:S(2)}) collective-permute-start(bf16[3,1024]{1,0:T(4,128)(2,1)S(1)} %slice.104), channel_id=1, source_target_pairs={{4,0},{8,4},{12,8},{5,1},{9,5},{13,9},{6,2},{10,6},{14,10},{7,3},{... | collective-permute-start | bytes 18440 | tf_op jit(solution)/shard_map/ppermute | solution.py:17
  118.7 31.8 %copy-start.40 = (pred[240]{0:T(512)(128)(4,1)S(1)}, pred[240]{0:T(512)(128)(4,1)}, u32[]{:S(2)}) copy-start(pred[240]{0:T(512)(128)(4,1)} %get-tuple-element.34) | copy-start | bytes 724
  118.7 31.8 %copy-start.41 = (pred[240]{0:T(512)(128)(4,1)S(1)}, pred[240]{0:T(512)(128)(4,1)}, u32[]{:S(2)}) copy-start(pred[240]{0:T(512)(128)(4,1)} %get-tuple-element.35) | copy-start | bytes 724
  118.8 31.8 %copy-start.42 = (pred[240]{0:T(512)(128)(4,1)S(1)}, pred[240]{0:T(512)(128)(4,1)}, u32[]{:S(2)}) copy-start(pred[240]{0:T(512)(128)(4,1)} %get-tuple-element.36) | copy-start | bytes 724
  (23 other events, 34.7 us)
Sparse Core Ops, SparseCore 0:
  10.2 40.6 all-gather.1
  107.2 58.9 reduce-scatter.1
where the time goes:
time: 174 us; the launch traced here: 173 us
  blocking collectives  61.6 us (35%)
  local copies, waits for them, and re-layouts  39.8 us (23%)
  other arithmetic  26 us (15%)
  between operations  16.8 us (10%)
  waiting for transfers between devices  13.5 us (8%)
  matrix products  8.95 us (5%)
  starting transfers between devices  6.41 us (4%)
    unnamed x2, blocking collectives  61.6 us
    reduce_scatter x1, waiting for transfers between devices, per_device(): lax.psum_scatter(kernel_part, ('seq', 'dp', 'fsdp'), scatter_dimension=0,...  12.8 us
    reshape x6, local copies, waits for them, and re-layouts, mix_backward(): hidden_grad = hidden_grad + jnp.repeat(block_term, block_size, axis=0)  10.4 us
    reduce_sum x3, other arithmetic, mix_backward(): block_mix = (choose_prob[block_size - 1][:, None] * mix_grad).reshape(row...  8.34 us
    unnamed x92, local copies, waits for them, and re-layouts  6.74 us
    ppermute x2, starting transfers between devices, shifted(): return lax.ppermute(value, axis, pairs)  6.34 us
    convert_element_type x2, other arithmetic, per_device(): hidden_low = (hidden_grad * valid[:, None]).astype(jnp.bfloat16)  5.24 us
    reduce_sum x3, other arithmetic, mix_backward(): hidden.reshape(row_count // block_size, block_size, width_all).sum(axis=1)  4.08 us
  transfers between devices with their start and end apart: 4, of which 1 were waited for; matrix products, arithmetic and copies ran while one was open for 12% of the time, Pallas kernels for 0%

commit v1 on v0

--- a/solution.py
+++ b/solution.py
@@ -1,6 +1,10 @@
+import functools
+
 import jax
 import jax.numpy as jnp
 from jax import lax
+from jax.experimental import pallas as pl
+from jax.experimental.pallas import tpu as pltpu
 from jax.sharding import PartitionSpec as P
 
 GROUPS = 8
@@ -73,7 +77,7 @@
     return (hidden_grad, weight_grad)
 
 
-def per_device(inputs, conv_weight, score_weight, lengths, offsets, cotangent):
+def per_device_general(inputs, conv_weight, score_weight, lengths, offsets, cotangent):
     local_rows = inputs.shape[1]
     width_all = inputs.shape[2]
     kernel_flat, score_full = (
@@ -137,6 +141,382 @@
     return (input_grad, kernel_grad, score_grad)
 
 
+SLOTS = 4
+HALF = SLOTS * GROUP_WIDTH
+PAD = 8
+SCORE_ROW = 2 * GROUP_WIDTH
+HALO_ROW = SCORE_ROW + 16
+BF = jnp.bfloat16
+F32 = jnp.float32
+
+
+def lanes(slot):
+    return slice(slot * GROUP_WIDTH, (slot + 1) * GROUP_WIDTH)
+
+
+def group_lanes(group):
+    return pl.ds(pl.multiple_of(group * GROUP_WIDTH, GROUP_WIDTH), GROUP_WIDTH)
+
+
+def slot_group(seq, slot, parity):
+    return 2 * lax.rem(seq - slot + 2 * SLOTS, SLOTS) + parity
+
+
+def call(body, out_shape, scratch=(), smem=0, cost=None):
+    def run(*args):
+        specs = [pl.BlockSpec(memory_space=pltpu.SMEM)] * smem
+        specs += [pl.BlockSpec(memory_space=pltpu.VMEM)] * (len(args) - smem)
+        return pl.pallas_call(
+            body,
+            out_shape=out_shape,
+            in_specs=specs,
+            out_specs=jax.tree.map(lambda _: pl.BlockSpec(memory_space=pltpu.VMEM), out_shape),
+            scratch_shapes=list(scratch),
+            cost_estimate=cost,
+            compiler_params=pltpu.CompilerParams(vmem_limit_bytes=48 * 1024 * 1024),
+        )(*args)
+
+    return run
+
+
+def pack_kernel(off_ref, len_ref, x_ref, c_ref, w_ref, score_ref, mx, mc, mw, mw1, md):
+    rows = x_ref.shape[1]
+    pairs = c_ref.shape[1]
+    s, d, f = (lax.axis_index(name) for name in ("seq", "dp", "fsdp"))
+    for j in range(SLOTS):
+        col = group_lanes(slot_group(s, j, 1 - d))
+        mx[:, lanes(j)] = x_ref[0, :, col]
+        mc[0:pairs, lanes(j)] = c_ref[0, :, col]
+        next_other = group_lanes(slot_group(s + 1, j, 1 - d))
+        md[:, lanes(j)] = x_ref[0, rows - PAD :, next_other]
+        next_own = group_lanes(slot_group(s + 1, j, d))
+        mw1[HALO_ROW + PAD * j : HALO_ROW + PAD * (j + 1), :] = x_ref[0, rows - PAD :, next_own]
+    lane = lax.broadcasted_iota(jnp.int32, (PAD, GROUP_WIDTH), 1)
+    start = s * rows
+    info = jnp.zeros((PAD, GROUP_WIDTH), jnp.int32)
+    for i in range(off_ref.shape[1]):
+        info = jnp.where(lane == i, jnp.clip(off_ref[0, i] - start, -4, rows + PAD), info)
+    info = jnp.where(lane == off_ref.shape[1], jnp.clip(len_ref[0] - start, 0, rows), info)
+    mc[pairs:, :] = jnp.zeros((mc.shape[0] - pairs, HALF), BF)
+    mc[pairs : pairs + PAD, lanes(0)] = (info.astype(F32) * 0.25).astype(BF)
+    value = score_ref[...].astype(F32)
+    both = jnp.concatenate([value, value], axis=1)
+    half = lax.broadcasted_iota(jnp.int32, (16, GROUP_WIDTH), 1) // (GROUP_WIDTH // 2)
+    row = lax.broadcasted_iota(jnp.int32, (16, GROUP_WIDTH), 0)
+    block = jnp.where((half == f) & (row == 0), jnp.broadcast_to(both, (16, GROUP_WIDTH)), 0.0)
+    for ref in (mw, mw1):
+        ref[0:SCORE_ROW, :] = w_ref[...]
+        ref[SCORE_ROW:HALO_ROW, :] = block.astype(BF)
+
+
+def row_info(mc_ref, pairs, files, extent):
+    info = mc_ref[pairs : pairs + PAD, lanes(0)].astype(F32)[0:1] * 4.0
+    lane = lax.broadcasted_iota(jnp.int32, (1, GROUP_WIDTH), 1)
+    length = jnp.sum(jnp.where(lane == files, info, 0.0), axis=1, keepdims=True)
+    pos = lax.broadcasted_iota(jnp.int32, (extent, GROUP_WIDTH), 0).astype(F32)
+    starts = jnp.where((lane < files) & (info <= pos), info, -4096.0)
+    since = pos - jnp.max(starts, axis=1, keepdims=True)
+    return since, (pos < length).astype(F32)
+
+
+def block_weights(rows):
+    q = lax.broadcasted_iota(jnp.int32, (rows, GROUP_WIDTH), 0)
+    r = lax.broadcasted_iota(jnp.int32, (rows, GROUP_WIDTH), 1)
+
+    def over(value, size):
+        if size == 1:
+            return value
+        if size == 3:
+            return lax.shift_right_logical(value * 21846, 16)
+        return lax.shift_right_logical(value, size // 2)
+
+    return [
+        [
+            jnp.where(over(q, size) == over(2 * r + odd, size), 1.0 / size, 0.0).astype(F32)
+            for size in range(1, 5)
+        ]
+        for odd in range(2)
+    ]
+
+
+def windows_of(tail, rows_value, since):
+    rows = rows_value.shape[0]
+    padded = jnp.concatenate([tail.astype(F32), rows_value.astype(F32)], axis=0)
+    out = [rows_value]
+    for lag in range(1, KERNEL):
+        moved = pltpu.roll(padded, lag, 0)[PAD:]
+        out.append(jnp.where(since[:rows] >= lag, moved, 0.0).astype(BF))
+    return out
+
+
+def stream_parts(x_ref, mx_ref, w1_ref, md_ref, j, stream):
+    s, d = lax.axis_index("seq"), lax.axis_index("dp")
+    if stream == 0:
+        return (
+            w1_ref[HALO_ROW + PAD * j : HALO_ROW + PAD * (j + 1), :],
+            x_ref[0, :, group_lanes(slot_group(s, j, d))],
+        )
+    return md_ref[:, lanes(j)], mx_ref[:, lanes(j)]
+
+
+def kernel_halves(w_refs, j):
+    f = lax.axis_index("fsdp")
+    mine, theirs = w_refs[j][0:SCORE_ROW, :], w_refs[SLOTS + j][0:SCORE_ROW, :]
+    first = jnp.full((SCORE_ROW, GROUP_WIDTH), f, jnp.int32) == 0
+    return jnp.where(first, mine, theirs), jnp.where(first, theirs, mine)
+
+
+def nt(a, b):
+    return lax.dot_general(a, b, (((1,), (1,)), ((), ())), preferred_element_type=F32)
+
+
+def two_terms(value):
+    high = value.astype(BF)
+    return high, (value - high.astype(F32)).astype(BF)
+
+
+def hidden_kernel(files, x_ref, c_ref, mx_ref, mc_ref, mcr_ref, md_ref, *refs):
+    w_refs, (h_out, l_out, r_out) = refs[: 2 * SLOTS], refs[2 * SLOTS :]
+    rows, pairs = x_ref.shape[1], c_ref.shape[1]
+    s, d = lax.axis_index("seq"), lax.axis_index("dp")
+    infos = [row_info(ref, pairs, files, rows) for ref in (mc_ref, mcr_ref)]
+    gram = [jnp.zeros((rows, GROUP_WIDTH), F32) for _ in range(2)]
+    for j in range(SLOTS):
+        low, high = kernel_halves(w_refs, j)
+        score = (
+            w_refs[j][SCORE_ROW:HALO_ROW, :].astype(F32)
+            + w_refs[SLOTS + j][SCORE_ROW:HALO_ROW, :].astype(F32)
+        )[0:PAD]
+        for stream in range(2):
+            since, valid = infos[stream]
+            tail, value = stream_parts(x_ref, mx_ref, w_refs[1], md_ref, j, stream)
+            win = windows_of(tail, value, since)
+            hidden = jnp.dot(
+                jnp.concatenate(win[:2], axis=1), low, preferred_element_type=F32
+            ) + jnp.dot(jnp.concatenate(win[2:], axis=1), high, preferred_element_type=F32)
+            hidden = hidden * valid
+            h_out[stream, :, lanes(j)] = hidden
+            if stream == 0:
+                cot = c_ref[0, :, group_lanes(slot_group(s, j, d))]
+            else:
+                cot = mcr_ref[0:pairs, lanes(j)]
+            left = jnp.concatenate([cot.astype(F32), score], axis=0).astype(BF)
+            l_out[stream, :, lanes(j)] = left
+            a, b = two_terms(hidden)
+            gram[stream] = gram[stream] + nt(a, left) + nt(b, left)
+    weights = block_weights(rows)
+    for stream in range(2):
+        column = gram[stream][:, pairs : pairs + 1]
+        inner = [
+            jnp.sum(weights[odd][b] * gram[stream], axis=0, keepdims=True) * 0.5
+            for odd in range(2)
+            for b in range(4)
+        ]
+        logit = [
+            jnp.sum(weights[odd][b] * column, axis=0, keepdims=True)
+            for odd in range(2)
+            for b in range(4)
+        ]
+        r_out[stream] = jnp.concatenate(inner + logit, axis=0)
+
+
+def mix_kernel(files, x_ref, mx_ref, md_ref, w1_ref, mc_ref, mcr_ref, h_ref, l_ref, r_ref, rr_ref,
+               hg_out, hh_out, mine_out, send_out):
+    rows = x_ref.shape[1]
+    pairs = rows // 2
+    f = lax.axis_index("fsdp")
+    weights = block_weights(rows)
+    infos = [row_info(ref, pairs, files, rows) for ref in (mc_ref, mcr_ref)]
+    lane = lax.broadcasted_iota(jnp.int32, (rows, GROUP_WIDTH), 1)
+    columns = []
+    for stream in range(2):
+        total = r_ref[stream] + rr_ref[1 - stream]
+        spread = jnp.zeros((rows, GROUP_WIDTH), F32)
+        carry = jnp.zeros((rows, GROUP_WIDTH), F32)
+        for odd in range(2):
+            inner = [total[4 * odd + b : 4 * odd + b + 1] for b in range(4)]
+            logit = [total[8 + 4 * odd + b : 8 + 4 * odd + b + 1] for b in range(4)]
+            top = jnp.maximum(jnp.maximum(logit[0], logit[1]), jnp.maximum(logit[2], logit[3]))
+            powers = [jnp.exp(v - top) for v in logit]
+            scale = 1.0 / (powers[0] + powers[1] + powers[2] + powers[3])
+            choose = [v * scale for v in powers]
+            mean = sum(c * m for c, m in zip(choose, inner))
+            for b in range(4):
+                spread = spread + weights[odd][b] * (choose[b] * 0.5)
+                carry = carry + weights[odd][b] * (choose[b] * (inner[b] - mean))
+        valid = infos[stream][1]
+        e = jnp.sum(carry, axis=1, keepdims=True)
+        columns.append(e)
+        mixed = jnp.where(lane == pairs, e, spread) * valid
+        a, b = two_terms(mixed)
+        for j in range(SLOTS):
+            left = l_ref[stream, :, lanes(j)]
+            grad = jnp.dot(a, left, preferred_element_type=F32) + jnp.dot(
+                b, left, preferred_element_type=F32
+            )
+            grad = grad.astype(BF)
+            hg_out[stream, :, lanes(j)] = grad
+            hh_out[PAD * stream : PAD * (stream + 1), lanes((j + SLOTS - 1) % SLOTS)] = grad[0:PAD]
+    first = jnp.full((SCORE_ROW, GROUP_WIDTH), f, jnp.int32) == 0
+    row = lax.broadcasted_iota(jnp.int32, (PAD, GROUP_WIDTH), 0)
+    for j in range(SLOTS):
+        low = jnp.zeros((SCORE_ROW, GROUP_WIDTH), F32)
+        high = jnp.zeros((SCORE_ROW, GROUP_WIDTH), F32)
+        score = jnp.zeros((1, GROUP_WIDTH), F32)
+        for stream in range(2):
+            tail, value = stream_parts(x_ref, mx_ref, w1_ref, md_ref, j, stream)
+            win = windows_of(tail, value, infos[stream][0])
+            grad = hg_out[stream, :, lanes(j)]
+            dims = (((0,), (0,)), ((), ()))
+            low = low + lax.dot_general(
+                jnp.concatenate(win[:2], axis=1), grad, dims, preferred_element_type=F32
+            )
+            high = high + lax.dot_general(
+                jnp.concatenate(win[2:], axis=1), grad, dims, preferred_element_type=F32
+            )
+            score = score + jnp.sum(
+                columns[stream] * h_ref[stream, :, lanes(j)], axis=0, keepdims=True
+            )
+        base = j * (SCORE_ROW + PAD)
+        score = jnp.where(row == 0, jnp.broadcast_to(score, row.shape), 0.0)
+        mine_out[base : base + SCORE_ROW, :] = jnp.where(first, low, high)
+        send_out[base : base + SCORE_ROW, :] = jnp.where(first, high, low)
+        mine_out[base + SCORE_ROW : base + SCORE_ROW + PAD, :] = score
+        send_out[base + SCORE_ROW : base + SCORE_ROW + PAD, :] = score
+
+
+def add_kernel(mine_ref, got_ref, *outs):
+    for j, out in zip(range(1, SLOTS), outs):
+        base = j * (SCORE_ROW + PAD)
+        total = mine_ref[base : base + SCORE_ROW + PAD, :] + got_ref[base : base + SCORE_ROW + PAD, :]
+        out[0:SCORE_ROW, :] = total[0:SCORE_ROW].astype(BF)
+        a, b = two_terms(total[SCORE_ROW:])
+        out[SCORE_ROW:, :] = jnp.concatenate([a.astype(F32), b.astype(F32)], axis=0).astype(BF)
+
+
+def sum_kernel(mine_ref, got_ref, z1, z2, z3, out_ref, score_ref):
+    f = lax.axis_index("fsdp")
+    total = mine_ref[0 : SCORE_ROW + PAD, :] + got_ref[0 : SCORE_ROW + PAD, :]
+    grad, score = total[0:SCORE_ROW], total[SCORE_ROW:]
+    for ref in (z1, z2, z3):
+        grad = grad + ref[0:SCORE_ROW, :].astype(F32)
+        pair = ref[SCORE_ROW:, :].astype(F32)
+        score = score + pair[0:PAD] + pair[PAD:]
+    out_ref[...] = grad
+    half = GROUP_WIDTH // 2
+    score_ref[...] = jnp.where(
+        jnp.full((1, half), f, jnp.int32) == 0, score[0:1, :half], score[0:1, half:]
+    )
+
+
+def input_kernel(files, hg_ref, hh_ref, mc_ref, mcr_ref, *refs):
+    w_refs, outs = refs[: 2 * SLOTS], refs[2 * SLOTS :]
+    rows = hg_ref.shape[1]
+    pairs = rows // 2
+    for stream, mref in enumerate((mc_ref, mcr_ref)):
+        since, _ = row_info(mref, pairs, files, rows + PAD)
+        for j in range(SLOTS):
+            padded = jnp.concatenate(
+                [
+                    hg_ref[stream, :, lanes(j)].astype(F32),
+                    hh_ref[PAD * stream : PAD * (stream + 1), lanes(j)].astype(F32),
+                ],
+                axis=0,
+            )
+            halves = kernel_halves(w_refs, j)
+            total = jnp.zeros((rows, GROUP_WIDTH), F32)
+            for lag in range(KERNEL):
+                if lag == 0:
+                    window = padded[:rows].astype(BF)
+                else:
+                    kept = jnp.where(since >= lag, padded, 0.0)
+                    window = pltpu.roll(kept, rows + PAD - lag, 0)[:rows].astype(BF)
+                part = halves[lag // 2][GROUP_WIDTH * (lag % 2) : GROUP_WIDTH * (lag % 2 + 1)]
+                total = total + nt(window, part)
+            outs[stream][:, lanes(j)] = total.astype(BF)
+
+
+def place_kernel(own_ref, got_ref, out_ref):
+    s, d = lax.axis_index("seq"), lax.axis_index("dp")
+    for j in range(SLOTS):
+        out_ref[0, :, group_lanes(slot_group(s, j, d))] = own_ref[:, lanes(j)]
+        out_ref[0, :, group_lanes(slot_group(s, j, 1 - d))] = got_ref[:, lanes(j)]
+
+
+def per_device_paired(inputs, conv_weight, score_weight, lengths, offsets, cotangent):
+    rows, pairs, files = inputs.shape[1], cotangent.shape[1], offsets.shape[1]
+    shape = jax.ShapeDtypeStruct
+
+    def flip(value, axis):
+        return lax.ppermute(value, axis, [(0, 1), (1, 0)])
+
+    def cycle(value, by):
+        return lax.ppermute(value, "seq", [(i, (i + by) % SLOTS) for i in range(SLOTS)])
+
+    def across(value, by):
+        pairs_of = [
+            (i * 2 + j, (i + by) * 2 + 1 - j)
+            for i in range(SLOTS)
+            for j in range(2)
+            if 0 <= i + by < SLOTS
+        ]
+        return lax.ppermute(value, ("seq", "dp"), pairs_of)
+
+    wide = HALO_ROW + PAD * SLOTS
+    mx, mc, mw, mw1, md = call(
+        pack_kernel,
+        (
+            shape((rows, HALF), BF),
+            shape((pairs + PAD, HALF), BF),
+            shape((HALO_ROW, GROUP_WIDTH), BF),
+            shape((wide, GROUP_WIDTH), BF),
+            shape((PAD, HALF), BF),
+        ),
+        smem=2,
+    )(offsets, lengths, inputs, cotangent, conv_weight, score_weight.reshape(1, -1))
+    mxr = flip(mx, "dp")
+    shards = [mw, cycle(mw1, 1), cycle(mw, 2), cycle(mw, 3)]
+    mcr = flip(mc, "dp")
+    mdr = across(md, 1)
+    shards = shards + [flip(w, "fsdp") for w in shards]
+    hidden, left, partial = call(
+        functools.partial(hidden_kernel, files),
+        (
+            shape((2, rows, HALF), F32),
+            shape((2, pairs + PAD, HALF), BF),
+            shape((2, 16, GROUP_WIDTH), F32),
+        ),
+    )(inputs, cotangent, mxr, mc, mcr, mdr, *shards)
+    partial_r = flip(partial, "dp")
+    grad_rows = SLOTS * (SCORE_ROW + PAD)
+    hg, hh, mine, send = call(
+        functools.partial(mix_kernel, files),
+        (
+            shape((2, rows, HALF), BF),
+            shape((2 * PAD, HALF), BF),
+            shape((grad_rows, GROUP_WIDTH), F32),
+            shape((grad_rows, GROUP_WIDTH), F32),
+        ),
+    )(inputs, mxr, mdr, shards[1], mc, mcr, hidden, left, partial, partial_r)
+    hhr = shifted(hh, "seq", -1)
+    got = flip(send, "fsdp")
+    sums = call(add_kernel, tuple(shape((HALO_ROW, GROUP_WIDTH), BF) for _ in range(SLOTS - 1)))(
+        mine, got
+    )
+    x_own, x_send = call(
+        functools.partial(input_kernel, files),
+        (shape((rows, HALF), BF), shape((rows, HALF), BF)),
+    )(hg, hhr, mc, mcr, *shards)
+    x_got = flip(x_send, "dp")
+    final = [cycle(value, -j) for j, value in zip(range(1, SLOTS), sums)]
+    input_grad = call(place_kernel, shape(inputs.shape, BF))(x_own, x_got)
+    kernel_grad, score_grad = call(
+        sum_kernel,
+        (shape((SCORE_ROW, GROUP_WIDTH), F32), shape((1, GROUP_WIDTH // 2), F32)),
+    )(mine, got, *final)
+    return (input_grad, kernel_grad, score_grad.reshape(-1))
+
+
 def solution(mesh):
     placed = (
         P(("parts", "dp", "fsdp"), "seq", None),
@@ -146,8 +526,9 @@
         P(("parts", "dp", "fsdp"), None),
         P(("parts", "dp", "fsdp"), "seq", None),
     )
+    paired = mesh.shape["seq"] == SLOTS and mesh.shape["dp"] == 2 and mesh.shape["fsdp"] == 2
     return jax.shard_map(
-        per_device,
+        per_device_paired if paired else per_device_general,
         mesh=mesh,
         in_specs=placed,
         out_specs=(

time: 174 us -> 49.4 us (0.28)
  blocking collectives: 61.6 us -> 0 us
  local copies, waits for them, and re-layouts: 39.8 us -> 3.47 us
  other arithmetic: 26 us -> 0 us
  between operations: 16.8 us -> 1.39 us
  starting transfers between devices: 6.41 us -> 20.3 us
  matrix products: 8.95 us -> 0 us
  Pallas kernels: 0 us -> 7.38 us
  waiting for transfers between devices: 13.5 us -> 16.5 us
    unnamed x2 -> x0, blocking collectives: 61.6 us -> none
    ppermute x0 -> x16, starting transfers between devices: none -> 19 us  [the longest x6 10.3 us: cycle(): lax.ppermute(value, 'seq', [(i, (i + by) % SLOTS) for i in range(SLOTS)])]
    reshape x11 -> x0, local copies, waits for them, and re-layouts: 16 us -> none  [the longest x6 10.4 us: mix_backward(): hidden_grad = hidden_grad + jnp.repeat(block_term, block_size, axis=0)]
    reduce_sum x14 -> x0, other arithmetic: 13.9 us -> none  [the longest x3 8.34 us: mix_backward(): block_mix = (choose_prob[block_size - 1][:, None] * mix_grad).reshape(row...]
    reduce_scatter x1 -> x0, waiting for transfers between devices: 12.8 us -> none  [per_device(): lax.psum_scatter(kernel_part, ('seq', 'dp', 'fsdp'), scatter_dimension=0,...]
    ppermute x0 -> x16, waiting for transfers between devices: none -> 12.2 us  [the longest x9 8.11 us: flip(): return lax.ppermute(value, axis, [(0, 1), (1, 0)])]
    dot_general x20 -> x0, matrix products: 8.95 us -> none  [the longest x4 2.91 us: per_device(): jnp.einsum('ngc,gco->ngo', window, kernel_full[:, tap_index], preferred_e...]
    pallas_call x0 -> x7, Pallas kernels: none -> 7.38 us  [run(): pl.pallas_call(body, out_shape=out_shape, in_specs=specs, out_specs=jax.t...]
  transfers between devices with their start and end apart: 4 -> 17, of which waited for: 1 -> 7; matrix products, arithmetic and copies ran while one was open for 12% -> 0% of each run, Pallas kernels for 0% -> 5%
where the time goes in v1:
time: 49.4 us; the launch traced here: 49.1 us
  starting transfers between devices  20.3 us (41%)
  waiting for transfers between devices  16.5 us (33%)
  Pallas kernels  7.38 us (15%)
  local copies, waits for them, and re-layouts  3.47 us (7%)
  between operations  1.39 us (3%)
    ppermute x6, starting transfers between devices, cycle(): lax.ppermute(value, 'seq', [(i, (i + by) % SLOTS) for i in range(SLOTS)])  10.3 us
    ppermute x9, waiting for transfers between devices, flip(): return lax.ppermute(value, axis, [(0, 1), (1, 0)])  8.11 us
    pallas_call x7, Pallas kernels, run(): pl.pallas_call(body, out_shape=out_shape, in_specs=specs, out_specs=jax.t...  7.38 us
    ppermute x9, starting transfers between devices, flip(): return lax.ppermute(value, axis, [(0, 1), (1, 0)])  5.28 us
    ppermute x1, waiting for transfers between devices, shifted(): return lax.ppermute(value, axis, pairs)  4.33 us
    unnamed x12, local copies, waits for them, and re-layouts  3.47 us
    ppermute x1, starting transfers between devices, across(): return lax.ppermute(value, ('seq', 'dp'), pairs_of)  3.44 us
    ppermute x6, waiting for transfers between devices, cycle(): lax.ppermute(value, 'seq', [(i, (i + by) % SLOTS) for i in range(SLOTS)])  2.88 us
  transfers between devices with their start and end apart: 17, of which 7 were waited for; matrix products, arithmetic and copies ran while one was open for 0% of the time, Pallas kernels for 5%

profile of v1, /device:TPU:0, one launch (start us, length us, event | category | flops | bytes accessed | tf_op | source)
XLA Modules:
  0.0 49.1 jit_solution(8146684151391237963)
XLA Ops:
  2.0 1.0 %copy-done = bf16[1,240,1024]{2,1,0:T(8,128)(2,1)S(1)} copy-done((bf16[1,240,1024]{2,1,0:T(8,128)(2,1)S(1)}, bf16[1,240,1024]{2,1,0:T(8,128)(2,1)}, u32[]{:S(2)}) %copy-start) | copy-done | bytes 491544
  3.0 0.9 %copy-done.2 = bf16[1,120,1024]{2,1,0:T(8,128)(2,1)S(1)} copy-done((bf16[1,120,1024]{2,1,0:T(8,128)(2,1)S(1)}, bf16[1,120,1024]{2,1,0:T(8,128)(2,1)}, u32[]{:S(2)}) %copy-start.2) | copy-done | bytes 245784
  3.9 0.8 %copy-done.3 = bf16[256,128]{1,0:T(8,128)(2,1)S(1)} copy-done((bf16[256,128]{1,0:T(8,128)(2,1)S(1)}, bf16[256,128]{1,0:T(8,128)(2,1)}, u32[]{:S(2)}) %copy-start.3) | copy-done | bytes 65560
  4.8 0.7 %shard_map.85 = (bf16[240,512]{1,0:T(8,128)(2,1)S(1)}, bf16[128,512]{1,0:T(8,128)(2,1)S(1)}, bf16[272,128]{1,0:T(8,128)(2,1)S(1)}, bf16[304,128]{1,0:T(8,128)(2,1)S(1)}, bf16[8,512]{1,0:T(8,128)(2,1)S(1)}) custom-call(s32[1,16]{1,0:T(1,128)S(1)} %copy-done.4, s32[1]{0:T(128)S(6)} %copy.9.len_ref, bf16[1,240,1024]{2,1,0:T(8,128)(2,1)S(1)} %copy-done, ...), custom_call_target="tpu_custom_call" | custom-call | tf_op jit(solution)/shard_map/pallas_call | solution.py:169
  5.4 3.0 %collective-permute-start = (bf16[240,512]{1,0:T(8,128)(2,1)S(1)}, bf16[240,512]{1,0:T(8,128)(2,1)S(1)}, u32[]{:S(2)}, u32[]{:S(2)}) collective-permute-start(bf16[240,512]{1,0:T(8,128)(2,1)S(1)} %get-tuple-element.22), channel_id=1, source_target_pairs={{0,2},{2,0},{1,3},{3,1},{4,6},{6,4},{5,7},{7,5},{8,10},{10,8},{9,1... | collective-permute-start | bytes 737288 | tf_op jit(solution)/shard_map/ppermute | solution.py:451
  8.4 1.6 %collective-permute-start.2 = (bf16[304,128]{1,0:T(8,128)(2,1)S(1)}, bf16[304,128]{1,0:T(8,128)(2,1)S(1)}, u32[]{:S(2)}, u32[]{:S(2)}) collective-permute-start(bf16[304,128]{1,0:T(8,128)(2,1)S(1)} %get-tuple-element.24), channel_id=1, source_target_pairs={{0,4},{4,8},{8,12},{12,0},{1,5},{5,9},{9,13},{13,1},{2,6},{6,10},{... | collective-permute-start | bytes 233480 | tf_op jit(solution)/shard_map/ppermute | solution.py:454
  10.0 3.4 %collective-permute-start.1 = (bf16[8,512]{1,0:T(8,128)(2,1)S(1)}, bf16[8,512]{1,0:T(8,128)(2,1)S(1)}, u32[]{:S(2)}, u32[]{:S(2)}) collective-permute-start(bf16[8,512]{1,0:T(8,128)(2,1)S(1)} %get-tuple-element.23), channel_id=1, source_target_pairs={{0,6},{2,4},{4,10},{6,8},{8,14},{10,12},{1,7},{3,5},{5,11},{7,9},{... | collective-permute-start | bytes 24584 | tf_op jit(solution)/shard_map/ppermute | solution.py:463
  13.6 1.2 %collective-permute-done.1.md_ref = bf16[8,512]{1,0:T(8,128)(2,1)S(1)} collective-permute-done((bf16[8,512]{1,0:T(8,128)(2,1)S(1)}, bf16[8,512]{1,0:T(8,128)(2,1)S(1)}, u32[]{:S(2)}, u32[]{:S(2)}) %collective-permute-start.1) | collective-permute-done | bytes 8224 | tf_op jit(solution)/shard_map/ppermute | solution.py:463
  14.8 5.0 %collective-permute-start.4 = (bf16[272,128]{1,0:T(8,128)(2,1)S(1)}, bf16[272,128]{1,0:T(8,128)(2,1)S(1)}, u32[]{:S(2)}, u32[]{:S(2)}) collective-permute-start(bf16[272,128]{1,0:T(8,128)(2,1)S(1)} %get-tuple-element.26.refs_0_), channel_id=1, source_target_pairs={{0,8},{4,12},{8,0},{12,4},{1,9},{5,13},{9,1},{13,5},{2,10},{6,14},... | collective-permute-start | bytes 208904 | tf_op jit(solution)/shard_map/ppermute | solution.py:454
  20.9 2.1 %collective-permute-done.4.refs_2_ = bf16[272,128]{1,0:T(8,128)(2,1)S(1)} collective-permute-done((bf16[272,128]{1,0:T(8,128)(2,1)S(1)}, bf16[272,128]{1,0:T(8,128)(2,1)S(1)}, u32[]{:S(2)}, u32[]{:S(2)}) %collective-permute-start.4) | collective-permute-done | bytes 69664 | tf_op jit(solution)/shard_map/ppermute | solution.py:454
  23.0 1.8 %collective-permute-done.3.mcr_ref = bf16[128,512]{1,0:T(8,128)(2,1)S(1)} collective-permute-done((bf16[128,512]{1,0:T(8,128)(2,1)S(1)}, bf16[128,512]{1,0:T(8,128)(2,1)S(1)}, u32[]{:S(2)}, u32[]{:S(2)}) %collective-permute-start.3) | collective-permute-done | bytes 131104 | tf_op jit(solution)/shard_map/ppermute | solution.py:451
  24.9 1.7 %shard_map.86 = (f32[2,240,512]{2,1,0:T(8,128)S(1)}, bf16[2,128,512]{2,1,0:T(8,128)(2,1)S(1)}, f32[2,16,128]{2,1,0:T(8,128)S(1)}) custom-call(bf16[1,240,1024]{2,1,0:T(8,128)(2,1)S(1)} %copy-done.1, bf16[1,120,1024]{2,1,0:T(8,128)(2,1)S(1)} %copy-done.2, bf16[240,512]{1,0:T(8,128)(2,1)S(1)} %collective-permute-done.mx_ref, ...), custom_call_target="tpu_custom_call" | custom-call | tf_op jit(solution)/shard_map/pallas_call | solution.py:169
  27.2 3.2 %collective-permute-done.10.rr_ref = f32[2,16,128]{2,1,0:T(8,128)S(1)} collective-permute-done((f32[2,16,128]{2,1,0:T(8,128)S(1)}, f32[2,16,128]{2,1,0:T(8,128)S(1)}, u32[]{:S(2)}, u32[]{:S(2)}) %collective-permute-start.10) | collective-permute-done | bytes 16416 | tf_op jit(solution)/shard_map/ppermute | solution.py:451
  30.4 1.8 %shard_map.87 = (bf16[2,240,512]{2,1,0:T(8,128)(2,1)S(1)}, bf16[16,512]{1,0:T(8,128)(2,1)S(1)}, f32[1056,128]{1,0:T(8,128)S(1)}, f32[1056,128]{1,0:T(8,128)S(1)}) custom-call(bf16[1,240,1024]{2,1,0:T(8,128)(2,1)S(1)} %copy-done.1, bf16[240,512]{1,0:T(8,128)(2,1)S(1)} %collective-permute-done.mx_ref, bf16[8,512]{1,0:T(8,128)(2,1)S(1)} %collective-permute-done.1.md_ref, ...), custom_call_target="tpu_custom_call" | custom-call | tf_op jit(solution)/shard_map/pallas_call | solution.py:169
  32.2 1.3 %collective-permute-start.11 = (bf16[16,512]{1,0:T(8,128)(2,1)S(1)}, bf16[16,512]{1,0:T(8,128)(2,1)S(1)}, u32[]{:S(2)}, u32[]{:S(2)}) collective-permute-start(bf16[16,512]{1,0:T(8,128)(2,1)S(1)} %get-tuple-element.31), channel_id=1, source_target_pairs={{4,0},{8,4},{12,8},{5,1},{9,5},{13,9},{6,2},{10,6},{14,10},{7,3},{... | collective-permute-start | bytes 49160 | tf_op jit(solution)/shard_map/ppermute | solution.py:21
  33.5 4.3 %collective-permute-done.11.hh_ref = bf16[16,512]{1,0:T(8,128)(2,1)S(1)} collective-permute-done((bf16[16,512]{1,0:T(8,128)(2,1)S(1)}, bf16[16,512]{1,0:T(8,128)(2,1)S(1)}, u32[]{:S(2)}, u32[]{:S(2)}) %collective-permute-start.11) | collective-permute-done | bytes 16416 | tf_op jit(solution)/shard_map/ppermute | solution.py:21
  37.9 1.6 %shard_map.88 = (bf16[240,512]{1,0:T(8,128)(2,1)S(1)}, bf16[240,512]{1,0:T(8,128)(2,1)S(1)}) custom-call(bf16[2,240,512]{2,1,0:T(8,128)(2,1)S(1)} %get-tuple-element.30.hg_ref, bf16[16,512]{1,0:T(8,128)(2,1)S(1)} %collective-permute-done.11.hh_ref, bf16[128,512]{1,0:T(8,128)(2,1)S(1)} %get-tuple-element.25.mc_ref, ...), custom_call_target="tpu_custom_call" | custom-call | tf_op jit(solution)/shard_map/pallas_call | solution.py:169
  40.1 0.7 %collective-permute-start.14 = (bf16[272,128]{1,0:T(8,128)(2,1)S(1)}, bf16[272,128]{1,0:T(8,128)(2,1)S(1)}, u32[]{:S(2)}, u32[]{:S(2)}) collective-permute-start(bf16[272,128]{1,0:T(8,128)(2,1)S(1)} %get-tuple-element.36), channel_id=1, source_target_pairs={{0,12},{4,0},{8,4},{12,8},{1,13},{5,1},{9,5},{13,9},{2,14},{6,2},{... | collective-permute-start | bytes 208904 | tf_op jit(solution)/shard_map/ppermute | solution.py:454
  40.8 0.9 %collective-permute-start.15 = (bf16[272,128]{1,0:T(8,128)(2,1)S(1)}, bf16[272,128]{1,0:T(8,128)(2,1)S(1)}, u32[]{:S(2)}, u32[]{:S(2)}) collective-permute-start(bf16[272,128]{1,0:T(8,128)(2,1)S(1)} %get-tuple-element.37), channel_id=1, source_target_pairs={{0,8},{4,12},{8,0},{12,4},{1,9},{5,13},{9,1},{13,5},{2,10},{6,14},... | collective-permute-start | bytes 208904 | tf_op jit(solution)/shard_map/ppermute | solution.py:454
  41.7 1.9 %collective-permute-start.16 = (bf16[272,128]{1,0:T(8,128)(2,1)S(1)}, bf16[272,128]{1,0:T(8,128)(2,1)S(1)}, u32[]{:S(2)}, u32[]{:S(2)}) collective-permute-start(bf16[272,128]{1,0:T(8,128)(2,1)S(1)} %get-tuple-element.38), channel_id=1, source_target_pairs={{0,4},{4,8},{8,12},{12,0},{1,5},{5,9},{9,13},{13,1},{2,6},{6,10},{... | collective-permute-start | bytes 208904 | tf_op jit(solution)/shard_map/ppermute | solution.py:454
  43.6 3.1 %collective-permute-done.12.got_ref = bf16[240,512]{1,0:T(8,128)(2,1)S(1)} collective-permute-done((bf16[240,512]{1,0:T(8,128)(2,1)S(1)}, bf16[240,512]{1,0:T(8,128)(2,1)S(1)}, u32[]{:S(2)}, u32[]{:S(2)}) %collective-permute-start.12) | collective-permute-done | bytes 245792 | tf_op jit(solution)/shard_map/ppermute | solution.py:451
  46.7 0.9 %shard_map.89 = bf16[1,240,1024]{2,1,0:T(8,128)(2,1)} custom-call(bf16[240,512]{1,0:T(8,128)(2,1)S(1)} %get-tuple-element.32.own_ref, bf16[240,512]{1,0:T(8,128)(2,1)S(1)} %collective-permute-done.12.got_ref), custom_call_target="tpu_custom_call" | custom-call | tf_op jit(solution)/shard_map/pallas_call | solution.py:169
  47.6 0.7 %collective-permute-done.15.z2 = bf16[272,128]{1,0:T(8,128)(2,1)S(1)} collective-permute-done((bf16[272,128]{1,0:T(8,128)(2,1)S(1)}, bf16[272,128]{1,0:T(8,128)(2,1)S(1)}, u32[]{:S(2)}, u32[]{:S(2)}) %collective-permute-start.15) | collective-permute-done | bytes 69664 | tf_op jit(solution)/shard_map/ppermute | solution.py:454
  48.4 0.7 %shard_map.91 = (f32[256,128]{1,0:T(8,128)}, f32[1,64]{1,0:T(1,128)}) custom-call(f32[1056,128]{1,0:T(8,128)S(1)} %get-tuple-element.34.mine_ref, f32[1056,128]{1,0:T(8,128)S(1)} %collective-permute-done.13.got_ref, bf16[272,128]{1,0:T(8,128)(2,1)S(1)} %collective-permute-done.14.z1, bf16[272,128]{1,0:T(8,128)(2,1)S(1)} %collective-permute-done.15.z2, ...), custom_call_target="tpu_custom_call" | custom-call | tf_op jit(solution)/shard_map/pallas_call | solution.py:169
  (29 shorter events, 3.1 us)
Async XLA Ops:
  1.3 0.7 %copy-start.4 = (s32[1,16]{1,0:T(1,128)S(1)}, s32[1,16]{1,0:T(1,128)}, u32[]{:S(2)}) copy-start(s32[1,16]{1,0:T(1,128)} %off_ref.1) | copy-start | bytes 196
  1.3 0.7 %copy-start.5 = (bf16[64]{0:T(256)(128)(2,1)S(1)}, bf16[64]{0:T(256)(128)(2,1)}, u32[]{:S(2)}) copy-start(bf16[64]{0:T(256)(128)(2,1)} %param.8) | copy-start | bytes 388
  1.9 1.0 %copy-start = (bf16[1,240,1024]{2,1,0:T(8,128)(2,1)S(1)}, bf16[1,240,1024]{2,1,0:T(8,128)(2,1)}, u32[]{:S(2)}) copy-start(bf16[1,240,1024]{2,1,0:T(8,128)(2,1)} %x_ref.5) | copy-start | bytes 1474564
  3.0 0.9 %copy-start.2 = (bf16[1,120,1024]{2,1,0:T(8,128)(2,1)S(1)}, bf16[1,120,1024]{2,1,0:T(8,128)(2,1)}, u32[]{:S(2)}) copy-start(bf16[1,120,1024]{2,1,0:T(8,128)(2,1)} %c_ref.3) | copy-start | bytes 737284
  3.9 0.8 %copy-start.3 = (bf16[256,128]{1,0:T(8,128)(2,1)S(1)}, bf16[256,128]{1,0:T(8,128)(2,1)}, u32[]{:S(2)}) copy-start(bf16[256,128]{1,0:T(8,128)(2,1)} %w_ref.1) | copy-start | bytes 196612
  4.8 20.1 %copy-start.1 = (bf16[1,240,1024]{2,1,0:T(8,128)(2,1)S(1)}, bf16[1,240,1024]{2,1,0:T(8,128)(2,1)}, u32[]{:S(2)}) copy-start(bf16[1,240,1024]{2,1,0:T(8,128)(2,1)} %x_ref.5) | copy-start | bytes 1474564
  5.4 19.4 %collective-permute-start = (bf16[240,512]{1,0:T(8,128)(2,1)S(1)}, bf16[240,512]{1,0:T(8,128)(2,1)S(1)}, u32[]{:S(2)}, u32[]{:S(2)}) collective-permute-start(bf16[240,512]{1,0:T(8,128)(2,1)S(1)} %get-tuple-element.22), channel_id=1, source_target_pairs={{0,2},{2,0},{1,3},{3,1},{4,6},{6,4},{5,7},{7,5},{8,10},{10,8},{9,1... | collective-permute-start | bytes 737288 | tf_op jit(solution)/shard_map/ppermute | solution.py:451
  8.4 11.4 %collective-permute-start.6 = (bf16[272,128]{1,0:T(8,128)(2,1)S(1)}, bf16[272,128]{1,0:T(8,128)(2,1)S(1)}, u32[]{:S(2)}, u32[]{:S(2)}) collective-permute-start(bf16[272,128]{1,0:T(8,128)(2,1)S(1)} %get-tuple-element.26.refs_0_), channel_id=1, source_target_pairs={{0,1},{1,0},{2,3},{3,2},{4,5},{5,4},{6,7},{7,6},{8,9},{9,8},{10,11... | collective-permute-start | bytes 208904 | tf_op jit(solution)/shard_map/ppermute | solution.py:451
  8.4 11.9 %collective-permute-start.2 = (bf16[304,128]{1,0:T(8,128)(2,1)S(1)}, bf16[304,128]{1,0:T(8,128)(2,1)S(1)}, u32[]{:S(2)}, u32[]{:S(2)}) collective-permute-start(bf16[304,128]{1,0:T(8,128)(2,1)S(1)} %get-tuple-element.24), channel_id=1, source_target_pairs={{0,4},{4,8},{8,12},{12,0},{1,5},{5,9},{9,13},{13,1},{2,6},{6,10},{... | collective-permute-start | bytes 233480 | tf_op jit(solution)/shard_map/ppermute | solution.py:454
  10.0 4.8 %collective-permute-start.1 = (bf16[8,512]{1,0:T(8,128)(2,1)S(1)}, bf16[8,512]{1,0:T(8,128)(2,1)S(1)}, u32[]{:S(2)}, u32[]{:S(2)}) collective-permute-start(bf16[8,512]{1,0:T(8,128)(2,1)S(1)} %get-tuple-element.23), channel_id=1, source_target_pairs={{0,6},{2,4},{4,10},{6,8},{8,14},{10,12},{1,7},{3,5},{5,11},{7,9},{... | collective-permute-start | bytes 24584 | tf_op jit(solution)/shard_map/ppermute | solution.py:463
  13.5 6.9 %collective-permute-start.5 = (bf16[272,128]{1,0:T(8,128)(2,1)S(1)}, bf16[272,128]{1,0:T(8,128)(2,1)S(1)}, u32[]{:S(2)}, u32[]{:S(2)}) collective-permute-start(bf16[272,128]{1,0:T(8,128)(2,1)S(1)} %get-tuple-element.26.refs_0_), channel_id=1, source_target_pairs={{0,12},{4,0},{8,4},{12,8},{1,13},{5,1},{9,5},{13,9},{2,14},{6,2},{... | collective-permute-start | bytes 208904 | tf_op jit(solution)/shard_map/ppermute | solution.py:454
  14.8 8.2 %collective-permute-start.4 = (bf16[272,128]{1,0:T(8,128)(2,1)S(1)}, bf16[272,128]{1,0:T(8,128)(2,1)S(1)}, u32[]{:S(2)}, u32[]{:S(2)}) collective-permute-start(bf16[272,128]{1,0:T(8,128)(2,1)S(1)} %get-tuple-element.26.refs_0_), channel_id=1, source_target_pairs={{0,8},{4,12},{8,0},{12,4},{1,9},{5,13},{9,1},{13,5},{2,10},{6,14},... | collective-permute-start | bytes 208904 | tf_op jit(solution)/shard_map/ppermute | solution.py:454
  19.9 5.0 %collective-permute-start.3 = (bf16[128,512]{1,0:T(8,128)(2,1)S(1)}, bf16[128,512]{1,0:T(8,128)(2,1)S(1)}, u32[]{:S(2)}, u32[]{:S(2)}) collective-permute-start(bf16[128,512]{1,0:T(8,128)(2,1)S(1)} %get-tuple-element.25.mc_ref), channel_id=1, source_target_pairs={{0,2},{2,0},{1,3},{3,1},{4,6},{6,4},{5,7},{7,5},{8,10},{10,8},{9,1... | collective-permute-start | bytes 393224 | tf_op jit(solution)/shard_map/ppermute | solution.py:451
  20.4 4.5 %collective-permute-start.7 = (bf16[304,128]{1,0:T(8,128)(2,1)S(1)}, bf16[304,128]{1,0:T(8,128)(2,1)S(1)}, u32[]{:S(2)}, u32[]{:S(2)}) collective-permute-start(bf16[304,128]{1,0:T(8,128)(2,1)S(1)} %collective-permute-done.2.refs_1_.w1_ref), channel_id=1, source_target_pairs={{0,1},{1,0},{2,3},{3,2},{4,5},{5,4},{6,7},{7,6},{8,9},{9,8},{10,11... | collective-permute-start | bytes 233480 | tf_op jit(solution)/shard_map/ppermute | solution.py:451
  20.4 4.4 %collective-permute-start.9 = (bf16[272,128]{1,0:T(8,128)(2,1)S(1)}, bf16[272,128]{1,0:T(8,128)(2,1)S(1)}, u32[]{:S(2)}, u32[]{:S(2)}) collective-permute-start(bf16[272,128]{1,0:T(8,128)(2,1)S(1)} %collective-permute-done.5.refs_3_), channel_id=1, source_target_pairs={{0,1},{1,0},{2,3},{3,2},{4,5},{5,4},{6,7},{7,6},{8,9},{9,8},{10,11... | collective-permute-start | bytes 208904 | tf_op jit(solution)/shard_map/ppermute | solution.py:451
  23.0 1.8 %collective-permute-start.8 = (bf16[272,128]{1,0:T(8,128)(2,1)S(1)}, bf16[272,128]{1,0:T(8,128)(2,1)S(1)}, u32[]{:S(2)}, u32[]{:S(2)}) collective-permute-start(bf16[272,128]{1,0:T(8,128)(2,1)S(1)} %collective-permute-done.4.refs_2_), channel_id=1, source_target_pairs={{0,1},{1,0},{2,3},{3,2},{4,5},{5,4},{6,7},{7,6},{8,9},{9,8},{10,11... | collective-permute-start | bytes 208904 | tf_op jit(solution)/shard_map/ppermute | solution.py:451
  26.6 3.8 %collective-permute-start.10 = (f32[2,16,128]{2,1,0:T(8,128)S(1)}, f32[2,16,128]{2,1,0:T(8,128)S(1)}, u32[]{:S(2)}, u32[]{:S(2)}) collective-permute-start(f32[2,16,128]{2,1,0:T(8,128)S(1)} %get-tuple-element.29.r_ref), channel_id=1, source_target_pairs={{0,2},{2,0},{1,3},{3,1},{4,6},{6,4},{5,7},{7,5},{8,10},{10,8},{9,1... | collective-permute-start | bytes 49160 | tf_op jit(solution)/shard_map/ppermute | solution.py:451
  32.1 7.9 %collective-permute-start.13 = (f32[1056,128]{1,0:T(8,128)S(1)}, f32[1056,128]{1,0:T(8,128)S(1)}, u32[]{:S(2)}, u32[]{:S(2)}) collective-permute-start(f32[1056,128]{1,0:T(8,128)S(1)} %get-tuple-element.35), channel_id=1, source_target_pairs={{0,1},{1,0},{2,3},{3,2},{4,5},{5,4},{6,7},{7,6},{8,9},{9,8},{10,11... | collective-permute-start | bytes 1622024 | tf_op jit(solution)/shard_map/ppermute | solution.py:451
  32.2 5.6 %collective-permute-start.11 = (bf16[16,512]{1,0:T(8,128)(2,1)S(1)}, bf16[16,512]{1,0:T(8,128)(2,1)S(1)}, u32[]{:S(2)}, u32[]{:S(2)}) collective-permute-start(bf16[16,512]{1,0:T(8,128)(2,1)S(1)} %get-tuple-element.31), channel_id=1, source_target_pairs={{4,0},{8,4},{12,8},{5,1},{9,5},{13,9},{6,2},{10,6},{14,10},{7,3},{... | collective-permute-start | bytes 49160 | tf_op jit(solution)/shard_map/ppermute | solution.py:21
  39.4 7.3 %collective-permute-start.12 = (bf16[240,512]{1,0:T(8,128)(2,1)S(1)}, bf16[240,512]{1,0:T(8,128)(2,1)S(1)}, u32[]{:S(2)}, u32[]{:S(2)}) collective-permute-start(bf16[240,512]{1,0:T(8,128)(2,1)S(1)} %get-tuple-element.33), channel_id=1, source_target_pairs={{0,2},{2,0},{1,3},{3,1},{4,6},{6,4},{5,7},{7,5},{8,10},{10,8},{9,1... | collective-permute-start | bytes 737288 | tf_op jit(solution)/shard_map/ppermute | solution.py:451
  40.1 7.6 %collective-permute-start.14 = (bf16[272,128]{1,0:T(8,128)(2,1)S(1)}, bf16[272,128]{1,0:T(8,128)(2,1)S(1)}, u32[]{:S(2)}, u32[]{:S(2)}) collective-permute-start(bf16[272,128]{1,0:T(8,128)(2,1)S(1)} %get-tuple-element.36), channel_id=1, source_target_pairs={{0,12},{4,0},{8,4},{12,8},{1,13},{5,1},{9,5},{13,9},{2,14},{6,2},{... | collective-permute-start | bytes 208904 | tf_op jit(solution)/shard_map/ppermute | solution.py:454
  40.8 7.6 %collective-permute-start.15 = (bf16[272,128]{1,0:T(8,128)(2,1)S(1)}, bf16[272,128]{1,0:T(8,128)(2,1)S(1)}, u32[]{:S(2)}, u32[]{:S(2)}) collective-permute-start(bf16[272,128]{1,0:T(8,128)(2,1)S(1)} %get-tuple-element.37), channel_id=1, source_target_pairs={{0,8},{4,12},{8,0},{12,4},{1,9},{5,13},{9,1},{13,5},{2,10},{6,14},... | collective-permute-start | bytes 208904 | tf_op jit(solution)/shard_map/ppermute | solution.py:454
  41.7 6.7 %collective-permute-start.16 = (bf16[272,128]{1,0:T(8,128)(2,1)S(1)}, bf16[272,128]{1,0:T(8,128)(2,1)S(1)}, u32[]{:S(2)}, u32[]{:S(2)}) collective-permute-start(bf16[272,128]{1,0:T(8,128)(2,1)S(1)} %get-tuple-element.38), channel_id=1, source_target_pairs={{0,4},{4,8},{8,12},{12,0},{1,5},{5,9},{9,13},{13,1},{2,6},{6,10},{... | collective-permute-start | bytes 208904 | tf_op jit(solution)/shard_map/ppermute | solution.py:454

commit v2 on v1

--- a/solution.py
+++ b/solution.py
@@ -162,55 +162,80 @@
     return 2 * lax.rem(seq - slot + 2 * SLOTS, SLOTS) + parity
 
 
-def call(body, out_shape, scratch=(), smem=0, cost=None):
+def call(body, out_shape, scratch=(), hbm=0):
     def run(*args):
-        specs = [pl.BlockSpec(memory_space=pltpu.SMEM)] * smem
-        specs += [pl.BlockSpec(memory_space=pltpu.VMEM)] * (len(args) - smem)
+        specs = [pl.BlockSpec(memory_space=pltpu.HBM)] * hbm
+        specs += [pl.BlockSpec(memory_space=pltpu.VMEM)] * (len(args) - hbm)
         return pl.pallas_call(
             body,
             out_shape=out_shape,
             in_specs=specs,
             out_specs=jax.tree.map(lambda _: pl.BlockSpec(memory_space=pltpu.VMEM), out_shape),
             scratch_shapes=list(scratch),
-            cost_estimate=cost,
             compiler_params=pltpu.CompilerParams(vmem_limit_bytes=48 * 1024 * 1024),
         )(*args)
 
     return run
 
 
-def pack_kernel(off_ref, len_ref, x_ref, c_ref, w_ref, score_ref, mx, mc, mw, mw1, md):
-    rows = x_ref.shape[1]
-    pairs = c_ref.shape[1]
+def pack_kernel(off_hbm, x_hbm, c_hbm, w_hbm, score_hbm, len_ref, mine, other, mw, mw1, md,
+                off_ref, x_ref, c_ref, score_ref, sems):
+    rows, pairs, files = x_ref.shape[1], c_ref.shape[1], off_ref.shape[1]
     s, d, f = (lax.axis_index(name) for name in ("seq", "dp", "fsdp"))
-    for j in range(SLOTS):
-        col = group_lanes(slot_group(s, j, 1 - d))
-        mx[:, lanes(j)] = x_ref[0, :, col]
-        mc[0:pairs, lanes(j)] = c_ref[0, :, col]
-        next_other = group_lanes(slot_group(s + 1, j, 1 - d))
-        md[:, lanes(j)] = x_ref[0, rows - PAD :, next_other]
-        next_own = group_lanes(slot_group(s + 1, j, d))
-        mw1[HALO_ROW + PAD * j : HALO_ROW + PAD * (j + 1), :] = x_ref[0, rows - PAD :, next_own]
+    copies = [
+        pltpu.make_async_copy(source, target, sems.at[i])
+        for i, (source, target) in enumerate(
+            (
+                (x_hbm, x_ref),
+                (c_hbm, c_ref),
+                (off_hbm, off_ref),
+                (score_hbm, score_ref),
+                (w_hbm, mw.at[0:SCORE_ROW]),
+                (w_hbm, mw1.at[0:SCORE_ROW]),
+            )
+        )
+    ]
+    for copy in copies:
+        copy.start()
+    for copy in copies[2:4]:
+        copy.wait()
     lane = lax.broadcasted_iota(jnp.int32, (PAD, GROUP_WIDTH), 1)
     start = s * rows
     info = jnp.zeros((PAD, GROUP_WIDTH), jnp.int32)
-    for i in range(off_ref.shape[1]):
+    for i in range(files):
         info = jnp.where(lane == i, jnp.clip(off_ref[0, i] - start, -4, rows + PAD), info)
-    info = jnp.where(lane == off_ref.shape[1], jnp.clip(len_ref[0] - start, 0, rows), info)
-    mc[pairs:, :] = jnp.zeros((mc.shape[0] - pairs, HALF), BF)
-    mc[pairs : pairs + PAD, lanes(0)] = (info.astype(F32) * 0.25).astype(BF)
+    info = jnp.where(lane == files, jnp.clip(len_ref[0:1, 0:1] - start, 0, rows), info)
+    info = (info.astype(F32) * 0.25).astype(BF)
     value = score_ref[...].astype(F32)
     both = jnp.concatenate([value, value], axis=1)
     half = lax.broadcasted_iota(jnp.int32, (16, GROUP_WIDTH), 1) // (GROUP_WIDTH // 2)
     row = lax.broadcasted_iota(jnp.int32, (16, GROUP_WIDTH), 0)
     block = jnp.where((half == f) & (row == 0), jnp.broadcast_to(both, (16, GROUP_WIDTH)), 0.0)
     for ref in (mw, mw1):
-        ref[0:SCORE_ROW, :] = w_ref[...]
         ref[SCORE_ROW:HALO_ROW, :] = block.astype(BF)
-
-
-def row_info(mc_ref, pairs, files, extent):
-    info = mc_ref[pairs : pairs + PAD, lanes(0)].astype(F32)[0:1] * 4.0
+    copies[0].wait()
+    for ref, parity in ((other, 1 - d), (mine, d)):
+        for j in range(SLOTS):
+            ref[0:rows, lanes(j)] = x_ref[0, :, group_lanes(slot_group(s, j, parity))]
+    for j in range(SLOTS):
+        next_other = group_lanes(slot_group(s + 1, j, 1 - d))
+        md[:, lanes(j)] = x_ref[0, rows - PAD :, next_other]
+        next_own = group_lanes(slot_group(s + 1, j, d))
+        mw1[HALO_ROW + PAD * j : HALO_ROW + PAD * (j + 1), :] = x_ref[0, rows - PAD :, next_own]
+    copies[1].wait()
+    for ref, parity in ((other, 1 - d), (mine, d)):
+        for j in range(SLOTS):
+            col = group_lanes(slot_group(s, j, parity))
+            ref[rows : rows + pairs, lanes(j)] = c_ref[0, :, col]
+        ref[rows + pairs :, :] = jnp.zeros((PAD, HALF), BF)
+        ref[rows + pairs :, lanes(0)] = info
+    copies[4].wait()
+    copies[5].wait()
+
+
+def row_info(message, files):
+    extent = (message.shape[0] - PAD) // 3 * 2
+    info = message[message.shape[0] - PAD :, lanes(0)].astype(F32)[0:1] * 4.0
     lane = lax.broadcasted_iota(jnp.int32, (1, GROUP_WIDTH), 1)
     length = jnp.sum(jnp.where(lane == files, info, 0.0), axis=1, keepdims=True)
     pos = lax.broadcasted_iota(jnp.int32, (extent, GROUP_WIDTH), 0).astype(F32)
@@ -245,18 +270,17 @@
     out = [rows_value]
     for lag in range(1, KERNEL):
         moved = pltpu.roll(padded, lag, 0)[PAD:]
-        out.append(jnp.where(since[:rows] >= lag, moved, 0.0).astype(BF))
+        out.append(jnp.where(since >= lag, moved, 0.0).astype(BF))
     return out
 
 
-def stream_parts(x_ref, mx_ref, w1_ref, md_ref, j, stream):
-    s, d = lax.axis_index("seq"), lax.axis_index("dp")
+def stream_parts(messages, w1_ref, md_ref, j, stream):
+    rows = (messages[stream].shape[0] - PAD) // 3 * 2
     if stream == 0:
-        return (
-            w1_ref[HALO_ROW + PAD * j : HALO_ROW + PAD * (j + 1), :],
-            x_ref[0, :, group_lanes(slot_group(s, j, d))],
-        )
-    return md_ref[:, lanes(j)], mx_ref[:, lanes(j)]
+        tail = w1_ref[HALO_ROW + PAD * j : HALO_ROW + PAD * (j + 1), :]
+    else:
+        tail = md_ref[:, lanes(j)]
+    return tail, messages[stream][0:rows, lanes(j)]
 
 
 def kernel_halves(w_refs, j):
@@ -275,11 +299,12 @@
     return high, (value - high.astype(F32)).astype(BF)
 
 
-def hidden_kernel(files, x_ref, c_ref, mx_ref, mc_ref, mcr_ref, md_ref, *refs):
+def hidden_kernel(files, mine_ref, other_ref, md_ref, *refs):
     w_refs, (h_out, l_out, r_out) = refs[: 2 * SLOTS], refs[2 * SLOTS :]
-    rows, pairs = x_ref.shape[1], c_ref.shape[1]
-    s, d = lax.axis_index("seq"), lax.axis_index("dp")
-    infos = [row_info(ref, pairs, files, rows) for ref in (mc_ref, mcr_ref)]
+    messages = (mine_ref, other_ref)
+    rows = h_out.shape[1]
+    pairs = rows // 2
+    infos = [row_info(ref, files) for ref in messages]
     gram = [jnp.zeros((rows, GROUP_WIDTH), F32) for _ in range(2)]
     for j in range(SLOTS):
         low, high = kernel_halves(w_refs, j)
@@ -289,17 +314,14 @@
         )[0:PAD]
         for stream in range(2):
             since, valid = infos[stream]
-            tail, value = stream_parts(x_ref, mx_ref, w_refs[1], md_ref, j, stream)
+            tail, value = stream_parts(messages, w_refs[1], md_ref, j, stream)
             win = windows_of(tail, value, since)
             hidden = jnp.dot(
                 jnp.concatenate(win[:2], axis=1), low, preferred_element_type=F32
             ) + jnp.dot(jnp.concatenate(win[2:], axis=1), high, preferred_element_type=F32)
             hidden = hidden * valid
             h_out[stream, :, lanes(j)] = hidden
-            if stream == 0:
-                cot = c_ref[0, :, group_lanes(slot_group(s, j, d))]
-            else:
-                cot = mcr_ref[0:pairs, lanes(j)]
+            cot = messages[stream][rows : rows + pairs, lanes(j)]
             left = jnp.concatenate([cot.astype(F32), score], axis=0).astype(BF)
             l_out[stream, :, lanes(j)] = left
             a, b = two_terms(hidden)
@@ -320,13 +342,14 @@
         r_out[stream] = jnp.concatenate(inner + logit, axis=0)
 
 
-def mix_kernel(files, x_ref, mx_ref, md_ref, w1_ref, mc_ref, mcr_ref, h_ref, l_ref, r_ref, rr_ref,
-               hg_out, hh_out, mine_out, send_out):
-    rows = x_ref.shape[1]
+def mix_kernel(files, mine_ref, other_ref, md_ref, w1_ref, h_ref, l_ref, r_ref, rr_ref,
+               hg_out, mine_out, send_out):
+    messages = (mine_ref, other_ref)
+    rows = h_ref.shape[1]
     pairs = rows // 2
     f = lax.axis_index("fsdp")
     weights = block_weights(rows)
-    infos = [row_info(ref, pairs, files, rows) for ref in (mc_ref, mcr_ref)]
+    infos = [row_info(ref, files) for ref in messages]
     lane = lax.broadcasted_iota(jnp.int32, (rows, GROUP_WIDTH), 1)
     columns = []
     for stream in range(2):
@@ -356,7 +379,6 @@
             )
             grad = grad.astype(BF)
             hg_out[stream, :, lanes(j)] = grad
-            hh_out[PAD * stream : PAD * (stream + 1), lanes((j + SLOTS - 1) % SLOTS)] = grad[0:PAD]
     first = jnp.full((SCORE_ROW, GROUP_WIDTH), f, jnp.int32) == 0
     row = lax.broadcasted_iota(jnp.int32, (PAD, GROUP_WIDTH), 0)
     for j in range(SLOTS):
@@ -364,7 +386,7 @@
         high = jnp.zeros((SCORE_ROW, GROUP_WIDTH), F32)
         score = jnp.zeros((1, GROUP_WIDTH), F32)
         for stream in range(2):
-            tail, value = stream_parts(x_ref, mx_ref, w1_ref, md_ref, j, stream)
+            tail, value = stream_parts(messages, w1_ref, md_ref, j, stream)
             win = windows_of(tail, value, infos[stream][0])
             grad = hg_out[stream, :, lanes(j)]
             dims = (((0,), (0,)), ((), ()))
@@ -385,13 +407,17 @@
         send_out[base + SCORE_ROW : base + SCORE_ROW + PAD, :] = score
 
 
-def add_kernel(mine_ref, got_ref, *outs):
+def add_kernel(mine_ref, got_ref, edge_ref, *outs):
     for j, out in zip(range(1, SLOTS), outs):
         base = j * (SCORE_ROW + PAD)
         total = mine_ref[base : base + SCORE_ROW + PAD, :] + got_ref[base : base + SCORE_ROW + PAD, :]
         out[0:SCORE_ROW, :] = total[0:SCORE_ROW].astype(BF)
         a, b = two_terms(total[SCORE_ROW:])
-        out[SCORE_ROW:, :] = jnp.concatenate([a.astype(F32), b.astype(F32)], axis=0).astype(BF)
+        out[SCORE_ROW:HALO_ROW, :] = jnp.concatenate([a.astype(F32), b.astype(F32)], axis=0).astype(BF)
+        if j == 1:
+            for slot in range(SLOTS):
+                edge = edge_ref[:, lanes(slot)]
+                out[HALO_ROW + PAD * slot : HALO_ROW + PAD * (slot + 1), :] = edge
 
 
 def sum_kernel(mine_ref, got_ref, z1, z2, z3, out_ref, score_ref):
@@ -400,7 +426,7 @@
     grad, score = total[0:SCORE_ROW], total[SCORE_ROW:]
     for ref in (z1, z2, z3):
         grad = grad + ref[0:SCORE_ROW, :].astype(F32)
-        pair = ref[SCORE_ROW:, :].astype(F32)
+        pair = ref[SCORE_ROW:HALO_ROW, :].astype(F32)
         score = score + pair[0:PAD] + pair[PAD:]
     out_ref[...] = grad
     half = GROUP_WIDTH // 2
@@ -409,38 +435,39 @@
     )
 
 
-def input_kernel(files, hg_ref, hh_ref, mc_ref, mcr_ref, *refs):
+def input_kernel(files, hg_ref, mine_ref, other_ref, *refs):
     w_refs, outs = refs[: 2 * SLOTS], refs[2 * SLOTS :]
     rows = hg_ref.shape[1]
-    pairs = rows // 2
-    for stream, mref in enumerate((mc_ref, mcr_ref)):
-        since, _ = row_info(mref, pairs, files, rows + PAD)
+    halves = [kernel_halves(w_refs, j) for j in range(SLOTS)]
+    for stream, message in enumerate((mine_ref, other_ref)):
+        since, _ = row_info(message, files)
         for j in range(SLOTS):
-            padded = jnp.concatenate(
-                [
-                    hg_ref[stream, :, lanes(j)].astype(F32),
-                    hh_ref[PAD * stream : PAD * (stream + 1), lanes(j)].astype(F32),
-                ],
-                axis=0,
-            )
-            halves = kernel_halves(w_refs, j)
-            total = jnp.zeros((rows, GROUP_WIDTH), F32)
+            grad = hg_ref[stream, :, lanes(j)].astype(F32)
+            total = jnp.zeros((PAD + rows, GROUP_WIDTH), F32)
             for lag in range(KERNEL):
-                if lag == 0:
-                    window = padded[:rows].astype(BF)
-                else:
-                    kept = jnp.where(since >= lag, padded, 0.0)
-                    window = pltpu.roll(kept, rows + PAD - lag, 0)[:rows].astype(BF)
-                part = halves[lag // 2][GROUP_WIDTH * (lag % 2) : GROUP_WIDTH * (lag % 2 + 1)]
-                total = total + nt(window, part)
-            outs[stream][:, lanes(j)] = total.astype(BF)
-
-
-def place_kernel(own_ref, got_ref, out_ref):
+                kept = grad if lag == 0 else jnp.where(since >= lag, grad, 0.0)
+                window = jnp.concatenate([jnp.zeros((PAD, GROUP_WIDTH), F32), kept], axis=0)
+                if lag > 0:
+                    window = pltpu.roll(window, PAD + rows - lag, 0)
+                part = halves[j][lag // 2][GROUP_WIDTH * (lag % 2) : GROUP_WIDTH * (lag % 2 + 1)]
+                total = total + nt(window.astype(BF), part)
+            outs[stream][:, lanes(j)] = total[PAD:].astype(BF)
+            outs[2 + stream][:, lanes((j + SLOTS - 1) % SLOTS)] = total[0:PAD].astype(BF)
+
+
+def place_kernel(own_ref, got_ref, z1_ref, edge_ref, out_ref):
+    rows = own_ref.shape[0]
     s, d = lax.axis_index("seq"), lax.axis_index("dp")
+    inside = jnp.full((2 * PAD, GROUP_WIDTH), s, jnp.int32) < SLOTS - 1
+    none = jnp.zeros((PAD, GROUP_WIDTH), F32)
     for j in range(SLOTS):
-        out_ref[0, :, group_lanes(slot_group(s, j, d))] = own_ref[:, lanes(j)]
-        out_ref[0, :, group_lanes(slot_group(s, j, 1 - d))] = got_ref[:, lanes(j)]
+        own_edge = z1_ref[HALO_ROW + PAD * j : HALO_ROW + PAD * (j + 1), :]
+        for ref, edge, parity in ((own_ref, own_edge, d), (got_ref, edge_ref[:, lanes(j)], 1 - d)):
+            col = group_lanes(slot_group(s, j, parity))
+            out_ref[0, 0 : rows - 2 * PAD, col] = ref[0 : rows - 2 * PAD, lanes(j)]
+            extra = jnp.where(inside, jnp.concatenate([none, edge.astype(F32)], axis=0), 0.0)
+            last = ref[rows - 2 * PAD :, lanes(j)].astype(F32) + extra
+            out_ref[0, rows - 2 * PAD :, col] = last.astype(BF)
 
 
 def per_device_paired(inputs, conv_weight, score_weight, lengths, offsets, cotangent):
@@ -463,20 +490,27 @@
         return lax.ppermute(value, ("seq", "dp"), pairs_of)
 
     wide = HALO_ROW + PAD * SLOTS
-    mx, mc, mw, mw1, md = call(
+    message = shape((rows + pairs + PAD, HALF), BF)
+    mine, other, mw, mw1, md = call(
         pack_kernel,
         (
-            shape((rows, HALF), BF),
-            shape((pairs + PAD, HALF), BF),
+            message,
+            message,
             shape((HALO_ROW, GROUP_WIDTH), BF),
             shape((wide, GROUP_WIDTH), BF),
             shape((PAD, HALF), BF),
         ),
-        smem=2,
-    )(offsets, lengths, inputs, cotangent, conv_weight, score_weight.reshape(1, -1))
-    mxr = flip(mx, "dp")
+        scratch=(
+            pltpu.SMEM(offsets.shape, jnp.int32),
+            pltpu.VMEM(inputs.shape, BF),
+            pltpu.VMEM(cotangent.shape, BF),
+            pltpu.VMEM((1, score_weight.shape[0]), BF),
+            pltpu.SemaphoreType.DMA((6,)),
+        ),
+        hbm=5,
+    )(*(pltpu.with_memory_space_constraint(v, pltpu.HBM) for v in (offsets, inputs, cotangent, conv_weight, score_weight.reshape(1, -1))), lengths.reshape(1, 1))
+    other = flip(other, "dp")
     shards = [mw, cycle(mw1, 1), cycle(mw, 2), cycle(mw, 3)]
-    mcr = flip(mc, "dp")
     mdr = across(md, 1)
     shards = shards + [flip(w, "fsdp") for w in shards]
     hidden, left, partial = call(
@@ -486,34 +520,43 @@
             shape((2, pairs + PAD, HALF), BF),
             shape((2, 16, GROUP_WIDTH), F32),
         ),
-    )(inputs, cotangent, mxr, mc, mcr, mdr, *shards)
+    )(mine, other, mdr, *shards)
     partial_r = flip(partial, "dp")
     grad_rows = SLOTS * (SCORE_ROW + PAD)
-    hg, hh, mine, send = call(
+    hg, kept, send = call(
         functools.partial(mix_kernel, files),
         (
             shape((2, rows, HALF), BF),
-            shape((2 * PAD, HALF), BF),
             shape((grad_rows, GROUP_WIDTH), F32),
             shape((grad_rows, GROUP_WIDTH), F32),
         ),
-    )(inputs, mxr, mdr, shards[1], mc, mcr, hidden, left, partial, partial_r)
-    hhr = shifted(hh, "seq", -1)
+    )(mine, other, mdr, shards[1], hidden, left, partial, partial_r)
     got = flip(send, "fsdp")
-    sums = call(add_kernel, tuple(shape((HALO_ROW, GROUP_WIDTH), BF) for _ in range(SLOTS - 1)))(
-        mine, got
-    )
-    x_own, x_send = call(
+    x_own, x_send, edge_own, edge_send = call(
         functools.partial(input_kernel, files),
-        (shape((rows, HALF), BF), shape((rows, HALF), BF)),
-    )(hg, hhr, mc, mcr, *shards)
+        (
+            shape((rows, HALF), BF),
+            shape((rows, HALF), BF),
+            shape((PAD, HALF), BF),
+            shape((PAD, HALF), BF),
+        ),
+    )(hg, mine, other, *shards)
     x_got = flip(x_send, "dp")
+    edge_got = across(edge_send, -1)
+    sums = call(
+        add_kernel,
+        (
+            shape((wide, GROUP_WIDTH), BF),
+            shape((HALO_ROW, GROUP_WIDTH), BF),
+            shape((HALO_ROW, GROUP_WIDTH), BF),
+        ),
+    )(kept, got, edge_own)
     final = [cycle(value, -j) for j, value in zip(range(1, SLOTS), sums)]
-    input_grad = call(place_kernel, shape(inputs.shape, BF))(x_own, x_got)
+    input_grad = call(place_kernel, shape(inputs.shape, BF))(x_own, x_got, final[0], edge_got)
     kernel_grad, score_grad = call(
         sum_kernel,
         (shape((SCORE_ROW, GROUP_WIDTH), F32), shape((1, GROUP_WIDTH // 2), F32)),
-    )(mine, got, *final)
+    )(kept, got, *final)
     return (input_grad, kernel_grad, score_grad.reshape(-1))
 
 

time: 49.4 us -> 39.7 us (0.80)
  waiting for transfers between devices: 16.5 us -> 10.2 us
  local copies, waits for them, and re-layouts: 3.47 us -> 0 us
    ppermute x1 -> x0, waiting for transfers between devices: 4.33 us -> none  [shifted(): return lax.ppermute(value, axis, pairs)]
    ppermute x9 -> x8, waiting for transfers between devices: 8.11 us -> 3.85 us  [flip(): return lax.ppermute(value, axis, [(0, 1), (1, 0)])]
    unnamed x12 -> x0, local copies, waits for them, and re-layouts: 3.47 us -> none
    ppermute x6, waiting for transfers between devices: 2.88 us -> 4.87 us  [cycle(): lax.ppermute(value, 'seq', [(i, (i + by) % SLOTS) for i in range(SLOTS)])]
    ppermute x1 -> x0, starting transfers between devices: 1.29 us -> none  [shifted(): return lax.ppermute(value, axis, pairs)]
    ppermute x1 -> x2, starting transfers between devices: 3.44 us -> 4.72 us  [across(): return lax.ppermute(value, ('seq', 'dp'), pairs_of)]
    ppermute x9 -> x8, starting transfers between devices: 5.28 us -> 6.1 us  [flip(): return lax.ppermute(value, axis, [(0, 1), (1, 0)])]
    ppermute x6, starting transfers between devices: 10.3 us -> 9.69 us  [cycle(): lax.ppermute(value, 'seq', [(i, (i + by) % SLOTS) for i in range(SLOTS)])]
  transfers between devices with their start and end apart: 17 -> 16, of which waited for: 7 -> 8; matrix products, arithmetic and copies ran while one was open for 0% -> 0% of each run, Pallas kernels for 5% -> 5%
where the time goes in v2:
time: 39.7 us; the launch traced here: 39.5 us
  starting transfers between devices  20.5 us (52%)
  waiting for transfers between devices  10.2 us (26%)
  Pallas kernels  7.5 us (19%)
  between operations  1.37 us (3%)
    ppermute x6, starting transfers between devices, cycle(): lax.ppermute(value, 'seq', [(i, (i + by) % SLOTS) for i in range(SLOTS)])  9.69 us
    pallas_call x7, Pallas kernels, run(): pl.pallas_call(body, out_shape=out_shape, in_specs=specs, out_specs=jax.t...  7.5 us
    ppermute x8, starting transfers between devices, flip(): return lax.ppermute(value, axis, [(0, 1), (1, 0)])  6.1 us
    ppermute x6, waiting for transfers between devices, cycle(): lax.ppermute(value, 'seq', [(i, (i + by) % SLOTS) for i in range(SLOTS)])  4.87 us
    ppermute x2, starting transfers between devices, across(): return lax.ppermute(value, ('seq', 'dp'), pairs_of)  4.72 us
    ppermute x8, waiting for transfers between devices, flip(): return lax.ppermute(value, axis, [(0, 1), (1, 0)])  3.85 us
    ppermute x2, waiting for transfers between devices, across(): return lax.ppermute(value, ('seq', 'dp'), pairs_of)  1.45 us
  transfers between devices with their start and end apart: 16, of which 8 were waited for; matrix products, arithmetic and copies ran while one was open for 0% of the time, Pallas kernels for 5%

profile of v2, /device:TPU:0, one launch (start us, length us, event | category | flops | bytes accessed | tf_op | source)
XLA Modules:
  0.0 39.5 jit_solution(2429563843460275283)
XLA Ops:
  1.3 1.3 %shard_map.85 = (bf16[368,512]{1,0:T(8,128)(2,1)S(1)}, bf16[368,512]{1,0:T(8,128)(2,1)S(1)}, bf16[272,128]{1,0:T(8,128)(2,1)S(1)}, bf16[304,128]{1,0:T(8,128)(2,1)S(1)}, bf16[8,512]{1,0:T(8,128)(2,1)S(1)}) custom-call(s32[1,16]{1,0:T(1,128)} %off_hbm.1, bf16[1,240,1024]{2,1,0:T(8,128)(2,1)} %x_hbm.1, bf16[1,120,1024]{2,1,0:T(8,128)(2,1)} %c_hbm.1, ...), custom_call_target="tpu_custom_call" | custom-call | tf_op jit(solution)/shard_map/pallas_call | solution.py:169
  2.6 3.0 %collective-permute-start = (bf16[368,512]{1,0:T(8,128)(2,1)S(1)}, bf16[368,512]{1,0:T(8,128)(2,1)S(1)}, u32[]{:S(2)}, u32[]{:S(2)}) collective-permute-start(bf16[368,512]{1,0:T(8,128)(2,1)S(1)} %get-tuple-element.24), channel_id=1, source_target_pairs={{0,2},{2,0},{1,3},{3,1},{4,6},{6,4},{5,7},{7,5},{8,10},{10,8},{9,1... | collective-permute-start | bytes 1130504 | tf_op jit(solution)/shard_map/ppermute | solution.py:478
  5.6 1.6 %collective-permute-start.2 = (bf16[304,128]{1,0:T(8,128)(2,1)S(1)}, bf16[304,128]{1,0:T(8,128)(2,1)S(1)}, u32[]{:S(2)}, u32[]{:S(2)}) collective-permute-start(bf16[304,128]{1,0:T(8,128)(2,1)S(1)} %get-tuple-element.26), channel_id=1, source_target_pairs={{0,4},{4,8},{8,12},{12,0},{1,5},{5,9},{9,13},{13,1},{2,6},{6,10},{... | collective-permute-start | bytes 233480 | tf_op jit(solution)/shard_map/ppermute | solution.py:481
  7.1 2.2 %collective-permute-start.4 = (bf16[272,128]{1,0:T(8,128)(2,1)S(1)}, bf16[272,128]{1,0:T(8,128)(2,1)S(1)}, u32[]{:S(2)}, u32[]{:S(2)}) collective-permute-start(bf16[272,128]{1,0:T(8,128)(2,1)S(1)} %get-tuple-element.27.refs_0_), channel_id=1, source_target_pairs={{0,12},{4,0},{8,4},{12,8},{1,13},{5,1},{9,5},{13,9},{2,14},{6,2},{... | collective-permute-start | bytes 208904 | tf_op jit(solution)/shard_map/ppermute | solution.py:481
  9.4 0.8 %collective-permute-start.3 = (bf16[272,128]{1,0:T(8,128)(2,1)S(1)}, bf16[272,128]{1,0:T(8,128)(2,1)S(1)}, u32[]{:S(2)}, u32[]{:S(2)}) collective-permute-start(bf16[272,128]{1,0:T(8,128)(2,1)S(1)} %get-tuple-element.27.refs_0_), channel_id=1, source_target_pairs={{0,8},{4,12},{8,0},{12,4},{1,9},{5,13},{9,1},{13,5},{2,10},{6,14},... | collective-permute-start | bytes 208904 | tf_op jit(solution)/shard_map/ppermute | solution.py:481
  10.2 3.4 %collective-permute-start.1 = (bf16[8,512]{1,0:T(8,128)(2,1)S(1)}, bf16[8,512]{1,0:T(8,128)(2,1)S(1)}, u32[]{:S(2)}, u32[]{:S(2)}) collective-permute-start(bf16[8,512]{1,0:T(8,128)(2,1)S(1)} %get-tuple-element.25), channel_id=1, source_target_pairs={{0,6},{2,4},{4,10},{6,8},{8,14},{10,12},{1,7},{3,5},{5,11},{7,9},{... | collective-permute-start | bytes 24584 | tf_op jit(solution)/shard_map/ppermute | solution.py:490
  13.7 1.3 %collective-permute-done.1.md_ref = bf16[8,512]{1,0:T(8,128)(2,1)S(1)} collective-permute-done((bf16[8,512]{1,0:T(8,128)(2,1)S(1)}, bf16[8,512]{1,0:T(8,128)(2,1)S(1)}, u32[]{:S(2)}, u32[]{:S(2)}) %collective-permute-start.1) | collective-permute-done | bytes 8224 | tf_op jit(solution)/shard_map/ppermute | solution.py:490
  15.0 0.5 %collective-permute-start.8 = (bf16[272,128]{1,0:T(8,128)(2,1)S(1)}, bf16[272,128]{1,0:T(8,128)(2,1)S(1)}, u32[]{:S(2)}, u32[]{:S(2)}) collective-permute-start(bf16[272,128]{1,0:T(8,128)(2,1)S(1)} %collective-permute-done.4.refs_3_), channel_id=1, source_target_pairs={{0,1},{1,0},{2,3},{3,2},{4,5},{5,4},{6,7},{7,6},{8,9},{9,8},{10,11... | collective-permute-start | bytes 208904 | tf_op jit(solution)/shard_map/ppermute | solution.py:478
  15.5 0.3 collective-permute-done.3.refs_2_
  15.8 0.4 %collective-permute-done.5.refs_4_ = bf16[272,128]{1,0:T(8,128)(2,1)S(1)} collective-permute-done((bf16[272,128]{1,0:T(8,128)(2,1)S(1)}, bf16[272,128]{1,0:T(8,128)(2,1)S(1)}, u32[]{:S(2)}, u32[]{:S(2)}) %collective-permute-start.5) | collective-permute-done | bytes 69664 | tf_op jit(solution)/shard_map/ppermute | solution.py:478
  16.4 0.7 %collective-permute-done.7.refs_6_ = bf16[272,128]{1,0:T(8,128)(2,1)S(1)} collective-permute-done((bf16[272,128]{1,0:T(8,128)(2,1)S(1)}, bf16[272,128]{1,0:T(8,128)(2,1)S(1)}, u32[]{:S(2)}, u32[]{:S(2)}) %collective-permute-start.7) | collective-permute-done | bytes 69664 | tf_op jit(solution)/shard_map/ppermute | solution.py:478
  17.1 1.7 %shard_map.86 = (f32[2,240,512]{2,1,0:T(8,128)S(1)}, bf16[2,128,512]{2,1,0:T(8,128)(2,1)S(1)}, f32[2,16,128]{2,1,0:T(8,128)S(1)}) custom-call(bf16[368,512]{1,0:T(8,128)(2,1)S(1)} %get-tuple-element.23.mine_ref, bf16[368,512]{1,0:T(8,128)(2,1)S(1)} %collective-permute-done.other_ref, bf16[8,512]{1,0:T(8,128)(2,1)S(1)} %collective-permute-done.1.md_ref, ...), custom_call_target="tpu_custom_call" | custom-call | tf_op jit(solution)/shard_map/pallas_call | solution.py:169
  18.8 1.2 %collective-permute-start.9 = (f32[2,16,128]{2,1,0:T(8,128)S(1)}, f32[2,16,128]{2,1,0:T(8,128)S(1)}, u32[]{:S(2)}, u32[]{:S(2)}) collective-permute-start(f32[2,16,128]{2,1,0:T(8,128)S(1)} %get-tuple-element.30.r_ref), channel_id=1, source_target_pairs={{0,2},{2,0},{1,3},{3,1},{4,6},{6,4},{5,7},{7,5},{8,10},{10,8},{9,1... | collective-permute-start | bytes 49160 | tf_op jit(solution)/shard_map/ppermute | solution.py:478
  20.0 2.6 %collective-permute-done.9.rr_ref = f32[2,16,128]{2,1,0:T(8,128)S(1)} collective-permute-done((f32[2,16,128]{2,1,0:T(8,128)S(1)}, f32[2,16,128]{2,1,0:T(8,128)S(1)}, u32[]{:S(2)}, u32[]{:S(2)}) %collective-permute-start.9) | collective-permute-done | bytes 16416 | tf_op jit(solution)/shard_map/ppermute | solution.py:478
  22.6 1.7 %shard_map.87 = (bf16[2,240,512]{2,1,0:T(8,128)(2,1)S(1)}, f32[1056,128]{1,0:T(8,128)S(1)}, f32[1056,128]{1,0:T(8,128)S(1)}) custom-call(bf16[368,512]{1,0:T(8,128)(2,1)S(1)} %get-tuple-element.23.mine_ref, bf16[368,512]{1,0:T(8,128)(2,1)S(1)} %collective-permute-done.other_ref, bf16[8,512]{1,0:T(8,128)(2,1)S(1)} %collective-permute-done.1.md_ref, ...), custom_call_target="tpu_custom_call" | custom-call | tf_op jit(solution)/shard_map/pallas_call | solution.py:169
  24.4 1.1 %shard_map.88 = (bf16[240,512]{1,0:T(8,128)(2,1)S(1)}, bf16[240,512]{1,0:T(8,128)(2,1)S(1)}, bf16[8,512]{1,0:T(8,128)(2,1)S(1)}, bf16[8,512]{1,0:T(8,128)(2,1)S(1)}) custom-call(bf16[2,240,512]{2,1,0:T(8,128)(2,1)S(1)} %get-tuple-element.31.hg_ref, bf16[368,512]{1,0:T(8,128)(2,1)S(1)} %get-tuple-element.23.mine_ref, ...), custom_call_target="tpu_custom_call" | custom-call | tf_op jit(solution)/shard_map/pallas_call | solution.py:169
  25.6 1.2 %collective-permute-start.10 = (bf16[240,512]{1,0:T(8,128)(2,1)S(1)}, bf16[240,512]{1,0:T(8,128)(2,1)S(1)}, u32[]{:S(2)}, u32[]{:S(2)}) collective-permute-start(bf16[240,512]{1,0:T(8,128)(2,1)S(1)} %get-tuple-element.33), channel_id=1, source_target_pairs={{0,2},{2,0},{1,3},{3,1},{4,6},{6,4},{5,7},{7,5},{8,10},{10,8},{9,1... | collective-permute-start | bytes 737288 | tf_op jit(solution)/shard_map/ppermute | solution.py:478
  26.8 3.0 %collective-permute-start.12 = (bf16[304,128]{1,0:T(8,128)(2,1)S(1)}, bf16[304,128]{1,0:T(8,128)(2,1)S(1)}, u32[]{:S(2)}, u32[]{:S(2)}) collective-permute-start(bf16[304,128]{1,0:T(8,128)(2,1)S(1)} %get-tuple-element.37), channel_id=1, source_target_pairs={{0,12},{4,0},{8,4},{12,8},{1,13},{5,1},{9,5},{13,9},{2,14},{6,2},{... | collective-permute-start | bytes 233480 | tf_op jit(solution)/shard_map/ppermute | solution.py:481
  29.9 0.9 %collective-permute-start.14 = (bf16[272,128]{1,0:T(8,128)(2,1)S(1)}, bf16[272,128]{1,0:T(8,128)(2,1)S(1)}, u32[]{:S(2)}, u32[]{:S(2)}) collective-permute-start(bf16[272,128]{1,0:T(8,128)(2,1)S(1)} %get-tuple-element.39), channel_id=1, source_target_pairs={{0,8},{4,12},{8,0},{12,4},{1,9},{5,13},{9,1},{13,5},{2,10},{6,14},... | collective-permute-start | bytes 208904 | tf_op jit(solution)/shard_map/ppermute | solution.py:481
  30.8 1.1 %collective-permute-start.15 = (bf16[272,128]{1,0:T(8,128)(2,1)S(1)}, bf16[272,128]{1,0:T(8,128)(2,1)S(1)}, u32[]{:S(2)}, u32[]{:S(2)}) collective-permute-start(bf16[272,128]{1,0:T(8,128)(2,1)S(1)} %get-tuple-element.40), channel_id=1, source_target_pairs={{0,4},{4,8},{8,12},{12,0},{1,5},{5,9},{9,13},{13,1},{2,6},{6,10},{... | collective-permute-start | bytes 208904 | tf_op jit(solution)/shard_map/ppermute | solution.py:481
  31.9 1.3 %collective-permute-start.13 = (bf16[8,512]{1,0:T(8,128)(2,1)S(1)}, bf16[8,512]{1,0:T(8,128)(2,1)S(1)}, u32[]{:S(2)}, u32[]{:S(2)}) collective-permute-start(bf16[8,512]{1,0:T(8,128)(2,1)S(1)} %get-tuple-element.38), channel_id=1, source_target_pairs={{4,2},{6,0},{8,6},{10,4},{12,10},{14,8},{5,3},{7,1},{9,7},{11,5},{... | collective-permute-start | bytes 24584 | tf_op jit(solution)/shard_map/ppermute | solution.py:490
  33.2 4.5 %collective-permute-done.14.z2 = bf16[272,128]{1,0:T(8,128)(2,1)S(1)} collective-permute-done((bf16[272,128]{1,0:T(8,128)(2,1)S(1)}, bf16[272,128]{1,0:T(8,128)(2,1)S(1)}, u32[]{:S(2)}, u32[]{:S(2)}) %collective-permute-start.14) | collective-permute-done | bytes 69664 | tf_op jit(solution)/shard_map/ppermute | solution.py:481
  37.7 0.7 %shard_map.91 = (f32[256,128]{1,0:T(8,128)}, f32[1,64]{1,0:T(1,128)}) custom-call(f32[1056,128]{1,0:T(8,128)S(1)} %get-tuple-element.34.mine_ref, f32[1056,128]{1,0:T(8,128)S(1)} %collective-permute-done.11.got_ref, bf16[304,128]{1,0:T(8,128)(2,1)S(1)} %collective-permute-done.12.z1_ref.z1, bf16[272,128]{1,0:T(8,128)(2,1)S(1)} %collective-permute-done.14.z2, ...), custom_call_target="tpu_custom_call" | custom-call | tf_op jit(solution)/shard_map/pallas_call | solution.py:169
  38.6 0.9 %shard_map.90 = bf16[1,240,1024]{2,1,0:T(8,128)(2,1)} custom-call(bf16[240,512]{1,0:T(8,128)(2,1)S(1)} %get-tuple-element.32.own_ref, bf16[240,512]{1,0:T(8,128)(2,1)S(1)} %collective-permute-done.10.got_ref, bf16[304,128]{1,0:T(8,128)(2,1)S(1)} %collective-permute-done.12.z1_ref.z1, bf16[8,512]{1,0:T(8,128)(2,1)S(1)} %collective-permute-done.13.edge_ref), custom_call_target="tpu_custom_call" | custom-call | tf_op jit(solution)/shard_map/pallas_call | solution.py:169
  (15 shorter events, 0.6 us)
Async XLA Ops:
  2.6 14.5 %collective-permute-start = (bf16[368,512]{1,0:T(8,128)(2,1)S(1)}, bf16[368,512]{1,0:T(8,128)(2,1)S(1)}, u32[]{:S(2)}, u32[]{:S(2)}) collective-permute-start(bf16[368,512]{1,0:T(8,128)(2,1)S(1)} %get-tuple-element.24), channel_id=1, source_target_pairs={{0,2},{2,0},{1,3},{3,1},{4,6},{6,4},{5,7},{7,5},{8,10},{10,8},{9,1... | collective-permute-start | bytes 1130504 | tf_op jit(solution)/shard_map/ppermute | solution.py:478
  5.6 8.1 %collective-permute-start.2 = (bf16[304,128]{1,0:T(8,128)(2,1)S(1)}, bf16[304,128]{1,0:T(8,128)(2,1)S(1)}, u32[]{:S(2)}, u32[]{:S(2)}) collective-permute-start(bf16[304,128]{1,0:T(8,128)(2,1)S(1)} %get-tuple-element.26), channel_id=1, source_target_pairs={{0,4},{4,8},{8,12},{12,0},{1,5},{5,9},{9,13},{13,1},{2,6},{6,10},{... | collective-permute-start | bytes 233480 | tf_op jit(solution)/shard_map/ppermute | solution.py:481
  7.1 7.8 %collective-permute-start.4 = (bf16[272,128]{1,0:T(8,128)(2,1)S(1)}, bf16[272,128]{1,0:T(8,128)(2,1)S(1)}, u32[]{:S(2)}, u32[]{:S(2)}) collective-permute-start(bf16[272,128]{1,0:T(8,128)(2,1)S(1)} %get-tuple-element.27.refs_0_), channel_id=1, source_target_pairs={{0,12},{4,0},{8,4},{12,8},{1,13},{5,1},{9,5},{13,9},{2,14},{6,2},{... | collective-permute-start | bytes 208904 | tf_op jit(solution)/shard_map/ppermute | solution.py:481
  9.4 6.4 %collective-permute-start.3 = (bf16[272,128]{1,0:T(8,128)(2,1)S(1)}, bf16[272,128]{1,0:T(8,128)(2,1)S(1)}, u32[]{:S(2)}, u32[]{:S(2)}) collective-permute-start(bf16[272,128]{1,0:T(8,128)(2,1)S(1)} %get-tuple-element.27.refs_0_), channel_id=1, source_target_pairs={{0,8},{4,12},{8,0},{12,4},{1,9},{5,13},{9,1},{13,5},{2,10},{6,14},... | collective-permute-start | bytes 208904 | tf_op jit(solution)/shard_map/ppermute | solution.py:481
  10.2 4.8 %collective-permute-start.1 = (bf16[8,512]{1,0:T(8,128)(2,1)S(1)}, bf16[8,512]{1,0:T(8,128)(2,1)S(1)}, u32[]{:S(2)}, u32[]{:S(2)}) collective-permute-start(bf16[8,512]{1,0:T(8,128)(2,1)S(1)} %get-tuple-element.25), channel_id=1, source_target_pairs={{0,6},{2,4},{4,10},{6,8},{8,14},{10,12},{1,7},{3,5},{5,11},{7,9},{... | collective-permute-start | bytes 24584 | tf_op jit(solution)/shard_map/ppermute | solution.py:490
  13.6 3.5 %collective-permute-start.6 = (bf16[304,128]{1,0:T(8,128)(2,1)S(1)}, bf16[304,128]{1,0:T(8,128)(2,1)S(1)}, u32[]{:S(2)}, u32[]{:S(2)}) collective-permute-start(bf16[304,128]{1,0:T(8,128)(2,1)S(1)} %collective-permute-done.2.refs_1_.w1_ref), channel_id=1, source_target_pairs={{0,1},{1,0},{2,3},{3,2},{4,5},{5,4},{6,7},{7,6},{8,9},{9,8},{10,11... | collective-permute-start | bytes 233480 | tf_op jit(solution)/shard_map/ppermute | solution.py:478
  15.0 1.3 %collective-permute-start.5 = (bf16[272,128]{1,0:T(8,128)(2,1)S(1)}, bf16[272,128]{1,0:T(8,128)(2,1)S(1)}, u32[]{:S(2)}, u32[]{:S(2)}) collective-permute-start(bf16[272,128]{1,0:T(8,128)(2,1)S(1)} %get-tuple-element.27.refs_0_), channel_id=1, source_target_pairs={{0,1},{1,0},{2,3},{3,2},{4,5},{5,4},{6,7},{7,6},{8,9},{9,8},{10,11... | collective-permute-start | bytes 208904 | tf_op jit(solution)/shard_map/ppermute | solution.py:478
  15.0 1.4 %collective-permute-start.8 = (bf16[272,128]{1,0:T(8,128)(2,1)S(1)}, bf16[272,128]{1,0:T(8,128)(2,1)S(1)}, u32[]{:S(2)}, u32[]{:S(2)}) collective-permute-start(bf16[272,128]{1,0:T(8,128)(2,1)S(1)} %collective-permute-done.4.refs_3_), channel_id=1, source_target_pairs={{0,1},{1,0},{2,3},{3,2},{4,5},{5,4},{6,7},{7,6},{8,9},{9,8},{10,11... | collective-permute-start | bytes 208904 | tf_op jit(solution)/shard_map/ppermute | solution.py:478
  15.8 1.3 %collective-permute-start.7 = (bf16[272,128]{1,0:T(8,128)(2,1)S(1)}, bf16[272,128]{1,0:T(8,128)(2,1)S(1)}, u32[]{:S(2)}, u32[]{:S(2)}) collective-permute-start(bf16[272,128]{1,0:T(8,128)(2,1)S(1)} %collective-permute-done.3.refs_2_), channel_id=1, source_target_pairs={{0,1},{1,0},{2,3},{3,2},{4,5},{5,4},{6,7},{7,6},{8,9},{9,8},{10,11... | collective-permute-start | bytes 208904 | tf_op jit(solution)/shard_map/ppermute | solution.py:478
  18.8 3.8 %collective-permute-start.9 = (f32[2,16,128]{2,1,0:T(8,128)S(1)}, f32[2,16,128]{2,1,0:T(8,128)S(1)}, u32[]{:S(2)}, u32[]{:S(2)}) collective-permute-start(f32[2,16,128]{2,1,0:T(8,128)S(1)} %get-tuple-element.30.r_ref), channel_id=1, source_target_pairs={{0,2},{2,0},{1,3},{3,1},{4,6},{6,4},{5,7},{7,5},{8,10},{10,8},{9,1... | collective-permute-start | bytes 49160 | tf_op jit(solution)/shard_map/ppermute | solution.py:478
  24.3 2.4 %collective-permute-start.11 = (f32[1056,128]{1,0:T(8,128)S(1)}, f32[1056,128]{1,0:T(8,128)S(1)}, u32[]{:S(2)}, u32[]{:S(2)}) collective-permute-start(f32[1056,128]{1,0:T(8,128)S(1)} %get-tuple-element.35), channel_id=1, source_target_pairs={{0,1},{1,0},{2,3},{3,2},{4,5},{5,4},{6,7},{7,6},{8,9},{9,8},{10,11... | collective-permute-start | bytes 1622024 | tf_op jit(solution)/shard_map/ppermute | solution.py:478
  25.6 13.1 %collective-permute-start.10 = (bf16[240,512]{1,0:T(8,128)(2,1)S(1)}, bf16[240,512]{1,0:T(8,128)(2,1)S(1)}, u32[]{:S(2)}, u32[]{:S(2)}) collective-permute-start(bf16[240,512]{1,0:T(8,128)(2,1)S(1)} %get-tuple-element.33), channel_id=1, source_target_pairs={{0,2},{2,0},{1,3},{3,1},{4,6},{6,4},{5,7},{7,5},{8,10},{10,8},{9,1... | collective-permute-start | bytes 737288 | tf_op jit(solution)/shard_map/ppermute | solution.py:478
  26.8 10.9 %collective-permute-start.12 = (bf16[304,128]{1,0:T(8,128)(2,1)S(1)}, bf16[304,128]{1,0:T(8,128)(2,1)S(1)}, u32[]{:S(2)}, u32[]{:S(2)}) collective-permute-start(bf16[304,128]{1,0:T(8,128)(2,1)S(1)} %get-tuple-element.37), channel_id=1, source_target_pairs={{0,12},{4,0},{8,4},{12,8},{1,13},{5,1},{9,5},{13,9},{2,14},{6,2},{... | collective-permute-start | bytes 233480 | tf_op jit(solution)/shard_map/ppermute | solution.py:481
  29.9 7.8 %collective-permute-start.14 = (bf16[272,128]{1,0:T(8,128)(2,1)S(1)}, bf16[272,128]{1,0:T(8,128)(2,1)S(1)}, u32[]{:S(2)}, u32[]{:S(2)}) collective-permute-start(bf16[272,128]{1,0:T(8,128)(2,1)S(1)} %get-tuple-element.39), channel_id=1, source_target_pairs={{0,8},{4,12},{8,0},{12,4},{1,9},{5,13},{9,1},{13,5},{2,10},{6,14},... | collective-permute-start | bytes 208904 | tf_op jit(solution)/shard_map/ppermute | solution.py:481
  30.8 6.9 %collective-permute-start.15 = (bf16[272,128]{1,0:T(8,128)(2,1)S(1)}, bf16[272,128]{1,0:T(8,128)(2,1)S(1)}, u32[]{:S(2)}, u32[]{:S(2)}) collective-permute-start(bf16[272,128]{1,0:T(8,128)(2,1)S(1)} %get-tuple-element.40), channel_id=1, source_target_pairs={{0,4},{4,8},{8,12},{12,0},{1,5},{5,9},{9,13},{13,1},{2,6},{6,10},{... | collective-permute-start | bytes 208904 | tf_op jit(solution)/shard_map/ppermute | solution.py:481
  31.9 6.7 %collective-permute-start.13 = (bf16[8,512]{1,0:T(8,128)(2,1)S(1)}, bf16[8,512]{1,0:T(8,128)(2,1)S(1)}, u32[]{:S(2)}, u32[]{:S(2)}) collective-permute-start(bf16[8,512]{1,0:T(8,128)(2,1)S(1)} %get-tuple-element.38), channel_id=1, source_target_pairs={{4,2},{6,0},{8,6},{10,4},{12,10},{14,8},{5,3},{7,1},{9,7},{11,5},{... | collective-permute-start | bytes 24584 | tf_op jit(solution)/shard_map/ppermute | solution.py:490

commit v3 on v0

--- a/solution.py
+++ b/solution.py
@@ -1,6 +1,10 @@
+import functools
+
 import jax
 import jax.numpy as jnp
 from jax import lax
+from jax.experimental import pallas as pl
+from jax.experimental.pallas import tpu as pltpu
 from jax.sharding import PartitionSpec as P
 
 GROUPS = 8
@@ -73,7 +77,7 @@
     return (hidden_grad, weight_grad)
 
 
-def per_device(inputs, conv_weight, score_weight, lengths, offsets, cotangent):
+def per_device_general(inputs, conv_weight, score_weight, lengths, offsets, cotangent):
     local_rows = inputs.shape[1]
     width_all = inputs.shape[2]
     kernel_flat, score_full = (
@@ -137,6 +141,549 @@
     return (input_grad, kernel_grad, score_grad)
 
 
+SLOTS = 4
+HALF = SLOTS * GROUP_WIDTH
+PAD = 8
+SCORE_ROW = 2 * GROUP_WIDTH
+HALO_ROW = SCORE_ROW + 16
+SHARD = HALO_ROW
+AHEAD = 4
+HEAD = 6
+BF = jnp.bfloat16
+F32 = jnp.float32
+
+
+def lanes(slot):
+    return slice(slot * GROUP_WIDTH, (slot + 1) * GROUP_WIDTH)
+
+
+def group_lanes(group):
+    return pl.ds(pl.multiple_of(group * GROUP_WIDTH, GROUP_WIDTH), GROUP_WIDTH)
+
+
+def slot_group(seq, slot, parity):
+    return 2 * lax.rem(seq - slot + 2 * SLOTS, SLOTS) + parity
+
+
+def call(body, out_shape, scratch=(), hbm=0, cost=None):
+    def run(*args):
+        specs = [pl.BlockSpec(memory_space=pltpu.HBM)] * hbm
+        specs += [pl.BlockSpec(memory_space=pltpu.VMEM)] * (len(args) - hbm)
+        return pl.pallas_call(
+            body,
+            out_shape=out_shape,
+            in_specs=specs,
+            out_specs=jax.tree.map(lambda _: pl.BlockSpec(memory_space=pltpu.VMEM), out_shape),
+            scratch_shapes=list(scratch),
+            cost_estimate=cost,
+            compiler_params=pltpu.CompilerParams(vmem_limit_bytes=48 * 1024 * 1024),
+        )(*args)
+
+    return run
+
+
+def appended(half, slot):
+    first = HALO_ROW + PAD * (SLOTS * half + slot)
+    return slice(first, first + PAD)
+
+
+def pack_kernel(off_hbm, x_hbm, c_hbm, w_hbm, score_hbm, len_ref, mine, other, mw1, mw2, mw3,
+                off_ref, x_ref, c_ref, score_ref, sems):
+    rows, pairs, files = x_ref.shape[1], c_ref.shape[1], off_ref.shape[1]
+    s, d, f = (lax.axis_index(name) for name in ("seq", "dp", "fsdp"))
+    copies = [
+        pltpu.make_async_copy(source, target, sems.at[i])
+        for i, (source, target) in enumerate(
+            (
+                (x_hbm, x_ref),
+                (c_hbm, c_ref),
+                (off_hbm, off_ref),
+                (score_hbm, score_ref),
+                (w_hbm, mw1.at[0:SCORE_ROW]),
+                (w_hbm, mw2.at[0:SCORE_ROW]),
+                (w_hbm, mw3.at[0:SCORE_ROW]),
+            )
+        )
+    ]
+    for copy in copies:
+        copy.start()
+    for copy in copies[2:4]:
+        copy.wait()
+    lane = lax.broadcasted_iota(jnp.int32, (PAD, GROUP_WIDTH), 1)
+    tile_row = lax.broadcasted_iota(jnp.int32, (PAD, GROUP_WIDTH), 0)
+    start = s * rows
+    info = jnp.zeros((PAD, GROUP_WIDTH), jnp.int32)
+    for i in range(files):
+        info = jnp.where(lane == i, jnp.clip(off_ref[0, i] - start, -4, rows + PAD), info)
+    info = jnp.where(lane == files, jnp.clip(len_ref[0:1, 0:1] - start, 0, rows + PAD), info)
+    info = (info.astype(F32) * 0.25).astype(BF)
+    value = score_ref[...].astype(F32)
+    both = jnp.concatenate([value, value], axis=1)
+    half = lax.broadcasted_iota(jnp.int32, (16, GROUP_WIDTH), 1) // (GROUP_WIDTH // 2)
+    row = lax.broadcasted_iota(jnp.int32, (16, GROUP_WIDTH), 0)
+    block = jnp.where((half == f) & (row == 0), jnp.broadcast_to(both, (16, GROUP_WIDTH)), 0.0)
+    for ref in (mw1, mw2, mw3):
+        ref[SCORE_ROW:HALO_ROW, :] = block.astype(BF)
+    copies[0].wait()
+    for ref, parity in ((other, 1 - d), (mine, d)):
+        for j in range(SLOTS):
+            ref[0:rows, lanes(j)] = x_ref[0, :, group_lanes(slot_group(s, j, parity))]
+    for half, parity in ((0, d), (1, 1 - d)):
+        for j in range(SLOTS):
+            after = group_lanes(slot_group(s + 1, j, parity))
+            mw1[appended(half, j), :] = x_ref[0, rows - PAD :, after]
+    copies[1].wait()
+    for ref, parity in ((other, 1 - d), (mine, d)):
+        for j in range(SLOTS):
+            col = group_lanes(slot_group(s, j, parity))
+            ref[rows : rows + pairs, lanes(j)] = c_ref[0, :, col]
+        ref[rows + pairs :, :] = jnp.zeros((PAD, HALF), BF)
+        ref[rows + pairs :, lanes(0)] = info
+    for half, parity in ((0, d), (1, 1 - d)):
+        for j in range(SLOTS):
+            before = group_lanes(slot_group(s - 1, j, parity))
+            moved = pltpu.roll(c_ref[0, 0:PAD, before].astype(F32), HEAD, 0)
+            head = jnp.where(tile_row < HEAD, x_ref[0, 0:PAD, before].astype(F32), moved)
+            mw3[appended(half, j), :] = head.astype(BF)
+    for copy in copies[4:]:
+        copy.wait()
+
+
+def join_kernel(w0, w1, w2, w3, joined, halo_own, halo_flip):
+    for j, ref in enumerate((w0, w1, w2, w3)):
+        joined[SHARD * j : SHARD * (j + 1), :] = ref[0:SHARD, :]
+    for half, out in enumerate((halo_own, halo_flip)):
+        for j in range(SLOTS):
+            out[0:PAD, lanes(j)] = w1[appended(half, j), :]
+            out[PAD:, lanes(j)] = w3[appended(half, j), :]
+
+
+def row_info(message, files, first, count):
+    info = message[message.shape[0] - PAD :, lanes(0)].astype(F32)[0:1] * 4.0
+    lane = lax.broadcasted_iota(jnp.int32, (1, GROUP_WIDTH), 1)
+    length = jnp.sum(jnp.where(lane == files, info, 0.0), axis=1, keepdims=True)
+    pos = lax.broadcasted_iota(jnp.int32, (count, GROUP_WIDTH), 0).astype(F32) + first
+    starts = jnp.where((lane < files) & (info <= pos), info, -4096.0)
+    since = pos - jnp.max(starts, axis=1, keepdims=True)
+    return since, (pos < length).astype(F32)
+
+
+def block_weights(count, ahead=0, start=0):
+    q = lax.broadcasted_iota(jnp.int32, (count, GROUP_WIDTH), 0)
+    r = lax.broadcasted_iota(jnp.int32, (count, GROUP_WIDTH), 1)
+    if ahead:
+        q = jnp.where(q < start, q, q + (ahead - start))
+
+    def over(value, size):
+        if size == 1:
+            return value
+        if size == 3:
+            return lax.shift_right_logical(value * 21846, 16)
+        return lax.shift_right_logical(value, size // 2)
+
+    return [
+        [
+            jnp.where(over(q, size) == over(2 * r + odd, size), 1.0 / size, 0.0).astype(F32)
+            for size in range(1, 5)
+        ]
+        for odd in range(2)
+    ]
+
+
+def message_rows(message):
+    return (message.shape[0] - PAD) // 3 * 2
+
+
+def windows_of(message, tail, j, since):
+    value = message[0 : message_rows(message), lanes(j)]
+    padded = jnp.concatenate([tail.astype(F32), value.astype(F32)], axis=0)
+    out = [value]
+    for lag in range(1, KERNEL):
+        moved = pltpu.roll(padded, lag, 0)[PAD:]
+        out.append(jnp.where(since >= lag, moved, 0.0).astype(BF))
+    return out
+
+
+def edge_windows_of(message, halo_ref, j, since):
+    rows = message_rows(message)
+    none = jnp.zeros((PAD, GROUP_WIDTH), F32)
+    halo = halo_ref[:, lanes(j)].astype(F32)
+    last = message[rows - 2 * PAD : rows, lanes(j)].astype(F32)[PAD:]
+    before = jnp.concatenate([halo[:PAD], none], axis=0)
+    after = jnp.concatenate([last, halo[PAD:]], axis=0)
+    out = []
+    for lag in range(KERNEL):
+        shift = [pltpu.roll(v, lag, 0)[PAD:] if lag else v[PAD:] for v in (before, after)]
+        moved = jnp.concatenate(shift, axis=0)
+        out.append(jnp.where(since >= lag, moved, 0.0).astype(BF))
+    return out
+
+
+def kernel_rows(w_refs, j):
+    return jnp.concatenate(kernel_halves(w_refs, j), axis=0)
+
+
+def kernel_halves(w_refs, j):
+    f = lax.axis_index("fsdp")
+    mine, theirs = (ref[SHARD * j : SHARD * j + SCORE_ROW, :] for ref in w_refs)
+    first = jnp.full((SCORE_ROW, GROUP_WIDTH), f, jnp.int32) == 0
+    return jnp.where(first, mine, theirs), jnp.where(first, theirs, mine)
+
+
+def nt(a, b):
+    return lax.dot_general(a, b, (((1,), (1,)), ((), ())), preferred_element_type=F32)
+
+
+def two_terms(value):
+    high = value.astype(BF)
+    return high, (value - high.astype(F32)).astype(BF)
+
+
+def gram_of(hidden, left):
+    a, b = two_terms(hidden)
+    return nt(a, left) + nt(b, left)
+
+
+def block_sums(weights, gram, column):
+    inner = [
+        jnp.sum(weights[odd][b] * gram, axis=0, keepdims=True) * 0.5
+        for odd in range(2)
+        for b in range(4)
+    ]
+    logit = [
+        jnp.sum(weights[odd][b] * column, axis=0, keepdims=True)
+        for odd in range(2)
+        for b in range(4)
+    ]
+    return jnp.concatenate(inner + logit, axis=0)
+
+
+def hidden_kernel(files, mine_ref, other_ref, wm_ref, wt_ref, h_out, l_out, r_out):
+    messages = (mine_ref, other_ref)
+    rows = h_out.shape[1]
+    pairs = rows // 2
+    infos = [row_info(ref, files, 0, rows) for ref in messages]
+    row = lax.broadcasted_iota(jnp.int32, (PAD, GROUP_WIDTH), 0)
+    none = jnp.zeros((PAD, GROUP_WIDTH), F32)
+    for j in range(SLOTS):
+        kernel = kernel_rows((wm_ref, wt_ref), j)
+        score_rows = slice(SHARD * j + SCORE_ROW, SHARD * (j + 1))
+        score = wm_ref[score_rows, :].astype(F32) + wt_ref[score_rows, :].astype(F32)
+        score = jnp.where(row == AHEAD, jnp.broadcast_to(score[0:1], row.shape), 0.0)
+        for stream in range(2):
+            since, valid = infos[stream]
+            win = jnp.concatenate(windows_of(messages[stream], none, j, since), axis=1)
+            hidden = jnp.dot(win, kernel, preferred_element_type=F32)
+            h_out[stream, :, lanes(j)] = hidden * valid
+            cot = messages[stream][rows : rows + pairs, lanes(j)]
+            left = jnp.concatenate([cot.astype(F32), score], axis=0).astype(BF)
+            l_out[stream, :, lanes(j)] = left
+    weights = block_weights(rows)
+    scored = pairs + AHEAD
+    for stream in range(2):
+        gram = gram_of(h_out[stream], l_out[stream])
+        r_out[stream] = block_sums(weights, gram, gram[:, scored : scored + 1])
+
+
+def edge_info(message, files):
+    rows = message_rows(message)
+    first, ahead = row_info(message, files, 0, PAD), row_info(message, files, rows, PAD)
+    return [jnp.concatenate(pair, axis=0) for pair in zip(first, ahead)]
+
+
+def edge_hidden_kernel(files, mine_ref, other_ref, own_halo, other_halo, wm_ref, wt_ref, l_ref,
+                       r_ref, h_out, l_out, r_out):
+    messages, halos = (mine_ref, other_ref), (own_halo, other_halo)
+    rows = message_rows(mine_ref)
+    kept = rows // 2 - PAD
+    infos = [edge_info(ref, files) for ref in messages]
+    row = lax.broadcasted_iota(jnp.int32, (2 * PAD, GROUP_WIDTH), 0)
+    for stream in range(2):
+        l_out[stream, 0:kept, :] = l_ref[stream, 0:kept, :]
+    for j in range(SLOTS):
+        kernel = kernel_rows((wm_ref, wt_ref), j)
+        wins = [
+            jnp.concatenate(edge_windows_of(messages[i], halos[i], j, infos[i][0]), axis=1)
+            for i in range(2)
+        ]
+        hidden = jnp.dot(jnp.concatenate(wins, axis=0), kernel, preferred_element_type=F32)
+        for stream in range(2):
+            block = hidden[2 * PAD * stream : 2 * PAD * (stream + 1)]
+            h_out[stream, :, lanes(j)] = block * infos[stream][1]
+            head = halos[stream][:, lanes(j)].astype(F32)
+            head = pltpu.roll(head, 2 * PAD - HEAD, 0)
+            old = l_ref[stream, kept:, lanes(j)].astype(F32)
+            take = (row >= PAD) & (row < PAD + 2)
+            l_out[stream, kept:, lanes(j)] = jnp.where(take, head, old).astype(BF)
+    weights = block_weights(2 * PAD, rows, PAD)
+    scored = rows // 2 + AHEAD
+    for stream in range(2):
+        gram = gram_of(h_out[stream], l_out[stream])
+        column = gram[:, scored : scored + 1]
+        r_out[stream] = r_ref[stream] + block_sums(weights, gram, column)
+
+
+def window_kernel(files, mine_ref, other_ref, own_halo, other_halo, after_ref, out_ref):
+    del after_ref
+    for stream, (message, halo) in enumerate(((mine_ref, own_halo), (other_ref, other_halo))):
+        since, _ = row_info(message, files, 0, message_rows(message))
+        for j in range(SLOTS):
+            win = windows_of(message, halo[0:PAD, lanes(j)], j, since)
+            for lag in range(KERNEL):
+                value = jnp.concatenate([win[lag], jnp.zeros((2 * PAD, GROUP_WIDTH), BF)], axis=0)
+                span = value.shape[0]
+                out_ref[j, lanes(lag), span * stream : span * (stream + 1)] = value.T
+
+
+def mixing(weights, total, count):
+    spread = jnp.zeros((count, GROUP_WIDTH), F32)
+    carry = jnp.zeros((count, GROUP_WIDTH), F32)
+    for odd in range(2):
+        for b in range(4):
+            choose, change = total[odd][b]
+            spread = spread + weights[odd][b] * choose
+            carry = carry + weights[odd][b] * change
+    return spread, jnp.sum(carry, axis=1, keepdims=True)
+
+
+def mix_kernel(files, mine_ref, other_ref, win_ref, h_ref, he_ref, l_ref, r_ref, rr_ref,
+               hg_out, hx_out, mine_out, send_out):
+    messages = (mine_ref, other_ref)
+    rows = h_ref.shape[1]
+    scored = rows // 2 + AHEAD
+    f = lax.axis_index("fsdp")
+    weights = block_weights(rows)
+    edge_weights = block_weights(2 * PAD, rows, PAD)
+    columns = []
+    for stream in range(2):
+        summed = r_ref[stream] + rr_ref[1 - stream]
+        total = []
+        for odd in range(2):
+            inner = [summed[4 * odd + b : 4 * odd + b + 1] for b in range(4)]
+            logit = [summed[8 + 4 * odd + b : 8 + 4 * odd + b + 1] for b in range(4)]
+            top = jnp.maximum(jnp.maximum(logit[0], logit[1]), jnp.maximum(logit[2], logit[3]))
+            powers = [jnp.exp(v - top) for v in logit]
+            scale = 1.0 / (powers[0] + powers[1] + powers[2] + powers[3])
+            choose = [v * scale for v in powers]
+            mean = sum(c * m for c, m in zip(choose, inner))
+            total.append([(c * 0.5, c * (m - mean)) for c, m in zip(choose, inner)])
+        parts = (
+            (weights, rows, row_info(messages[stream], files, 0, rows)[1]),
+            (edge_weights, 2 * PAD, edge_info(messages[stream], files)[1]),
+        )
+        terms = []
+        for part_weights, count, valid in parts:
+            spread, e = mixing(part_weights, total, count)
+            lane = lax.broadcasted_iota(jnp.int32, (count, GROUP_WIDTH), 1)
+            terms.append(two_terms(jnp.where(lane == scored, e, spread) * valid))
+            if count == rows:
+                columns.append(e)
+        left = l_ref[stream]
+        grad = jnp.dot(
+            jnp.concatenate([jnp.concatenate(pair, axis=1) for pair in terms], axis=0),
+            jnp.concatenate([left, left], axis=0),
+            preferred_element_type=F32,
+        ).astype(BF)
+        hg_out[stream] = grad[:rows]
+        hx_out[stream] = grad[rows:]
+    first = jnp.full((SCORE_ROW, GROUP_WIDTH), f, jnp.int32) == 0
+    row = lax.broadcasted_iota(jnp.int32, (PAD, GROUP_WIDTH), 0)
+    for j in range(SLOTS):
+        none = jnp.zeros((2 * PAD, GROUP_WIDTH), BF)
+        grads = [v for i in range(2) for v in (hg_out[i, :, lanes(j)], none)]
+        both = jnp.dot(
+            win_ref[j], jnp.concatenate(grads, axis=0), preferred_element_type=F32
+        )
+        low, high = both[:SCORE_ROW], both[SCORE_ROW:]
+        score = jnp.zeros((1, GROUP_WIDTH), F32)
+        for stream in range(2):
+            value = columns[stream] * h_ref[stream, :, lanes(j)]
+            edge = columns[stream][0:PAD] * he_ref[stream, 0:PAD, lanes(j)]
+            score = score + jnp.sum(value, axis=0, keepdims=True)
+            score = score + jnp.sum(edge, axis=0, keepdims=True)
+        base = j * (SCORE_ROW + PAD)
+        score = jnp.where(row == 0, jnp.broadcast_to(score, row.shape), 0.0)
+        mine_out[base : base + SCORE_ROW, :] = jnp.where(first, low, high)
+        send_out[base : base + SCORE_ROW, :] = jnp.where(first, high, low)
+        mine_out[base + SCORE_ROW : base + SCORE_ROW + PAD, :] = score
+        send_out[base + SCORE_ROW : base + SCORE_ROW + PAD, :] = score
+
+
+def add_kernel(kept_ref, got_ref, *outs):
+    for j, out in zip(range(1, SLOTS), outs):
+        base = j * (SCORE_ROW + PAD)
+        total = kept_ref[base : base + SCORE_ROW + PAD, :] + got_ref[base : base + SCORE_ROW + PAD, :]
+        out[0:SCORE_ROW, :] = total[0:SCORE_ROW].astype(BF)
+        a, b = two_terms(total[SCORE_ROW:])
+        out[SCORE_ROW:, :] = jnp.concatenate([a.astype(F32), b.astype(F32)], axis=0).astype(BF)
+
+
+def input_half(files, stream, hg_ref, hx_ref, message, w_refs, out):
+    rows = hg_ref.shape[1]
+    since, _ = row_info(message, files, 0, rows + PAD)
+    for j in range(SLOTS):
+        halves = kernel_halves(w_refs, j)
+        ahead = hx_ref[stream, :, lanes(j)].astype(F32)[PAD:]
+        grad = jnp.concatenate([hg_ref[stream, :, lanes(j)].astype(F32), ahead], axis=0)
+        total = jnp.zeros((rows + PAD, GROUP_WIDTH), F32)
+        for lag in range(KERNEL):
+            window = grad if lag == 0 else jnp.where(since >= lag, grad, 0.0)
+            if lag > 0:
+                window = pltpu.roll(window, rows + PAD - lag, 0)
+            part = halves[lag // 2][GROUP_WIDTH * (lag % 2) : GROUP_WIDTH * (lag % 2 + 1)]
+            total = total + nt(window.astype(BF), part)
+        out[:, lanes(j)] = total[:rows].astype(BF)
+
+
+def send_kernel(files, hg_ref, hx_ref, other_ref, wm_ref, wt_ref, out):
+    input_half(files, 1, hg_ref, hx_ref, other_ref, (wm_ref, wt_ref), out)
+
+
+def own_kernel(files, hg_ref, hx_ref, mine_ref, wm_ref, wt_ref, x_out, value_ref, sems):
+    input_half(files, 0, hg_ref, hx_ref, mine_ref, (wm_ref, wt_ref), value_ref)
+    for copy in half_copies(value_ref, x_out, lax.axis_index("dp"), sems):
+        copy.wait()
+
+
+def half_copies(value_ref, x_out, parity, sems):
+    s = lax.axis_index("seq")
+    copies = [
+        pltpu.make_async_copy(
+            value_ref.at[:, lanes(j)],
+            x_out.at[0, :, group_lanes(slot_group(s, j, parity))],
+            sems.at[j],
+        )
+        for j in range(SLOTS)
+    ]
+    for copy in copies:
+        copy.start()
+    return copies
+
+
+def finish_kernel(kept_ref, got_ref, z1, z2, z3, x_got_ref, x_hbm,
+                  x_out, grad_out, score_out, grad_ref, score_ref, sems):
+    del x_hbm
+    f = lax.axis_index("fsdp")
+    copies = half_copies(x_got_ref, x_out, 1 - lax.axis_index("dp"), sems)
+    total = kept_ref[0 : SCORE_ROW + PAD, :] + got_ref[0 : SCORE_ROW + PAD, :]
+    grad, score = total[0:SCORE_ROW], total[SCORE_ROW:]
+    for ref in (z1, z2, z3):
+        grad = grad + ref[0:SCORE_ROW, :].astype(F32)
+        pair = ref[SCORE_ROW:, :].astype(F32)
+        score = score + pair[0:PAD] + pair[PAD:]
+    grad_ref[...] = grad
+    copy_grad = pltpu.make_async_copy(grad_ref, grad_out, sems.at[SLOTS])
+    copy_grad.start()
+    half = GROUP_WIDTH // 2
+    score_ref[...] = jnp.where(
+        jnp.full((1, half), f, jnp.int32) == 0, score[0:1, :half], score[0:1, half:]
+    )
+    copy_score = pltpu.make_async_copy(score_ref, score_out, sems.at[SLOTS + 1])
+    copy_score.start()
+    for copy in copies + [copy_grad, copy_score]:
+        copy.wait()
+
+
+def per_device_paired(inputs, conv_weight, score_weight, lengths, offsets, cotangent):
+    rows, pairs, files = inputs.shape[1], cotangent.shape[1], offsets.shape[1]
+    shape = jax.ShapeDtypeStruct
+
+    def flip(value, axis):
+        return lax.ppermute(value, axis, [(0, 1), (1, 0)])
+
+    def cycle(value, by):
+        return lax.ppermute(value, "seq", [(i, (i + by) % SLOTS) for i in range(SLOTS)])
+
+    message = shape((rows + pairs + PAD, HALF), BF)
+    mine, other, mw1, mw2, mw3 = call(
+        pack_kernel,
+        (
+            message,
+            message,
+            shape((HALO_ROW + 2 * PAD * SLOTS, GROUP_WIDTH), BF),
+            shape((HALO_ROW, GROUP_WIDTH), BF),
+            shape((HALO_ROW + 2 * PAD * SLOTS, GROUP_WIDTH), BF),
+        ),
+        scratch=(
+            pltpu.SMEM(offsets.shape, jnp.int32),
+            pltpu.VMEM(inputs.shape, BF),
+            pltpu.VMEM(cotangent.shape, BF),
+            pltpu.VMEM((1, score_weight.shape[0]), BF),
+            pltpu.SemaphoreType.DMA((7,)),
+        ),
+        hbm=5,
+    )(*(pltpu.with_memory_space_constraint(v, pltpu.HBM) for v in (offsets, inputs, cotangent, conv_weight, score_weight.reshape(1, -1))), lengths.reshape(1, 1))
+    other = flip(other, "dp")
+    halo = shape((2 * PAD, HALF), BF)
+    kernel_mine, halo_own, halo_other = call(
+        join_kernel, (shape((SLOTS * SHARD, GROUP_WIDTH), BF), halo, halo)
+    )(mw2, cycle(mw1, 1), cycle(mw2, 2), cycle(mw3, 3))
+    halo_other = flip(halo_other, "dp")
+    shards = (kernel_mine, flip(kernel_mine, "fsdp"))
+    left = shape((2, pairs + PAD, HALF), BF)
+    sums = shape((2, 16, GROUP_WIDTH), F32)
+    hidden, left_main, partial = call(
+        functools.partial(hidden_kernel, files), (shape((2, rows, HALF), F32), left, sums)
+    )(mine, other, *shards)
+    edge_hidden, left, partial = call(
+        functools.partial(edge_hidden_kernel, files),
+        (shape((2, 2 * PAD, HALF), F32), left, sums),
+    )(mine, other, halo_own, halo_other, *shards, left_main, partial)
+    partial_r = flip(partial, "dp")
+    windows = call(
+        functools.partial(window_kernel, files),
+        shape((SLOTS, KERNEL * GROUP_WIDTH, 2 * (rows + 2 * PAD)), BF),
+        cost=pl.CostEstimate(flops=0, transcendentals=0, bytes_accessed=2 * 1024 * 1024),
+    )(mine, other, halo_own, halo_other, partial)
+    grad_rows = SLOTS * (SCORE_ROW + PAD)
+    hg, hg_ahead, kept, send = call(
+        functools.partial(mix_kernel, files),
+        (
+            shape((2, rows, HALF), BF),
+            shape((2, 2 * PAD, HALF), BF),
+            shape((grad_rows, GROUP_WIDTH), F32),
+            shape((grad_rows, GROUP_WIDTH), F32),
+        ),
+    )(mine, other, windows, hidden, edge_hidden, left, partial, partial_r)
+    got = flip(send, "fsdp")
+    x_send = call(functools.partial(send_kernel, files), shape((rows, HALF), BF))(
+        hg, hg_ahead, other, *shards
+    )
+    x_got = flip(x_send, "dp")
+    summed = shape((HALO_ROW, GROUP_WIDTH), BF)
+    sums = call(add_kernel, (summed, summed, summed))(kept, got)
+    final = [cycle(value, -j) for j, value in zip(range(1, SLOTS), sums)]
+    vmem, hbm = pl.BlockSpec(memory_space=pltpu.VMEM), pl.BlockSpec(memory_space=pltpu.HBM)
+    params = pltpu.CompilerParams(vmem_limit_bytes=48 * 1024 * 1024)
+    input_grad = pl.pallas_call(
+        functools.partial(own_kernel, files),
+        out_shape=shape(inputs.shape, BF),
+        in_specs=[vmem] * 5,
+        out_specs=hbm,
+        scratch_shapes=[pltpu.VMEM((rows, HALF), BF), pltpu.SemaphoreType.DMA((SLOTS,))],
+        compiler_params=params,
+        cost_estimate=pl.CostEstimate(flops=0, transcendentals=0, bytes_accessed=4 * 1024 * 1024),
+    )(hg, hg_ahead, mine, *shards)
+    input_grad, kernel_grad, score_grad = pl.pallas_call(
+        finish_kernel,
+        out_shape=(
+            shape(inputs.shape, BF),
+            shape((SCORE_ROW, GROUP_WIDTH), F32),
+            shape((1, GROUP_WIDTH // 2), F32),
+        ),
+        in_specs=[vmem] * 6 + [hbm],
+        out_specs=(hbm, hbm, hbm),
+        scratch_shapes=[
+            pltpu.VMEM((SCORE_ROW, GROUP_WIDTH), F32),
+            pltpu.VMEM((1, GROUP_WIDTH // 2), F32),
+            pltpu.SemaphoreType.DMA((SLOTS + 2,)),
+        ],
+        input_output_aliases={6: 0},
+        compiler_params=params,
+    )(kept, got, *final, x_got, input_grad)
+    return (input_grad, kernel_grad, score_grad.reshape(-1))
+
+
 def solution(mesh):
     placed = (
         P(("parts", "dp", "fsdp"), "seq", None),
@@ -146,8 +693,9 @@
         P(("parts", "dp", "fsdp"), None),
         P(("parts", "dp", "fsdp"), "seq", None),
     )
+    paired = mesh.shape["seq"] == SLOTS and mesh.shape["dp"] == 2 and mesh.shape["fsdp"] == 2
     return jax.shard_map(
-        per_device,
+        per_device_paired if paired else per_device_general,
         mesh=mesh,
         in_specs=placed,
         out_specs=(

time: 174 us -> 38.2 us (0.22)
  blocking collectives: 61.6 us -> 0 us
  local copies, waits for them, and re-layouts: 39.8 us -> 0 us
  other arithmetic: 26 us -> 0 us
  between operations: 16.8 us -> 1.36 us
  matrix products: 8.95 us -> 0 us
  Pallas kernels: 0 us -> 8.39 us
  starting transfers between devices: 6.41 us -> 12.4 us
  waiting for transfers between devices: 13.5 us -> 16 us
    unnamed x2 -> x0, blocking collectives: 61.6 us -> none
    reshape x11 -> x0, local copies, waits for them, and re-layouts: 16 us -> none  [the longest x6 10.4 us: mix_backward(): hidden_grad = hidden_grad + jnp.repeat(block_term, block_size, axis=0)]
    ppermute x2 -> x12, waiting for transfers between devices: 0.01 us -> 16 us  [the longest x6 8.25 us: cycle(): lax.ppermute(value, 'seq', [(i, (i + by) % SLOTS) for i in range(SLOTS)])]
    reduce_sum x14 -> x0, other arithmetic: 13.9 us -> none  [the longest x3 8.34 us: mix_backward(): block_mix = (choose_prob[block_size - 1][:, None] * mix_grad).reshape(row...]
    reduce_scatter x1 -> x0, waiting for transfers between devices: 12.8 us -> none  [per_device(): lax.psum_scatter(kernel_part, ('seq', 'dp', 'fsdp'), scatter_dimension=0,...]
    dot_general x20 -> x0, matrix products: 8.95 us -> none  [the longest x4 2.91 us: per_device(): jnp.einsum('ngc,gco->ngo', window, kernel_full[:, tap_index], preferred_e...]
    pallas_call x0 -> x10, Pallas kernels: none -> 8.39 us  [the longest x8 6.17 us: run(): pl.pallas_call(body, out_shape=out_shape, in_specs=specs, out_specs=jax.t...]
    unnamed x92 -> x0, local copies, waits for them, and re-layouts: 6.74 us -> none
  transfers between devices with their start and end apart: 4 -> 12, of which waited for: 1 -> 7; matrix products, arithmetic and copies ran while one was open for 12% -> 0% of each run, Pallas kernels for 0% -> 12%
where the time goes in v3:
time: 38.2 us; the launch traced here: 38.1 us
  waiting for transfers between devices  16 us (42%)
  starting transfers between devices  12.4 us (32%)
  Pallas kernels  8.39 us (22%)
  between operations  1.36 us (4%)
    ppermute x6, waiting for transfers between devices, cycle(): lax.ppermute(value, 'seq', [(i, (i + by) % SLOTS) for i in range(SLOTS)])  8.25 us
    ppermute x6, waiting for transfers between devices, flip(): return lax.ppermute(value, axis, [(0, 1), (1, 0)])  7.7 us
    ppermute x6, starting transfers between devices, cycle(): lax.ppermute(value, 'seq', [(i, (i + by) % SLOTS) for i in range(SLOTS)])  7.43 us
    pallas_call x8, Pallas kernels, run(): pl.pallas_call(body, out_shape=out_shape, in_specs=specs, out_specs=jax.t...  6.17 us
    ppermute x6, starting transfers between devices, flip(): return lax.ppermute(value, axis, [(0, 1), (1, 0)])  4.95 us
    pallas_call x1, Pallas kernels, per_device_paired(): pl.pallas_call(functools.partial(own_kernel, files), out_shape=shape(inpu...  1.41 us
    pallas_call x1, Pallas kernels, per_device_paired(): pl.pallas_call(finish_kernel, out_shape=(shape(inputs.shape, BF), shape((...  0.81 us
  transfers between devices with their start and end apart: 12, of which 7 were waited for; matrix products, arithmetic and copies ran while one was open for 0% of the time, Pallas kernels for 12%

profile of v3, /device:TPU:0, one launch (start us, length us, event | category | flops | bytes accessed | tf_op | source)
XLA Modules:
  0.0 38.1 jit_solution(6774864390670655635)
XLA Ops:
  1.3 1.3 %shard_map.85 = (bf16[368,512]{1,0:T(8,128)(2,1)S(1)}, bf16[368,512]{1,0:T(8,128)(2,1)S(1)}, bf16[336,128]{1,0:T(8,128)(2,1)S(1)}, bf16[272,128]{1,0:T(8,128)(2,1)S(1)}, bf16[336,128]{1,0:T(8,128)(2,1)S(1)}) custom-call(s32[1,16]{1,0:T(1,128)} %off_hbm.1, bf16[1,240,1024]{2,1,0:T(8,128)(2,1)} %x_hbm.1, bf16[1,120,1024]{2,1,0:T(8,128)(2,1)} %c_hbm.1, ...), custom_call_target="tpu_custom_call" | custom-call | tf_op jit(solution)/shard_map/pallas_call | solution.py:172
  2.6 3.0 %collective-permute-start = (bf16[368,512]{1,0:T(8,128)(2,1)S(1)}, bf16[368,512]{1,0:T(8,128)(2,1)S(1)}, u32[]{:S(2)}, u32[]{:S(2)}) collective-permute-start(bf16[368,512]{1,0:T(8,128)(2,1)S(1)} %get-tuple-element.28), channel_id=1, source_target_pairs={{0,2},{2,0},{1,3},{3,1},{4,6},{6,4},{5,7},{7,5},{8,10},{10,8},{9,1... | collective-permute-start | bytes 1130504 | tf_op jit(solution)/shard_map/ppermute | solution.py:592
  5.6 1.6 %collective-permute-start.1 = (bf16[336,128]{1,0:T(8,128)(2,1)S(1)}, bf16[336,128]{1,0:T(8,128)(2,1)S(1)}, u32[]{:S(2)}, u32[]{:S(2)}) collective-permute-start(bf16[336,128]{1,0:T(8,128)(2,1)S(1)} %get-tuple-element.30), channel_id=1, source_target_pairs={{0,4},{4,8},{8,12},{12,0},{1,5},{5,9},{9,13},{13,1},{2,6},{6,10},{... | collective-permute-start | bytes 258056 | tf_op jit(solution)/shard_map/ppermute | solution.py:595
  7.2 2.2 %collective-permute-start.3 = (bf16[336,128]{1,0:T(8,128)(2,1)S(1)}, bf16[336,128]{1,0:T(8,128)(2,1)S(1)}, u32[]{:S(2)}, u32[]{:S(2)}) collective-permute-start(bf16[336,128]{1,0:T(8,128)(2,1)S(1)} %get-tuple-element.31), channel_id=1, source_target_pairs={{0,12},{4,0},{8,4},{12,8},{1,13},{5,1},{9,5},{13,9},{2,14},{6,2},{... | collective-permute-start | bytes 258056 | tf_op jit(solution)/shard_map/ppermute | solution.py:595
  9.4 0.8 %collective-permute-start.2 = (bf16[272,128]{1,0:T(8,128)(2,1)S(1)}, bf16[272,128]{1,0:T(8,128)(2,1)S(1)}, u32[]{:S(2)}, u32[]{:S(2)}) collective-permute-start(bf16[272,128]{1,0:T(8,128)(2,1)S(1)} %get-tuple-element.29.w0), channel_id=1, source_target_pairs={{0,8},{4,12},{8,0},{12,4},{1,9},{5,13},{9,1},{13,5},{2,10},{6,14},... | collective-permute-start | bytes 208904 | tf_op jit(solution)/shard_map/ppermute | solution.py:595
  10.2 6.1 %collective-permute-done.2.w2 = bf16[272,128]{1,0:T(8,128)(2,1)S(1)} collective-permute-done((bf16[272,128]{1,0:T(8,128)(2,1)S(1)}, bf16[272,128]{1,0:T(8,128)(2,1)S(1)}, u32[]{:S(2)}, u32[]{:S(2)}) %collective-permute-start.2) | collective-permute-done | bytes 69664 | tf_op jit(solution)/shard_map/ppermute | solution.py:595
  16.4 0.6 %collective-permute-start.4 = (bf16[16,512]{1,0:T(8,128)(2,1)S(1)}, bf16[16,512]{1,0:T(8,128)(2,1)S(1)}, u32[]{:S(2)}, u32[]{:S(2)}) collective-permute-start(bf16[16,512]{1,0:T(8,128)(2,1)S(1)} %get-tuple-element.33), channel_id=1, source_target_pairs={{0,2},{2,0},{1,3},{3,1},{4,6},{6,4},{5,7},{7,5},{8,10},{10,8},{9,1... | collective-permute-start | bytes 49160 | tf_op jit(solution)/shard_map/ppermute | solution.py:592
  17.0 0.9 %collective-permute-done.5.wt_ref = bf16[1088,128]{1,0:T(8,128)(2,1)S(1)} collective-permute-done((bf16[1088,128]{1,0:T(8,128)(2,1)S(1)}, bf16[1088,128]{1,0:T(8,128)(2,1)S(1)}, u32[]{:S(2)}, u32[]{:S(2)}) %collective-permute-start.5) | collective-permute-done | bytes 278560 | tf_op jit(solution)/shard_map/ppermute | solution.py:592
  17.9 1.5 %shard_map.87 = (f32[2,240,512]{2,1,0:T(8,128)S(1)}, bf16[2,128,512]{2,1,0:T(8,128)(2,1)S(1)}, f32[2,16,128]{2,1,0:T(8,128)S(1)}) custom-call(bf16[368,512]{1,0:T(8,128)(2,1)S(1)} %get-tuple-element.27.mine_ref, bf16[368,512]{1,0:T(8,128)(2,1)S(1)} %collective-permute-done.other_ref, bf16[1088,128]{1,0:T(8,128)(2,1)S(1)} %get-tuple-element.34.wm_ref, ...), custom_call_target="tpu_custom_call" | custom-call | tf_op jit(solution)/shard_map/pallas_call | solution.py:172
  19.4 0.8 %collective-permute-done.4.other_halo = bf16[16,512]{1,0:T(8,128)(2,1)S(1)} collective-permute-done((bf16[16,512]{1,0:T(8,128)(2,1)S(1)}, bf16[16,512]{1,0:T(8,128)(2,1)S(1)}, u32[]{:S(2)}, u32[]{:S(2)}) %collective-permute-start.4) | collective-permute-done | bytes 16416 | tf_op jit(solution)/shard_map/ppermute | solution.py:592
  20.2 0.5 %shard_map.88 = (f32[2,16,512]{2,1,0:T(8,128)S(1)}, bf16[2,128,512]{2,1,0:T(8,128)(2,1)S(1)}, f32[2,16,128]{2,1,0:T(8,128)S(1)}) custom-call(bf16[368,512]{1,0:T(8,128)(2,1)S(1)} %get-tuple-element.27.mine_ref, bf16[368,512]{1,0:T(8,128)(2,1)S(1)} %collective-permute-done.other_ref, bf16[16,512]{1,0:T(8,128)(2,1)S(1)} %get-tuple-element.32.own_halo, ...), custom_call_target="tpu_custom_call" | custom-call | tf_op jit(solution)/shard_map/pallas_call | solution.py:172
  20.7 0.6 %collective-permute-start.6 = (f32[2,16,128]{2,1,0:T(8,128)S(1)}, f32[2,16,128]{2,1,0:T(8,128)S(1)}, u32[]{:S(2)}, u32[]{:S(2)}) collective-permute-start(f32[2,16,128]{2,1,0:T(8,128)S(1)} %get-tuple-element.37.after_ref.r_ref), channel_id=1, source_target_pairs={{0,2},{2,0},{1,3},{3,1},{4,6},{6,4},{5,7},{7,5},{8,10},{10,8},{9,1... | collective-permute-start | bytes 49160 | tf_op jit(solution)/shard_map/ppermute | solution.py:592
  21.3 0.8 %shard_map.89.win_ref = bf16[4,512,512]{2,1,0:T(8,128)(2,1)S(1)} custom-call(bf16[368,512]{1,0:T(8,128)(2,1)S(1)} %get-tuple-element.27.mine_ref, bf16[368,512]{1,0:T(8,128)(2,1)S(1)} %collective-permute-done.other_ref, bf16[16,512]{1,0:T(8,128)(2,1)S(1)} %get-tuple-element.32.own_halo, bf16[16,512]{1,0:T(8,128)(2,1)S(1)} %collective-permute-done.4.other_halo, ...), custom_call_target="tpu_custom_call" | custom-call | bytes 2097152 | tf_op jit(solution)/shard_map/pallas_call | solution.py:172
  22.1 2.4 %collective-permute-done.6.rr_ref = f32[2,16,128]{2,1,0:T(8,128)S(1)} collective-permute-done((f32[2,16,128]{2,1,0:T(8,128)S(1)}, f32[2,16,128]{2,1,0:T(8,128)S(1)}, u32[]{:S(2)}, u32[]{:S(2)}) %collective-permute-start.6) | collective-permute-done | bytes 16416 | tf_op jit(solution)/shard_map/ppermute | solution.py:592
  24.5 1.3 %shard_map.90 = (bf16[2,240,512]{2,1,0:T(8,128)(2,1)S(1)}, bf16[2,16,512]{2,1,0:T(8,128)(2,1)S(1)}, f32[1056,128]{1,0:T(8,128)S(1)}, f32[1056,128]{1,0:T(8,128)S(1)}) custom-call(bf16[368,512]{1,0:T(8,128)(2,1)S(1)} %get-tuple-element.27.mine_ref, bf16[368,512]{1,0:T(8,128)(2,1)S(1)} %collective-permute-done.other_ref, ...), custom_call_target="tpu_custom_call" | custom-call | tf_op jit(solution)/shard_map/pallas_call | solution.py:172
  26.0 0.7 %shard_map.92 = bf16[240,512]{1,0:T(8,128)(2,1)S(1)} custom-call(bf16[2,240,512]{2,1,0:T(8,128)(2,1)S(1)} %get-tuple-element.46.hg_ref, bf16[2,16,512]{2,1,0:T(8,128)(2,1)S(1)} %get-tuple-element.47.hx_ref, bf16[368,512]{1,0:T(8,128)(2,1)S(1)} %collective-permute-done.other_ref, bf16[1088,128]{1,0:T(8,128)(2,1)S(1)} %get-tuple-element.34.wm_ref, ...), custom_call_target="tpu_custom_call" | custom-call | tf_op jit(solution)/shard_map/pallas_call | solution.py:172
  26.7 0.6 %collective-permute-start.11 = (bf16[240,512]{1,0:T(8,128)(2,1)S(1)}, bf16[240,512]{1,0:T(8,128)(2,1)S(1)}, u32[]{:S(2)}, u32[]{:S(2)}) collective-permute-start(bf16[240,512]{1,0:T(8,128)(2,1)S(1)} %shard_map.92), channel_id=1, source_target_pairs={{0,2},{2,0},{1,3},{3,1},{4,6},{6,4},{5,7},{7,5},{8,10},{10,8},{9,1... | collective-permute-start | bytes 737288 | tf_op jit(solution)/shard_map/ppermute | solution.py:592
  27.3 0.6 %collective-permute-done.7.got_ref = f32[1056,128]{1,0:T(8,128)S(1)} collective-permute-done((f32[1056,128]{1,0:T(8,128)S(1)}, f32[1056,128]{1,0:T(8,128)S(1)}, u32[]{:S(2)}, u32[]{:S(2)}) %collective-permute-start.7) | collective-permute-done | bytes 540704 | tf_op jit(solution)/shard_map/ppermute | solution.py:592
  27.9 2.2 %collective-permute-start.8 = (bf16[272,128]{1,0:T(8,128)(2,1)S(1)}, bf16[272,128]{1,0:T(8,128)(2,1)S(1)}, u32[]{:S(2)}, u32[]{:S(2)}) collective-permute-start(bf16[272,128]{1,0:T(8,128)(2,1)S(1)} %get-tuple-element.43), channel_id=1, source_target_pairs={{0,12},{4,0},{8,4},{12,8},{1,13},{5,1},{9,5},{13,9},{2,14},{6,2},{... | collective-permute-start | bytes 208904 | tf_op jit(solution)/shard_map/ppermute | solution.py:595
  30.1 0.6 %collective-permute-start.10 = (bf16[272,128]{1,0:T(8,128)(2,1)S(1)}, bf16[272,128]{1,0:T(8,128)(2,1)S(1)}, u32[]{:S(2)}, u32[]{:S(2)}) collective-permute-start(bf16[272,128]{1,0:T(8,128)(2,1)S(1)} %get-tuple-element.45), channel_id=1, source_target_pairs={{0,4},{4,8},{8,12},{12,0},{1,5},{5,9},{9,13},{13,1},{2,6},{6,10},{... | collective-permute-start | bytes 208904 | tf_op jit(solution)/shard_map/ppermute | solution.py:595
  30.8 1.4 %shard_map.93.x_hbm = bf16[1,240,1024]{2,1,0:T(8,128)(2,1)} custom-call(bf16[2,240,512]{2,1,0:T(8,128)(2,1)S(1)} %get-tuple-element.46.hg_ref, bf16[2,16,512]{2,1,0:T(8,128)(2,1)S(1)} %get-tuple-element.47.hx_ref, bf16[368,512]{1,0:T(8,128)(2,1)S(1)} %get-tuple-element.27.mine_ref, bf16[1088,128]{1,0:T(8,128)(2,1)S(1)} %get-tuple-element.34.wm_ref, ...), custom_call_target="tpu_custom_call" | custom-call | bytes 4194304 | tf_op jit(solution)/shard_map/pallas_call | solution.py:658
  32.2 2.9 %collective-permute-done.11.x_got_ref = bf16[240,512]{1,0:T(8,128)(2,1)S(1)} collective-permute-done((bf16[240,512]{1,0:T(8,128)(2,1)S(1)}, bf16[240,512]{1,0:T(8,128)(2,1)S(1)}, u32[]{:S(2)}, u32[]{:S(2)}) %collective-permute-start.11) | collective-permute-done | bytes 245792 | tf_op jit(solution)/shard_map/ppermute | solution.py:592
  35.1 2.2 %collective-permute-done.9.z2 = bf16[272,128]{1,0:T(8,128)(2,1)S(1)} collective-permute-done((bf16[272,128]{1,0:T(8,128)(2,1)S(1)}, bf16[272,128]{1,0:T(8,128)(2,1)S(1)}, u32[]{:S(2)}, u32[]{:S(2)}) %collective-permute-start.9) | collective-permute-done | bytes 69664 | tf_op jit(solution)/shard_map/ppermute | solution.py:595
  37.3 0.8 %shard_map.94 = (bf16[1,240,1024]{2,1,0:T(8,128)(2,1)}, f32[256,128]{1,0:T(8,128)}, f32[1,64]{1,0:T(1,128)}) custom-call(f32[1056,128]{1,0:T(8,128)S(1)} %get-tuple-element.41.kept_ref, f32[1056,128]{1,0:T(8,128)S(1)} %collective-permute-done.7.got_ref, bf16[272,128]{1,0:T(8,128)(2,1)S(1)} %collective-permute-done.8.z1, ...), custom_call_target="tpu_custom_call", output_to_operand_aliasing={{0}: (6, {})} | custom-call | tf_op jit(solution)/shard_map/pallas_call | solution.py:667
  (10 shorter events, 0.2 us)
Async XLA Ops:
  2.6 15.3 %collective-permute-start = (bf16[368,512]{1,0:T(8,128)(2,1)S(1)}, bf16[368,512]{1,0:T(8,128)(2,1)S(1)}, u32[]{:S(2)}, u32[]{:S(2)}) collective-permute-start(bf16[368,512]{1,0:T(8,128)(2,1)S(1)} %get-tuple-element.28), channel_id=1, source_target_pairs={{0,2},{2,0},{1,3},{3,1},{4,6},{6,4},{5,7},{7,5},{8,10},{10,8},{9,1... | collective-permute-start | bytes 1130504 | tf_op jit(solution)/shard_map/ppermute | solution.py:592
  5.6 10.7 %collective-permute-start.1 = (bf16[336,128]{1,0:T(8,128)(2,1)S(1)}, bf16[336,128]{1,0:T(8,128)(2,1)S(1)}, u32[]{:S(2)}, u32[]{:S(2)}) collective-permute-start(bf16[336,128]{1,0:T(8,128)(2,1)S(1)} %get-tuple-element.30), channel_id=1, source_target_pairs={{0,4},{4,8},{8,12},{12,0},{1,5},{5,9},{9,13},{13,1},{2,6},{6,10},{... | collective-permute-start | bytes 258056 | tf_op jit(solution)/shard_map/ppermute | solution.py:595
  7.2 9.1 %collective-permute-start.3 = (bf16[336,128]{1,0:T(8,128)(2,1)S(1)}, bf16[336,128]{1,0:T(8,128)(2,1)S(1)}, u32[]{:S(2)}, u32[]{:S(2)}) collective-permute-start(bf16[336,128]{1,0:T(8,128)(2,1)S(1)} %get-tuple-element.31), channel_id=1, source_target_pairs={{0,12},{4,0},{8,4},{12,8},{1,13},{5,1},{9,5},{13,9},{2,14},{6,2},{... | collective-permute-start | bytes 258056 | tf_op jit(solution)/shard_map/ppermute | solution.py:595
  9.4 6.9 %collective-permute-start.2 = (bf16[272,128]{1,0:T(8,128)(2,1)S(1)}, bf16[272,128]{1,0:T(8,128)(2,1)S(1)}, u32[]{:S(2)}, u32[]{:S(2)}) collective-permute-start(bf16[272,128]{1,0:T(8,128)(2,1)S(1)} %get-tuple-element.29.w0), channel_id=1, source_target_pairs={{0,8},{4,12},{8,0},{12,4},{1,9},{5,13},{9,1},{13,5},{2,10},{6,14},... | collective-permute-start | bytes 208904 | tf_op jit(solution)/shard_map/ppermute | solution.py:595
  16.3 1.6 %collective-permute-start.5 = (bf16[1088,128]{1,0:T(8,128)(2,1)S(1)}, bf16[1088,128]{1,0:T(8,128)(2,1)S(1)}, u32[]{:S(2)}, u32[]{:S(2)}) collective-permute-start(bf16[1088,128]{1,0:T(8,128)(2,1)S(1)} %get-tuple-element.34.wm_ref), channel_id=1, source_target_pairs={{0,1},{1,0},{2,3},{3,2},{4,5},{5,4},{6,7},{7,6},{8,9},{9,8},{10,11... | collective-permute-start | bytes 835592 | tf_op jit(solution)/shard_map/ppermute | solution.py:592
  16.4 3.8 %collective-permute-start.4 = (bf16[16,512]{1,0:T(8,128)(2,1)S(1)}, bf16[16,512]{1,0:T(8,128)(2,1)S(1)}, u32[]{:S(2)}, u32[]{:S(2)}) collective-permute-start(bf16[16,512]{1,0:T(8,128)(2,1)S(1)} %get-tuple-element.33), channel_id=1, source_target_pairs={{0,2},{2,0},{1,3},{3,1},{4,6},{6,4},{5,7},{7,5},{8,10},{10,8},{9,1... | collective-permute-start | bytes 49160 | tf_op jit(solution)/shard_map/ppermute | solution.py:592
  20.7 3.8 %collective-permute-start.6 = (f32[2,16,128]{2,1,0:T(8,128)S(1)}, f32[2,16,128]{2,1,0:T(8,128)S(1)}, u32[]{:S(2)}, u32[]{:S(2)}) collective-permute-start(f32[2,16,128]{2,1,0:T(8,128)S(1)} %get-tuple-element.37.after_ref.r_ref), channel_id=1, source_target_pairs={{0,2},{2,0},{1,3},{3,1},{4,6},{6,4},{5,7},{7,5},{8,10},{10,8},{9,1... | collective-permute-start | bytes 49160 | tf_op jit(solution)/shard_map/ppermute | solution.py:592
  25.9 2.0 %collective-permute-start.7 = (f32[1056,128]{1,0:T(8,128)S(1)}, f32[1056,128]{1,0:T(8,128)S(1)}, u32[]{:S(2)}, u32[]{:S(2)}) collective-permute-start(f32[1056,128]{1,0:T(8,128)S(1)} %get-tuple-element.42), channel_id=1, source_target_pairs={{0,1},{1,0},{2,3},{3,2},{4,5},{5,4},{6,7},{7,6},{8,9},{9,8},{10,11... | collective-permute-start | bytes 1622024 | tf_op jit(solution)/shard_map/ppermute | solution.py:592
  26.7 8.4 %collective-permute-start.11 = (bf16[240,512]{1,0:T(8,128)(2,1)S(1)}, bf16[240,512]{1,0:T(8,128)(2,1)S(1)}, u32[]{:S(2)}, u32[]{:S(2)}) collective-permute-start(bf16[240,512]{1,0:T(8,128)(2,1)S(1)} %shard_map.92), channel_id=1, source_target_pairs={{0,2},{2,0},{1,3},{3,1},{4,6},{6,4},{5,7},{7,5},{8,10},{10,8},{9,1... | collective-permute-start | bytes 737288 | tf_op jit(solution)/shard_map/ppermute | solution.py:592
  27.9 7.2 %collective-permute-start.8 = (bf16[272,128]{1,0:T(8,128)(2,1)S(1)}, bf16[272,128]{1,0:T(8,128)(2,1)S(1)}, u32[]{:S(2)}, u32[]{:S(2)}) collective-permute-start(bf16[272,128]{1,0:T(8,128)(2,1)S(1)} %get-tuple-element.43), channel_id=1, source_target_pairs={{0,12},{4,0},{8,4},{12,8},{1,13},{5,1},{9,5},{13,9},{2,14},{6,2},{... | collective-permute-start | bytes 208904 | tf_op jit(solution)/shard_map/ppermute | solution.py:595
  30.1 7.2 %collective-permute-start.9 = (bf16[272,128]{1,0:T(8,128)(2,1)S(1)}, bf16[272,128]{1,0:T(8,128)(2,1)S(1)}, u32[]{:S(2)}, u32[]{:S(2)}) collective-permute-start(bf16[272,128]{1,0:T(8,128)(2,1)S(1)} %get-tuple-element.44), channel_id=1, source_target_pairs={{0,8},{4,12},{8,0},{12,4},{1,9},{5,13},{9,1},{13,5},{2,10},{6,14},... | collective-permute-start | bytes 208904 | tf_op jit(solution)/shard_map/ppermute | solution.py:595
  30.1 7.2 %collective-permute-start.10 = (bf16[272,128]{1,0:T(8,128)(2,1)S(1)}, bf16[272,128]{1,0:T(8,128)(2,1)S(1)}, u32[]{:S(2)}, u32[]{:S(2)}) collective-permute-start(bf16[272,128]{1,0:T(8,128)(2,1)S(1)} %get-tuple-element.45), channel_id=1, source_target_pairs={{0,4},{4,8},{8,12},{12,0},{1,5},{5,9},{9,13},{13,1},{2,6},{6,10},{... | collective-permute-start | bytes 208904 | tf_op jit(solution)/shard_map/ppermute | solution.py:595

commit v4 on v3

--- a/solution.py
+++ b/solution.py
@@ -145,8 +145,8 @@
 HALF = SLOTS * GROUP_WIDTH
 PAD = 8
 SCORE_ROW = 2 * GROUP_WIDTH
-HALO_ROW = SCORE_ROW + 16
-SHARD = HALO_ROW
+HALO_ROW = SCORE_ROW + PAD
+SHARD = SCORE_ROW + 2 * PAD
 AHEAD = 4
 HEAD = 6
 BF = jnp.bfloat16
@@ -219,9 +219,8 @@
     info = (info.astype(F32) * 0.25).astype(BF)
     value = score_ref[...].astype(F32)
     both = jnp.concatenate([value, value], axis=1)
-    half = lax.broadcasted_iota(jnp.int32, (16, GROUP_WIDTH), 1) // (GROUP_WIDTH // 2)
-    row = lax.broadcasted_iota(jnp.int32, (16, GROUP_WIDTH), 0)
-    block = jnp.where((half == f) & (row == 0), jnp.broadcast_to(both, (16, GROUP_WIDTH)), 0.0)
+    keep = (lane // (GROUP_WIDTH // 2) == f) & (tile_row == 0)
+    block = jnp.where(keep, jnp.broadcast_to(both, (PAD, GROUP_WIDTH)), 0.0)
     for ref in (mw1, mw2, mw3):
         ref[SCORE_ROW:HALO_ROW, :] = block.astype(BF)
     copies[0].wait()
@@ -250,8 +249,11 @@
 
 
 def join_kernel(w0, w1, w2, w3, joined, halo_own, halo_flip):
+    none = jnp.zeros((SHARD - HALO_ROW, GROUP_WIDTH), F32)
     for j, ref in enumerate((w0, w1, w2, w3)):
-        joined[SHARD * j : SHARD * (j + 1), :] = ref[0:SHARD, :]
+        joined[SHARD * j : SHARD * j + SCORE_ROW, :] = ref[0:SCORE_ROW, :]
+        score = jnp.concatenate([ref[SCORE_ROW:HALO_ROW, :].astype(F32), none], axis=0)
+        joined[SHARD * j + SCORE_ROW : SHARD * (j + 1), :] = score.astype(BF)
     for half, out in enumerate((halo_own, halo_flip)):
         for j in range(SLOTS):
             out[0:PAD, lanes(j)] = w1[appended(half, j), :]
@@ -510,12 +512,13 @@
 
 
 def add_kernel(kept_ref, got_ref, *outs):
+    row = lax.broadcasted_iota(jnp.int32, (PAD, GROUP_WIDTH), 0)
     for j, out in zip(range(1, SLOTS), outs):
         base = j * (SCORE_ROW + PAD)
         total = kept_ref[base : base + SCORE_ROW + PAD, :] + got_ref[base : base + SCORE_ROW + PAD, :]
         out[0:SCORE_ROW, :] = total[0:SCORE_ROW].astype(BF)
-        a, b = two_terms(total[SCORE_ROW:])
-        out[SCORE_ROW:, :] = jnp.concatenate([a.astype(F32), b.astype(F32)], axis=0).astype(BF)
+        a, b = (jnp.broadcast_to(v.astype(F32)[0:1], row.shape) for v in two_terms(total[SCORE_ROW:]))
+        out[SCORE_ROW:, :] = jnp.where(row == 0, a, jnp.where(row == 1, b, 0.0)).astype(BF)
 
 
 def input_half(files, stream, hg_ref, hx_ref, message, w_refs, out):
@@ -570,7 +573,7 @@
     for ref in (z1, z2, z3):
         grad = grad + ref[0:SCORE_ROW, :].astype(F32)
         pair = ref[SCORE_ROW:, :].astype(F32)
-        score = score + pair[0:PAD] + pair[PAD:]
+        score = score + jnp.sum(pair, axis=0, keepdims=True)
     grad_ref[...] = grad
     copy_grad = pltpu.make_async_copy(grad_ref, grad_out, sems.at[SLOTS])
     copy_grad.start()

time: 38.2 us -> 37.9 us (level)
  waiting for transfers between devices: 16 us -> 15.6 us
where the time goes in v4:
time: 37.9 us; the launch traced here: 37.8 us
  waiting for transfers between devices  15.6 us (41%)
  starting transfers between devices  12.4 us (33%)
  Pallas kernels  8.39 us (22%)
  between operations  1.36 us (4%)
    ppermute x6, waiting for transfers between devices, cycle(): lax.ppermute(value, 'seq', [(i, (i + by) % SLOTS) for i in range(SLOTS)])  7.95 us
    ppermute x6, waiting for transfers between devices, flip(): return lax.ppermute(value, axis, [(0, 1), (1, 0)])  7.67 us
    ppermute x6, starting transfers between devices, cycle(): lax.ppermute(value, 'seq', [(i, (i + by) % SLOTS) for i in range(SLOTS)])  7.45 us
    pallas_call x8, Pallas kernels, run(): pl.pallas_call(body, out_shape=out_shape, in_specs=specs, out_specs=jax.t...  6.17 us
    ppermute x6, starting transfers between devices, flip(): return lax.ppermute(value, axis, [(0, 1), (1, 0)])  4.95 us
    pallas_call x1, Pallas kernels, per_device_paired(): pl.pallas_call(functools.partial(own_kernel, files), out_shape=shape(inpu...  1.41 us
    pallas_call x1, Pallas kernels, per_device_paired(): pl.pallas_call(finish_kernel, out_shape=(shape(inputs.shape, BF), shape((...  0.81 us
  transfers between devices with their start and end apart: 12, of which 7 were waited for; matrix products, arithmetic and copies ran while one was open for 0% of the time, Pallas kernels for 12%

profile of v4, /device:TPU:0, one launch (start us, length us, event | category | flops | bytes accessed | tf_op | source)
XLA Modules:
  0.0 37.8 jit_solution(2633689535790078196)
XLA Ops:
  1.3 1.3 %shard_map.85 = (bf16[368,512]{1,0:T(8,128)(2,1)S(1)}, bf16[368,512]{1,0:T(8,128)(2,1)S(1)}, bf16[328,128]{1,0:T(8,128)(2,1)S(1)}, bf16[264,128]{1,0:T(8,128)(2,1)S(1)}, bf16[328,128]{1,0:T(8,128)(2,1)S(1)}) custom-call(s32[1,16]{1,0:T(1,128)} %off_hbm.1, bf16[1,240,1024]{2,1,0:T(8,128)(2,1)} %x_hbm.1, bf16[1,120,1024]{2,1,0:T(8,128)(2,1)} %c_hbm.1, ...), custom_call_target="tpu_custom_call" | custom-call | tf_op jit(solution)/shard_map/pallas_call | solution.py:172
  2.6 3.0 %collective-permute-start = (bf16[368,512]{1,0:T(8,128)(2,1)S(1)}, bf16[368,512]{1,0:T(8,128)(2,1)S(1)}, u32[]{:S(2)}, u32[]{:S(2)}) collective-permute-start(bf16[368,512]{1,0:T(8,128)(2,1)S(1)} %get-tuple-element.28), channel_id=1, source_target_pairs={{0,2},{2,0},{1,3},{3,1},{4,6},{6,4},{5,7},{7,5},{8,10},{10,8},{9,1... | collective-permute-start | bytes 1130504 | tf_op jit(solution)/shard_map/ppermute | solution.py:595
  5.6 1.6 %collective-permute-start.1 = (bf16[328,128]{1,0:T(8,128)(2,1)S(1)}, bf16[328,128]{1,0:T(8,128)(2,1)S(1)}, u32[]{:S(2)}, u32[]{:S(2)}) collective-permute-start(bf16[328,128]{1,0:T(8,128)(2,1)S(1)} %get-tuple-element.30), channel_id=1, source_target_pairs={{0,4},{4,8},{8,12},{12,0},{1,5},{5,9},{9,13},{13,1},{2,6},{6,10},{... | collective-permute-start | bytes 251912 | tf_op jit(solution)/shard_map/ppermute | solution.py:598
  7.2 2.2 %collective-permute-start.3 = (bf16[328,128]{1,0:T(8,128)(2,1)S(1)}, bf16[328,128]{1,0:T(8,128)(2,1)S(1)}, u32[]{:S(2)}, u32[]{:S(2)}) collective-permute-start(bf16[328,128]{1,0:T(8,128)(2,1)S(1)} %get-tuple-element.31), channel_id=1, source_target_pairs={{0,12},{4,0},{8,4},{12,8},{1,13},{5,1},{9,5},{13,9},{2,14},{6,2},{... | collective-permute-start | bytes 251912 | tf_op jit(solution)/shard_map/ppermute | solution.py:598
  9.4 0.8 %collective-permute-start.2 = (bf16[264,128]{1,0:T(8,128)(2,1)S(1)}, bf16[264,128]{1,0:T(8,128)(2,1)S(1)}, u32[]{:S(2)}, u32[]{:S(2)}) collective-permute-start(bf16[264,128]{1,0:T(8,128)(2,1)S(1)} %get-tuple-element.29.w0), channel_id=1, source_target_pairs={{0,8},{4,12},{8,0},{12,4},{1,9},{5,13},{9,1},{13,5},{2,10},{6,14},... | collective-permute-start | bytes 202760 | tf_op jit(solution)/shard_map/ppermute | solution.py:598
  10.2 5.9 %collective-permute-done.2.w2 = bf16[264,128]{1,0:T(8,128)(2,1)S(1)} collective-permute-done((bf16[264,128]{1,0:T(8,128)(2,1)S(1)}, bf16[264,128]{1,0:T(8,128)(2,1)S(1)}, u32[]{:S(2)}, u32[]{:S(2)}) %collective-permute-start.2) | collective-permute-done | bytes 67616 | tf_op jit(solution)/shard_map/ppermute | solution.py:598
  16.2 0.6 %collective-permute-start.4 = (bf16[16,512]{1,0:T(8,128)(2,1)S(1)}, bf16[16,512]{1,0:T(8,128)(2,1)S(1)}, u32[]{:S(2)}, u32[]{:S(2)}) collective-permute-start(bf16[16,512]{1,0:T(8,128)(2,1)S(1)} %get-tuple-element.33), channel_id=1, source_target_pairs={{0,2},{2,0},{1,3},{3,1},{4,6},{6,4},{5,7},{7,5},{8,10},{10,8},{9,1... | collective-permute-start | bytes 49160 | tf_op jit(solution)/shard_map/ppermute | solution.py:595
  16.8 0.9 %collective-permute-done.5.wt_ref = bf16[1088,128]{1,0:T(8,128)(2,1)S(1)} collective-permute-done((bf16[1088,128]{1,0:T(8,128)(2,1)S(1)}, bf16[1088,128]{1,0:T(8,128)(2,1)S(1)}, u32[]{:S(2)}, u32[]{:S(2)}) %collective-permute-start.5) | collective-permute-done | bytes 278560 | tf_op jit(solution)/shard_map/ppermute | solution.py:595
  17.8 1.4 %shard_map.87 = (f32[2,240,512]{2,1,0:T(8,128)S(1)}, bf16[2,128,512]{2,1,0:T(8,128)(2,1)S(1)}, f32[2,16,128]{2,1,0:T(8,128)S(1)}) custom-call(bf16[368,512]{1,0:T(8,128)(2,1)S(1)} %get-tuple-element.27.mine_ref, bf16[368,512]{1,0:T(8,128)(2,1)S(1)} %collective-permute-done.other_ref, bf16[1088,128]{1,0:T(8,128)(2,1)S(1)} %get-tuple-element.34.wm_ref, ...), custom_call_target="tpu_custom_call" | custom-call | tf_op jit(solution)/shard_map/pallas_call | solution.py:172
  19.2 0.8 %collective-permute-done.4.other_halo = bf16[16,512]{1,0:T(8,128)(2,1)S(1)} collective-permute-done((bf16[16,512]{1,0:T(8,128)(2,1)S(1)}, bf16[16,512]{1,0:T(8,128)(2,1)S(1)}, u32[]{:S(2)}, u32[]{:S(2)}) %collective-permute-start.4) | collective-permute-done | bytes 16416 | tf_op jit(solution)/shard_map/ppermute | solution.py:595
  20.0 0.5 %shard_map.88 = (f32[2,16,512]{2,1,0:T(8,128)S(1)}, bf16[2,128,512]{2,1,0:T(8,128)(2,1)S(1)}, f32[2,16,128]{2,1,0:T(8,128)S(1)}) custom-call(bf16[368,512]{1,0:T(8,128)(2,1)S(1)} %get-tuple-element.27.mine_ref, bf16[368,512]{1,0:T(8,128)(2,1)S(1)} %collective-permute-done.other_ref, bf16[16,512]{1,0:T(8,128)(2,1)S(1)} %get-tuple-element.32.own_halo, ...), custom_call_target="tpu_custom_call" | custom-call | tf_op jit(solution)/shard_map/pallas_call | solution.py:172
  20.6 0.6 %collective-permute-start.6 = (f32[2,16,128]{2,1,0:T(8,128)S(1)}, f32[2,16,128]{2,1,0:T(8,128)S(1)}, u32[]{:S(2)}, u32[]{:S(2)}) collective-permute-start(f32[2,16,128]{2,1,0:T(8,128)S(1)} %get-tuple-element.37.after_ref.r_ref), channel_id=1, source_target_pairs={{0,2},{2,0},{1,3},{3,1},{4,6},{6,4},{5,7},{7,5},{8,10},{10,8},{9,1... | collective-permute-start | bytes 49160 | tf_op jit(solution)/shard_map/ppermute | solution.py:595
  21.2 0.8 %shard_map.89.win_ref = bf16[4,512,512]{2,1,0:T(8,128)(2,1)S(1)} custom-call(bf16[368,512]{1,0:T(8,128)(2,1)S(1)} %get-tuple-element.27.mine_ref, bf16[368,512]{1,0:T(8,128)(2,1)S(1)} %collective-permute-done.other_ref, bf16[16,512]{1,0:T(8,128)(2,1)S(1)} %get-tuple-element.32.own_halo, bf16[16,512]{1,0:T(8,128)(2,1)S(1)} %collective-permute-done.4.other_halo, ...), custom_call_target="tpu_custom_call" | custom-call | bytes 2097152 | tf_op jit(solution)/shard_map/pallas_call | solution.py:172
  21.9 2.4 %collective-permute-done.6.rr_ref = f32[2,16,128]{2,1,0:T(8,128)S(1)} collective-permute-done((f32[2,16,128]{2,1,0:T(8,128)S(1)}, f32[2,16,128]{2,1,0:T(8,128)S(1)}, u32[]{:S(2)}, u32[]{:S(2)}) %collective-permute-start.6) | collective-permute-done | bytes 16416 | tf_op jit(solution)/shard_map/ppermute | solution.py:595
  24.4 1.3 %shard_map.90 = (bf16[2,240,512]{2,1,0:T(8,128)(2,1)S(1)}, bf16[2,16,512]{2,1,0:T(8,128)(2,1)S(1)}, f32[1056,128]{1,0:T(8,128)S(1)}, f32[1056,128]{1,0:T(8,128)S(1)}) custom-call(bf16[368,512]{1,0:T(8,128)(2,1)S(1)} %get-tuple-element.27.mine_ref, bf16[368,512]{1,0:T(8,128)(2,1)S(1)} %collective-permute-done.other_ref, ...), custom_call_target="tpu_custom_call" | custom-call | tf_op jit(solution)/shard_map/pallas_call | solution.py:172
  25.8 0.7 %shard_map.92 = bf16[240,512]{1,0:T(8,128)(2,1)S(1)} custom-call(bf16[2,240,512]{2,1,0:T(8,128)(2,1)S(1)} %get-tuple-element.46.hg_ref, bf16[2,16,512]{2,1,0:T(8,128)(2,1)S(1)} %get-tuple-element.47.hx_ref, bf16[368,512]{1,0:T(8,128)(2,1)S(1)} %collective-permute-done.other_ref, bf16[1088,128]{1,0:T(8,128)(2,1)S(1)} %get-tuple-element.34.wm_ref, ...), custom_call_target="tpu_custom_call" | custom-call | tf_op jit(solution)/shard_map/pallas_call | solution.py:172
  26.5 0.6 %collective-permute-start.11 = (bf16[240,512]{1,0:T(8,128)(2,1)S(1)}, bf16[240,512]{1,0:T(8,128)(2,1)S(1)}, u32[]{:S(2)}, u32[]{:S(2)}) collective-permute-start(bf16[240,512]{1,0:T(8,128)(2,1)S(1)} %shard_map.92), channel_id=1, source_target_pairs={{0,2},{2,0},{1,3},{3,1},{4,6},{6,4},{5,7},{7,5},{8,10},{10,8},{9,1... | collective-permute-start | bytes 737288 | tf_op jit(solution)/shard_map/ppermute | solution.py:595
  27.1 0.6 %collective-permute-done.7.got_ref = f32[1056,128]{1,0:T(8,128)S(1)} collective-permute-done((f32[1056,128]{1,0:T(8,128)S(1)}, f32[1056,128]{1,0:T(8,128)S(1)}, u32[]{:S(2)}, u32[]{:S(2)}) %collective-permute-start.7) | collective-permute-done | bytes 540704 | tf_op jit(solution)/shard_map/ppermute | solution.py:595
  27.8 2.2 %collective-permute-start.8 = (bf16[264,128]{1,0:T(8,128)(2,1)S(1)}, bf16[264,128]{1,0:T(8,128)(2,1)S(1)}, u32[]{:S(2)}, u32[]{:S(2)}) collective-permute-start(bf16[264,128]{1,0:T(8,128)(2,1)S(1)} %get-tuple-element.43), channel_id=1, source_target_pairs={{0,12},{4,0},{8,4},{12,8},{1,13},{5,1},{9,5},{13,9},{2,14},{6,2},{... | collective-permute-start | bytes 202760 | tf_op jit(solution)/shard_map/ppermute | solution.py:598
  30.0 0.6 %collective-permute-start.10 = (bf16[264,128]{1,0:T(8,128)(2,1)S(1)}, bf16[264,128]{1,0:T(8,128)(2,1)S(1)}, u32[]{:S(2)}, u32[]{:S(2)}) collective-permute-start(bf16[264,128]{1,0:T(8,128)(2,1)S(1)} %get-tuple-element.45), channel_id=1, source_target_pairs={{0,4},{4,8},{8,12},{12,0},{1,5},{5,9},{9,13},{13,1},{2,6},{6,10},{... | collective-permute-start | bytes 202760 | tf_op jit(solution)/shard_map/ppermute | solution.py:598
  30.6 1.4 %shard_map.93.x_hbm = bf16[1,240,1024]{2,1,0:T(8,128)(2,1)} custom-call(bf16[2,240,512]{2,1,0:T(8,128)(2,1)S(1)} %get-tuple-element.46.hg_ref, bf16[2,16,512]{2,1,0:T(8,128)(2,1)S(1)} %get-tuple-element.47.hx_ref, bf16[368,512]{1,0:T(8,128)(2,1)S(1)} %get-tuple-element.27.mine_ref, bf16[1088,128]{1,0:T(8,128)(2,1)S(1)} %get-tuple-element.34.wm_ref, ...), custom_call_target="tpu_custom_call" | custom-call | bytes 4194304 | tf_op jit(solution)/shard_map/pallas_call | solution.py:661
  32.0 2.9 %collective-permute-done.11.x_got_ref = bf16[240,512]{1,0:T(8,128)(2,1)S(1)} collective-permute-done((bf16[240,512]{1,0:T(8,128)(2,1)S(1)}, bf16[240,512]{1,0:T(8,128)(2,1)S(1)}, u32[]{:S(2)}, u32[]{:S(2)}) %collective-permute-start.11) | collective-permute-done | bytes 245792 | tf_op jit(solution)/shard_map/ppermute | solution.py:595
  34.9 2.1 %collective-permute-done.9.z2 = bf16[264,128]{1,0:T(8,128)(2,1)S(1)} collective-permute-done((bf16[264,128]{1,0:T(8,128)(2,1)S(1)}, bf16[264,128]{1,0:T(8,128)(2,1)S(1)}, u32[]{:S(2)}, u32[]{:S(2)}) %collective-permute-start.9) | collective-permute-done | bytes 67616 | tf_op jit(solution)/shard_map/ppermute | solution.py:598
  37.0 0.8 %shard_map.94 = (bf16[1,240,1024]{2,1,0:T(8,128)(2,1)}, f32[256,128]{1,0:T(8,128)}, f32[1,64]{1,0:T(1,128)}) custom-call(f32[1056,128]{1,0:T(8,128)S(1)} %get-tuple-element.41.kept_ref, f32[1056,128]{1,0:T(8,128)S(1)} %collective-permute-done.7.got_ref, bf16[264,128]{1,0:T(8,128)(2,1)S(1)} %collective-permute-done.8.z1, ...), custom_call_target="tpu_custom_call", output_to_operand_aliasing={{0}: (6, {})} | custom-call | tf_op jit(solution)/shard_map/pallas_call | solution.py:670
  (10 shorter events, 0.2 us)
Async XLA Ops:
  2.6 15.2 %collective-permute-start = (bf16[368,512]{1,0:T(8,128)(2,1)S(1)}, bf16[368,512]{1,0:T(8,128)(2,1)S(1)}, u32[]{:S(2)}, u32[]{:S(2)}) collective-permute-start(bf16[368,512]{1,0:T(8,128)(2,1)S(1)} %get-tuple-element.28), channel_id=1, source_target_pairs={{0,2},{2,0},{1,3},{3,1},{4,6},{6,4},{5,7},{7,5},{8,10},{10,8},{9,1... | collective-permute-start | bytes 1130504 | tf_op jit(solution)/shard_map/ppermute | solution.py:595
  5.6 10.5 %collective-permute-start.1 = (bf16[328,128]{1,0:T(8,128)(2,1)S(1)}, bf16[328,128]{1,0:T(8,128)(2,1)S(1)}, u32[]{:S(2)}, u32[]{:S(2)}) collective-permute-start(bf16[328,128]{1,0:T(8,128)(2,1)S(1)} %get-tuple-element.30), channel_id=1, source_target_pairs={{0,4},{4,8},{8,12},{12,0},{1,5},{5,9},{9,13},{13,1},{2,6},{6,10},{... | collective-permute-start | bytes 251912 | tf_op jit(solution)/shard_map/ppermute | solution.py:598
  7.2 8.9 %collective-permute-start.3 = (bf16[328,128]{1,0:T(8,128)(2,1)S(1)}, bf16[328,128]{1,0:T(8,128)(2,1)S(1)}, u32[]{:S(2)}, u32[]{:S(2)}) collective-permute-start(bf16[328,128]{1,0:T(8,128)(2,1)S(1)} %get-tuple-element.31), channel_id=1, source_target_pairs={{0,12},{4,0},{8,4},{12,8},{1,13},{5,1},{9,5},{13,9},{2,14},{6,2},{... | collective-permute-start | bytes 251912 | tf_op jit(solution)/shard_map/ppermute | solution.py:598
  9.4 6.7 %collective-permute-start.2 = (bf16[264,128]{1,0:T(8,128)(2,1)S(1)}, bf16[264,128]{1,0:T(8,128)(2,1)S(1)}, u32[]{:S(2)}, u32[]{:S(2)}) collective-permute-start(bf16[264,128]{1,0:T(8,128)(2,1)S(1)} %get-tuple-element.29.w0), channel_id=1, source_target_pairs={{0,8},{4,12},{8,0},{12,4},{1,9},{5,13},{9,1},{13,5},{2,10},{6,14},... | collective-permute-start | bytes 202760 | tf_op jit(solution)/shard_map/ppermute | solution.py:598
  16.1 1.6 %collective-permute-start.5 = (bf16[1088,128]{1,0:T(8,128)(2,1)S(1)}, bf16[1088,128]{1,0:T(8,128)(2,1)S(1)}, u32[]{:S(2)}, u32[]{:S(2)}) collective-permute-start(bf16[1088,128]{1,0:T(8,128)(2,1)S(1)} %get-tuple-element.34.wm_ref), channel_id=1, source_target_pairs={{0,1},{1,0},{2,3},{3,2},{4,5},{5,4},{6,7},{7,6},{8,9},{9,8},{10,11... | collective-permute-start | bytes 835592 | tf_op jit(solution)/shard_map/ppermute | solution.py:595
  16.2 3.8 %collective-permute-start.4 = (bf16[16,512]{1,0:T(8,128)(2,1)S(1)}, bf16[16,512]{1,0:T(8,128)(2,1)S(1)}, u32[]{:S(2)}, u32[]{:S(2)}) collective-permute-start(bf16[16,512]{1,0:T(8,128)(2,1)S(1)} %get-tuple-element.33), channel_id=1, source_target_pairs={{0,2},{2,0},{1,3},{3,1},{4,6},{6,4},{5,7},{7,5},{8,10},{10,8},{9,1... | collective-permute-start | bytes 49160 | tf_op jit(solution)/shard_map/ppermute | solution.py:595
  20.6 3.8 %collective-permute-start.6 = (f32[2,16,128]{2,1,0:T(8,128)S(1)}, f32[2,16,128]{2,1,0:T(8,128)S(1)}, u32[]{:S(2)}, u32[]{:S(2)}) collective-permute-start(f32[2,16,128]{2,1,0:T(8,128)S(1)} %get-tuple-element.37.after_ref.r_ref), channel_id=1, source_target_pairs={{0,2},{2,0},{1,3},{3,1},{4,6},{6,4},{5,7},{7,5},{8,10},{10,8},{9,1... | collective-permute-start | bytes 49160 | tf_op jit(solution)/shard_map/ppermute | solution.py:595
  25.7 2.0 %collective-permute-start.7 = (f32[1056,128]{1,0:T(8,128)S(1)}, f32[1056,128]{1,0:T(8,128)S(1)}, u32[]{:S(2)}, u32[]{:S(2)}) collective-permute-start(f32[1056,128]{1,0:T(8,128)S(1)} %get-tuple-element.42), channel_id=1, source_target_pairs={{0,1},{1,0},{2,3},{3,2},{4,5},{5,4},{6,7},{7,6},{8,9},{9,8},{10,11... | collective-permute-start | bytes 1622024 | tf_op jit(solution)/shard_map/ppermute | solution.py:595
  26.5 8.4 %collective-permute-start.11 = (bf16[240,512]{1,0:T(8,128)(2,1)S(1)}, bf16[240,512]{1,0:T(8,128)(2,1)S(1)}, u32[]{:S(2)}, u32[]{:S(2)}) collective-permute-start(bf16[240,512]{1,0:T(8,128)(2,1)S(1)} %shard_map.92), channel_id=1, source_target_pairs={{0,2},{2,0},{1,3},{3,1},{4,6},{6,4},{5,7},{7,5},{8,10},{10,8},{9,1... | collective-permute-start | bytes 737288 | tf_op jit(solution)/shard_map/ppermute | solution.py:595
  27.8 7.2 %collective-permute-start.8 = (bf16[264,128]{1,0:T(8,128)(2,1)S(1)}, bf16[264,128]{1,0:T(8,128)(2,1)S(1)}, u32[]{:S(2)}, u32[]{:S(2)}) collective-permute-start(bf16[264,128]{1,0:T(8,128)(2,1)S(1)} %get-tuple-element.43), channel_id=1, source_target_pairs={{0,12},{4,0},{8,4},{12,8},{1,13},{5,1},{9,5},{13,9},{2,14},{6,2},{... | collective-permute-start | bytes 202760 | tf_op jit(solution)/shard_map/ppermute | solution.py:598
  30.0 7.0 %collective-permute-start.9 = (bf16[264,128]{1,0:T(8,128)(2,1)S(1)}, bf16[264,128]{1,0:T(8,128)(2,1)S(1)}, u32[]{:S(2)}, u32[]{:S(2)}) collective-permute-start(bf16[264,128]{1,0:T(8,128)(2,1)S(1)} %get-tuple-element.44), channel_id=1, source_target_pairs={{0,8},{4,12},{8,0},{12,4},{1,9},{5,13},{9,1},{13,5},{2,10},{6,14},... | collective-permute-start | bytes 202760 | tf_op jit(solution)/shard_map/ppermute | solution.py:598
  30.0 7.0 %collective-permute-start.10 = (bf16[264,128]{1,0:T(8,128)(2,1)S(1)}, bf16[264,128]{1,0:T(8,128)(2,1)S(1)}, u32[]{:S(2)}, u32[]{:S(2)}) collective-permute-start(bf16[264,128]{1,0:T(8,128)(2,1)S(1)} %get-tuple-element.45), channel_id=1, source_target_pairs={{0,4},{4,8},{8,12},{12,0},{1,5},{5,9},{9,13},{13,1},{2,6},{6,10},{... | collective-permute-start | bytes 202760 | tf_op jit(solution)/shard_map/ppermute | solution.py:598

commit v5 on v4

--- a/solution.py
+++ b/solution.py
@@ -149,6 +149,8 @@
 SHARD = SCORE_ROW + 2 * PAD
 AHEAD = 4
 HEAD = 6
+SPARE = 16
+JOINED_SPARE = 48
 BF = jnp.bfloat16
 F32 = jnp.float32
 
@@ -223,6 +225,8 @@
     block = jnp.where(keep, jnp.broadcast_to(both, (PAD, GROUP_WIDTH)), 0.0)
     for ref in (mw1, mw2, mw3):
         ref[SCORE_ROW:HALO_ROW, :] = block.astype(BF)
+    if SPARE:
+        mw1[HALO_ROW + 2 * PAD * SLOTS :, :] = jnp.zeros((SPARE, GROUP_WIDTH), BF)
     copies[0].wait()
     for ref, parity in ((other, 1 - d), (mine, d)):
         for j in range(SLOTS):
@@ -249,6 +253,8 @@
 
 
 def join_kernel(w0, w1, w2, w3, joined, halo_own, halo_flip):
+    if JOINED_SPARE:
+        joined[SLOTS * SHARD :, :] = jnp.zeros((JOINED_SPARE, GROUP_WIDTH), BF)
     none = jnp.zeros((SHARD - HALO_ROW, GROUP_WIDTH), F32)
     for j, ref in enumerate((w0, w1, w2, w3)):
         joined[SHARD * j : SHARD * j + SCORE_ROW, :] = ref[0:SCORE_ROW, :]
@@ -518,7 +524,9 @@
         total = kept_ref[base : base + SCORE_ROW + PAD, :] + got_ref[base : base + SCORE_ROW + PAD, :]
         out[0:SCORE_ROW, :] = total[0:SCORE_ROW].astype(BF)
         a, b = (jnp.broadcast_to(v.astype(F32)[0:1], row.shape) for v in two_terms(total[SCORE_ROW:]))
-        out[SCORE_ROW:, :] = jnp.where(row == 0, a, jnp.where(row == 1, b, 0.0)).astype(BF)
+        if out.shape[0] > HALO_ROW:
+            out[HALO_ROW:, :] = jnp.zeros((out.shape[0] - HALO_ROW, GROUP_WIDTH), BF)
+        out[SCORE_ROW:HALO_ROW, :] = jnp.where(row == 0, a, jnp.where(row == 1, b, 0.0)).astype(BF)
 
 
 def input_half(files, stream, hg_ref, hx_ref, message, w_refs, out):
@@ -572,7 +580,7 @@
     grad, score = total[0:SCORE_ROW], total[SCORE_ROW:]
     for ref in (z1, z2, z3):
         grad = grad + ref[0:SCORE_ROW, :].astype(F32)
-        pair = ref[SCORE_ROW:, :].astype(F32)
+        pair = ref[SCORE_ROW:HALO_ROW, :].astype(F32)
         score = score + jnp.sum(pair, axis=0, keepdims=True)
     grad_ref[...] = grad
     copy_grad = pltpu.make_async_copy(grad_ref, grad_out, sems.at[SLOTS])
@@ -603,7 +611,7 @@
         (
             message,
             message,
-            shape((HALO_ROW + 2 * PAD * SLOTS, GROUP_WIDTH), BF),
+            shape((HALO_ROW + 2 * PAD * SLOTS + SPARE, GROUP_WIDTH), BF),
             shape((HALO_ROW, GROUP_WIDTH), BF),
             shape((HALO_ROW + 2 * PAD * SLOTS, GROUP_WIDTH), BF),
         ),
@@ -619,7 +627,7 @@
     other = flip(other, "dp")
     halo = shape((2 * PAD, HALF), BF)
     kernel_mine, halo_own, halo_other = call(
-        join_kernel, (shape((SLOTS * SHARD, GROUP_WIDTH), BF), halo, halo)
+        join_kernel, (shape((SLOTS * SHARD + JOINED_SPARE, GROUP_WIDTH), BF), halo, halo)
     )(mw2, cycle(mw1, 1), cycle(mw2, 2), cycle(mw3, 3))
     halo_other = flip(halo_other, "dp")
     shards = (kernel_mine, flip(kernel_mine, "fsdp"))
@@ -654,7 +662,8 @@
     )
     x_got = flip(x_send, "dp")
     summed = shape((HALO_ROW, GROUP_WIDTH), BF)
-    sums = call(add_kernel, (summed, summed, summed))(kept, got)
+    first = shape((HALO_ROW + PAD, GROUP_WIDTH), BF)
+    sums = call(add_kernel, tuple(first if j == 2 else summed for j in range(1, SLOTS)))(kept, got)
     final = [cycle(value, -j) for j, value in zip(range(1, SLOTS), sums)]
     vmem, hbm = pl.BlockSpec(memory_space=pltpu.VMEM), pl.BlockSpec(memory_space=pltpu.HBM)
     params = pltpu.CompilerParams(vmem_limit_bytes=48 * 1024 * 1024)

time: 37.9 us -> 36.8 us (0.971)
  waiting for transfers between devices: 15.6 us -> 13 us
  starting transfers between devices: 12.4 us -> 13.9 us
    ppermute x6, starting transfers between devices: 7.45 us -> 9.26 us  [cycle(): lax.ppermute(value, 'seq', [(i, (i + by) % SLOTS) for i in range(SLOTS)])]
    ppermute x6, waiting for transfers between devices: 7.67 us -> 6.17 us  [flip(): return lax.ppermute(value, axis, [(0, 1), (1, 0)])]
    ppermute x6, waiting for transfers between devices: 7.95 us -> 6.83 us  [cycle(): lax.ppermute(value, 'seq', [(i, (i + by) % SLOTS) for i in range(SLOTS)])]
where the time goes in v5:
time: 36.8 us; the launch traced here: 36.7 us
  starting transfers between devices  13.9 us (38%)
  waiting for transfers between devices  13 us (35%)
  Pallas kernels  8.47 us (23%)
  between operations  1.36 us (4%)
    ppermute x6, starting transfers between devices, cycle(): lax.ppermute(value, 'seq', [(i, (i + by) % SLOTS) for i in range(SLOTS)])  9.26 us
    ppermute x6, waiting for transfers between devices, cycle(): lax.ppermute(value, 'seq', [(i, (i + by) % SLOTS) for i in range(SLOTS)])  6.83 us
    pallas_call x8, Pallas kernels, run(): pl.pallas_call(body, out_shape=out_shape, in_specs=specs, out_specs=jax.t...  6.23 us
    ppermute x6, waiting for transfers between devices, flip(): return lax.ppermute(value, axis, [(0, 1), (1, 0)])  6.17 us
    ppermute x6, starting transfers between devices, flip(): return lax.ppermute(value, axis, [(0, 1), (1, 0)])  4.6 us
    pallas_call x1, Pallas kernels, per_device_paired(): pl.pallas_call(functools.partial(own_kernel, files), out_shape=shape(inpu...  1.43 us
    pallas_call x1, Pallas kernels, per_device_paired(): pl.pallas_call(finish_kernel, out_shape=(shape(inputs.shape, BF), shape((...  0.81 us
  transfers between devices with their start and end apart: 12, of which 7 were waited for; matrix products, arithmetic and copies ran while one was open for 0% of the time, Pallas kernels for 12%

profile of v5, /device:TPU:0, one launch (start us, length us, event | category | flops | bytes accessed | tf_op | source)
XLA Modules:
  0.0 36.7 jit_solution(16769125809551552640)
XLA Ops:
  1.3 1.3 %shard_map.85 = (bf16[368,512]{1,0:T(8,128)(2,1)S(1)}, bf16[368,512]{1,0:T(8,128)(2,1)S(1)}, bf16[344,128]{1,0:T(8,128)(2,1)S(1)}, bf16[264,128]{1,0:T(8,128)(2,1)S(1)}, bf16[328,128]{1,0:T(8,128)(2,1)S(1)}) custom-call(s32[1,16]{1,0:T(1,128)} %off_hbm.1, bf16[1,240,1024]{2,1,0:T(8,128)(2,1)} %x_hbm.1, bf16[1,120,1024]{2,1,0:T(8,128)(2,1)} %c_hbm.1, ...), custom_call_target="tpu_custom_call" | custom-call | tf_op jit(solution)/shard_map/pallas_call | solution.py:174
  2.6 3.1 %collective-permute-start.1 = (bf16[344,128]{1,0:T(8,128)(2,1)S(1)}, bf16[344,128]{1,0:T(8,128)(2,1)S(1)}, u32[]{:S(2)}, u32[]{:S(2)}) collective-permute-start(bf16[344,128]{1,0:T(8,128)(2,1)S(1)} %get-tuple-element.30), channel_id=1, source_target_pairs={{0,4},{4,8},{8,12},{12,0},{1,5},{5,9},{9,13},{13,1},{2,6},{6,10},{... | collective-permute-start | bytes 264200 | tf_op jit(solution)/shard_map/ppermute | solution.py:606
  5.7 1.5 %collective-permute-start = (bf16[368,512]{1,0:T(8,128)(2,1)S(1)}, bf16[368,512]{1,0:T(8,128)(2,1)S(1)}, u32[]{:S(2)}, u32[]{:S(2)}) collective-permute-start(bf16[368,512]{1,0:T(8,128)(2,1)S(1)} %get-tuple-element.28), channel_id=1, source_target_pairs={{0,2},{2,0},{1,3},{3,1},{4,6},{6,4},{5,7},{7,5},{8,10},{10,8},{9,1... | collective-permute-start | bytes 1130504 | tf_op jit(solution)/shard_map/ppermute | solution.py:603
  7.2 2.2 %collective-permute-start.3 = (bf16[328,128]{1,0:T(8,128)(2,1)S(1)}, bf16[328,128]{1,0:T(8,128)(2,1)S(1)}, u32[]{:S(2)}, u32[]{:S(2)}) collective-permute-start(bf16[328,128]{1,0:T(8,128)(2,1)S(1)} %get-tuple-element.31), channel_id=1, source_target_pairs={{0,12},{4,0},{8,4},{12,8},{1,13},{5,1},{9,5},{13,9},{2,14},{6,2},{... | collective-permute-start | bytes 251912 | tf_op jit(solution)/shard_map/ppermute | solution.py:606
  9.4 0.8 %collective-permute-start.2 = (bf16[264,128]{1,0:T(8,128)(2,1)S(1)}, bf16[264,128]{1,0:T(8,128)(2,1)S(1)}, u32[]{:S(2)}, u32[]{:S(2)}) collective-permute-start(bf16[264,128]{1,0:T(8,128)(2,1)S(1)} %get-tuple-element.29.w0), channel_id=1, source_target_pairs={{0,8},{4,12},{8,0},{12,4},{1,9},{5,13},{9,1},{13,5},{2,10},{6,14},... | collective-permute-start | bytes 202760 | tf_op jit(solution)/shard_map/ppermute | solution.py:606
  10.2 5.3 %collective-permute-done.2.w2 = bf16[264,128]{1,0:T(8,128)(2,1)S(1)} collective-permute-done((bf16[264,128]{1,0:T(8,128)(2,1)S(1)}, bf16[264,128]{1,0:T(8,128)(2,1)S(1)}, u32[]{:S(2)}, u32[]{:S(2)}) %collective-permute-start.2) | collective-permute-done | bytes 67616 | tf_op jit(solution)/shard_map/ppermute | solution.py:606
  15.6 1.0 %collective-permute-start.4 = (bf16[16,512]{1,0:T(8,128)(2,1)S(1)}, bf16[16,512]{1,0:T(8,128)(2,1)S(1)}, u32[]{:S(2)}, u32[]{:S(2)}) collective-permute-start(bf16[16,512]{1,0:T(8,128)(2,1)S(1)} %get-tuple-element.33), channel_id=1, source_target_pairs={{0,2},{2,0},{1,3},{3,1},{4,6},{6,4},{5,7},{7,5},{8,10},{10,8},{9,1... | collective-permute-start | bytes 49160 | tf_op jit(solution)/shard_map/ppermute | solution.py:603
  16.6 0.6 %collective-permute-done.5.wt_ref = bf16[1136,128]{1,0:T(8,128)(2,1)S(1)} collective-permute-done((bf16[1136,128]{1,0:T(8,128)(2,1)S(1)}, bf16[1136,128]{1,0:T(8,128)(2,1)S(1)}, u32[]{:S(2)}, u32[]{:S(2)}) %collective-permute-start.5) | collective-permute-done | bytes 290848 | tf_op jit(solution)/shard_map/ppermute | solution.py:603
  17.2 1.5 %shard_map.87 = (f32[2,240,512]{2,1,0:T(8,128)S(1)}, bf16[2,128,512]{2,1,0:T(8,128)(2,1)S(1)}, f32[2,16,128]{2,1,0:T(8,128)S(1)}) custom-call(bf16[368,512]{1,0:T(8,128)(2,1)S(1)} %get-tuple-element.27.mine_ref, bf16[368,512]{1,0:T(8,128)(2,1)S(1)} %collective-permute-done.other_ref, bf16[1136,128]{1,0:T(8,128)(2,1)S(1)} %get-tuple-element.34.wm_ref, ...), custom_call_target="tpu_custom_call" | custom-call | tf_op jit(solution)/shard_map/pallas_call | solution.py:174
  18.7 0.8 %collective-permute-done.4.other_halo = bf16[16,512]{1,0:T(8,128)(2,1)S(1)} collective-permute-done((bf16[16,512]{1,0:T(8,128)(2,1)S(1)}, bf16[16,512]{1,0:T(8,128)(2,1)S(1)}, u32[]{:S(2)}, u32[]{:S(2)}) %collective-permute-start.4) | collective-permute-done | bytes 16416 | tf_op jit(solution)/shard_map/ppermute | solution.py:603
  19.4 0.6 %shard_map.88 = (f32[2,16,512]{2,1,0:T(8,128)S(1)}, bf16[2,128,512]{2,1,0:T(8,128)(2,1)S(1)}, f32[2,16,128]{2,1,0:T(8,128)S(1)}) custom-call(bf16[368,512]{1,0:T(8,128)(2,1)S(1)} %get-tuple-element.27.mine_ref, bf16[368,512]{1,0:T(8,128)(2,1)S(1)} %collective-permute-done.other_ref, bf16[16,512]{1,0:T(8,128)(2,1)S(1)} %get-tuple-element.32.own_halo, ...), custom_call_target="tpu_custom_call" | custom-call | tf_op jit(solution)/shard_map/pallas_call | solution.py:174
  20.0 1.0 %collective-permute-start.6 = (f32[2,16,128]{2,1,0:T(8,128)S(1)}, f32[2,16,128]{2,1,0:T(8,128)S(1)}, u32[]{:S(2)}, u32[]{:S(2)}) collective-permute-start(f32[2,16,128]{2,1,0:T(8,128)S(1)} %get-tuple-element.37.after_ref.r_ref), channel_id=1, source_target_pairs={{0,2},{2,0},{1,3},{3,1},{4,6},{6,4},{5,7},{7,5},{8,10},{10,8},{9,1... | collective-permute-start | bytes 49160 | tf_op jit(solution)/shard_map/ppermute | solution.py:603
  21.0 0.8 %shard_map.89.win_ref = bf16[4,512,512]{2,1,0:T(8,128)(2,1)S(1)} custom-call(bf16[368,512]{1,0:T(8,128)(2,1)S(1)} %get-tuple-element.27.mine_ref, bf16[368,512]{1,0:T(8,128)(2,1)S(1)} %collective-permute-done.other_ref, bf16[16,512]{1,0:T(8,128)(2,1)S(1)} %get-tuple-element.32.own_halo, bf16[16,512]{1,0:T(8,128)(2,1)S(1)} %collective-permute-done.4.other_halo, ...), custom_call_target="tpu_custom_call" | custom-call | bytes 2097152 | tf_op jit(solution)/shard_map/pallas_call | solution.py:174
  21.8 2.0 %collective-permute-done.6.rr_ref = f32[2,16,128]{2,1,0:T(8,128)S(1)} collective-permute-done((f32[2,16,128]{2,1,0:T(8,128)S(1)}, f32[2,16,128]{2,1,0:T(8,128)S(1)}, u32[]{:S(2)}, u32[]{:S(2)}) %collective-permute-start.6) | collective-permute-done | bytes 16416 | tf_op jit(solution)/shard_map/ppermute | solution.py:603
  23.8 1.4 %shard_map.90 = (bf16[2,240,512]{2,1,0:T(8,128)(2,1)S(1)}, bf16[2,16,512]{2,1,0:T(8,128)(2,1)S(1)}, f32[1056,128]{1,0:T(8,128)S(1)}, f32[1056,128]{1,0:T(8,128)S(1)}) custom-call(bf16[368,512]{1,0:T(8,128)(2,1)S(1)} %get-tuple-element.27.mine_ref, bf16[368,512]{1,0:T(8,128)(2,1)S(1)} %collective-permute-done.other_ref, ...), custom_call_target="tpu_custom_call" | custom-call | tf_op jit(solution)/shard_map/pallas_call | solution.py:174
  25.3 0.7 %shard_map.92 = bf16[240,512]{1,0:T(8,128)(2,1)S(1)} custom-call(bf16[2,240,512]{2,1,0:T(8,128)(2,1)S(1)} %get-tuple-element.46.hg_ref, bf16[2,16,512]{2,1,0:T(8,128)(2,1)S(1)} %get-tuple-element.47.hx_ref, bf16[368,512]{1,0:T(8,128)(2,1)S(1)} %collective-permute-done.other_ref, bf16[1136,128]{1,0:T(8,128)(2,1)S(1)} %get-tuple-element.34.wm_ref, ...), custom_call_target="tpu_custom_call" | custom-call | tf_op jit(solution)/shard_map/pallas_call | solution.py:174
  26.0 1.0 %collective-permute-start.11 = (bf16[240,512]{1,0:T(8,128)(2,1)S(1)}, bf16[240,512]{1,0:T(8,128)(2,1)S(1)}, u32[]{:S(2)}, u32[]{:S(2)}) collective-permute-start(bf16[240,512]{1,0:T(8,128)(2,1)S(1)} %shard_map.92), channel_id=1, source_target_pairs={{0,2},{2,0},{1,3},{3,1},{4,6},{6,4},{5,7},{7,5},{8,10},{10,8},{9,1... | collective-permute-start | bytes 737288 | tf_op jit(solution)/shard_map/ppermute | solution.py:603
  27.2 1.1 %collective-permute-start.9 = (bf16[272,128]{1,0:T(8,128)(2,1)S(1)}, bf16[272,128]{1,0:T(8,128)(2,1)S(1)}, u32[]{:S(2)}, u32[]{:S(2)}) collective-permute-start(bf16[272,128]{1,0:T(8,128)(2,1)S(1)} %get-tuple-element.44), channel_id=1, source_target_pairs={{0,8},{4,12},{8,0},{12,4},{1,9},{5,13},{9,1},{13,5},{2,10},{6,14},... | collective-permute-start | bytes 208904 | tf_op jit(solution)/shard_map/ppermute | solution.py:606
  28.4 1.4 %collective-permute-start.8 = (bf16[264,128]{1,0:T(8,128)(2,1)S(1)}, bf16[264,128]{1,0:T(8,128)(2,1)S(1)}, u32[]{:S(2)}, u32[]{:S(2)}) collective-permute-start(bf16[264,128]{1,0:T(8,128)(2,1)S(1)} %get-tuple-element.43), channel_id=1, source_target_pairs={{0,12},{4,0},{8,4},{12,8},{1,13},{5,1},{9,5},{13,9},{2,14},{6,2},{... | collective-permute-start | bytes 202760 | tf_op jit(solution)/shard_map/ppermute | solution.py:606
  29.7 0.6 %collective-permute-start.10 = (bf16[264,128]{1,0:T(8,128)(2,1)S(1)}, bf16[264,128]{1,0:T(8,128)(2,1)S(1)}, u32[]{:S(2)}, u32[]{:S(2)}) collective-permute-start(bf16[264,128]{1,0:T(8,128)(2,1)S(1)} %get-tuple-element.45), channel_id=1, source_target_pairs={{0,4},{4,8},{8,12},{12,0},{1,5},{5,9},{9,13},{13,1},{2,6},{6,10},{... | collective-permute-start | bytes 202760 | tf_op jit(solution)/shard_map/ppermute | solution.py:606
  30.4 1.4 %shard_map.93.x_hbm = bf16[1,240,1024]{2,1,0:T(8,128)(2,1)} custom-call(bf16[2,240,512]{2,1,0:T(8,128)(2,1)S(1)} %get-tuple-element.46.hg_ref, bf16[2,16,512]{2,1,0:T(8,128)(2,1)S(1)} %get-tuple-element.47.hx_ref, bf16[368,512]{1,0:T(8,128)(2,1)S(1)} %get-tuple-element.27.mine_ref, bf16[1136,128]{1,0:T(8,128)(2,1)S(1)} %get-tuple-element.34.wm_ref, ...), custom_call_target="tpu_custom_call" | custom-call | bytes 4194304 | tf_op jit(solution)/shard_map/pallas_call | solution.py:670
  31.8 2.6 %collective-permute-done.11.x_got_ref = bf16[240,512]{1,0:T(8,128)(2,1)S(1)} collective-permute-done((bf16[240,512]{1,0:T(8,128)(2,1)S(1)}, bf16[240,512]{1,0:T(8,128)(2,1)S(1)}, u32[]{:S(2)}, u32[]{:S(2)}) %collective-permute-start.11) | collective-permute-done | bytes 245792 | tf_op jit(solution)/shard_map/ppermute | solution.py:603
  34.4 1.5 %collective-permute-done.10.z3 = bf16[264,128]{1,0:T(8,128)(2,1)S(1)} collective-permute-done((bf16[264,128]{1,0:T(8,128)(2,1)S(1)}, bf16[264,128]{1,0:T(8,128)(2,1)S(1)}, u32[]{:S(2)}, u32[]{:S(2)}) %collective-permute-start.10) | collective-permute-done | bytes 67616 | tf_op jit(solution)/shard_map/ppermute | solution.py:606
  35.9 0.8 %shard_map.94 = (bf16[1,240,1024]{2,1,0:T(8,128)(2,1)}, f32[256,128]{1,0:T(8,128)}, f32[1,64]{1,0:T(1,128)}) custom-call(f32[1056,128]{1,0:T(8,128)S(1)} %get-tuple-element.41.kept_ref, f32[1056,128]{1,0:T(8,128)S(1)} %collective-permute-done.7.got_ref, bf16[264,128]{1,0:T(8,128)(2,1)S(1)} %collective-permute-done.8.z1, ...), custom_call_target="tpu_custom_call", output_to_operand_aliasing={{0}: (6, {})} | custom-call | tf_op jit(solution)/shard_map/pallas_call | solution.py:679
  (10 shorter events, 0.4 us)
Async XLA Ops:
  2.6 12.9 %collective-permute-start.1 = (bf16[344,128]{1,0:T(8,128)(2,1)S(1)}, bf16[344,128]{1,0:T(8,128)(2,1)S(1)}, u32[]{:S(2)}, u32[]{:S(2)}) collective-permute-start(bf16[344,128]{1,0:T(8,128)(2,1)S(1)} %get-tuple-element.30), channel_id=1, source_target_pairs={{0,4},{4,8},{8,12},{12,0},{1,5},{5,9},{9,13},{13,1},{2,6},{6,10},{... | collective-permute-start | bytes 264200 | tf_op jit(solution)/shard_map/ppermute | solution.py:606
  5.7 11.0 %collective-permute-start = (bf16[368,512]{1,0:T(8,128)(2,1)S(1)}, bf16[368,512]{1,0:T(8,128)(2,1)S(1)}, u32[]{:S(2)}, u32[]{:S(2)}) collective-permute-start(bf16[368,512]{1,0:T(8,128)(2,1)S(1)} %get-tuple-element.28), channel_id=1, source_target_pairs={{0,2},{2,0},{1,3},{3,1},{4,6},{6,4},{5,7},{7,5},{8,10},{10,8},{9,1... | collective-permute-start | bytes 1130504 | tf_op jit(solution)/shard_map/ppermute | solution.py:603
  7.2 8.4 %collective-permute-start.3 = (bf16[328,128]{1,0:T(8,128)(2,1)S(1)}, bf16[328,128]{1,0:T(8,128)(2,1)S(1)}, u32[]{:S(2)}, u32[]{:S(2)}) collective-permute-start(bf16[328,128]{1,0:T(8,128)(2,1)S(1)} %get-tuple-element.31), channel_id=1, source_target_pairs={{0,12},{4,0},{8,4},{12,8},{1,13},{5,1},{9,5},{13,9},{2,14},{6,2},{... | collective-permute-start | bytes 251912 | tf_op jit(solution)/shard_map/ppermute | solution.py:606
  9.4 6.1 %collective-permute-start.2 = (bf16[264,128]{1,0:T(8,128)(2,1)S(1)}, bf16[264,128]{1,0:T(8,128)(2,1)S(1)}, u32[]{:S(2)}, u32[]{:S(2)}) collective-permute-start(bf16[264,128]{1,0:T(8,128)(2,1)S(1)} %get-tuple-element.29.w0), channel_id=1, source_target_pairs={{0,8},{4,12},{8,0},{12,4},{1,9},{5,13},{9,1},{13,5},{2,10},{6,14},... | collective-permute-start | bytes 202760 | tf_op jit(solution)/shard_map/ppermute | solution.py:606
  15.6 1.6 %collective-permute-start.5 = (bf16[1136,128]{1,0:T(8,128)(2,1)S(1)}, bf16[1136,128]{1,0:T(8,128)(2,1)S(1)}, u32[]{:S(2)}, u32[]{:S(2)}) collective-permute-start(bf16[1136,128]{1,0:T(8,128)(2,1)S(1)} %get-tuple-element.34.wm_ref), channel_id=1, source_target_pairs={{0,1},{1,0},{2,3},{3,2},{4,5},{5,4},{6,7},{7,6},{8,9},{9,8},{10,11... | collective-permute-start | bytes 872456 | tf_op jit(solution)/shard_map/ppermute | solution.py:603
  15.6 3.8 %collective-permute-start.4 = (bf16[16,512]{1,0:T(8,128)(2,1)S(1)}, bf16[16,512]{1,0:T(8,128)(2,1)S(1)}, u32[]{:S(2)}, u32[]{:S(2)}) collective-permute-start(bf16[16,512]{1,0:T(8,128)(2,1)S(1)} %get-tuple-element.33), channel_id=1, source_target_pairs={{0,2},{2,0},{1,3},{3,1},{4,6},{6,4},{5,7},{7,5},{8,10},{10,8},{9,1... | collective-permute-start | bytes 49160 | tf_op jit(solution)/shard_map/ppermute | solution.py:603
  20.0 3.8 %collective-permute-start.6 = (f32[2,16,128]{2,1,0:T(8,128)S(1)}, f32[2,16,128]{2,1,0:T(8,128)S(1)}, u32[]{:S(2)}, u32[]{:S(2)}) collective-permute-start(f32[2,16,128]{2,1,0:T(8,128)S(1)} %get-tuple-element.37.after_ref.r_ref), channel_id=1, source_target_pairs={{0,2},{2,0},{1,3},{3,1},{4,6},{6,4},{5,7},{7,5},{8,10},{10,8},{9,1... | collective-permute-start | bytes 49160 | tf_op jit(solution)/shard_map/ppermute | solution.py:603
  25.2 2.0 %collective-permute-start.7 = (f32[1056,128]{1,0:T(8,128)S(1)}, f32[1056,128]{1,0:T(8,128)S(1)}, u32[]{:S(2)}, u32[]{:S(2)}) collective-permute-start(f32[1056,128]{1,0:T(8,128)S(1)} %get-tuple-element.42), channel_id=1, source_target_pairs={{0,1},{1,0},{2,3},{3,2},{4,5},{5,4},{6,7},{7,6},{8,9},{9,8},{10,11... | collective-permute-start | bytes 1622024 | tf_op jit(solution)/shard_map/ppermute | solution.py:603
  26.0 8.4 %collective-permute-start.11 = (bf16[240,512]{1,0:T(8,128)(2,1)S(1)}, bf16[240,512]{1,0:T(8,128)(2,1)S(1)}, u32[]{:S(2)}, u32[]{:S(2)}) collective-permute-start(bf16[240,512]{1,0:T(8,128)(2,1)S(1)} %shard_map.92), channel_id=1, source_target_pairs={{0,2},{2,0},{1,3},{3,1},{4,6},{6,4},{5,7},{7,5},{8,10},{10,8},{9,1... | collective-permute-start | bytes 737288 | tf_op jit(solution)/shard_map/ppermute | solution.py:603
  27.2 8.7 %collective-permute-start.9 = (bf16[272,128]{1,0:T(8,128)(2,1)S(1)}, bf16[272,128]{1,0:T(8,128)(2,1)S(1)}, u32[]{:S(2)}, u32[]{:S(2)}) collective-permute-start(bf16[272,128]{1,0:T(8,128)(2,1)S(1)} %get-tuple-element.44), channel_id=1, source_target_pairs={{0,8},{4,12},{8,0},{12,4},{1,9},{5,13},{9,1},{13,5},{2,10},{6,14},... | collective-permute-start | bytes 208904 | tf_op jit(solution)/shard_map/ppermute | solution.py:606
  28.4 6.0 %collective-permute-start.8 = (bf16[264,128]{1,0:T(8,128)(2,1)S(1)}, bf16[264,128]{1,0:T(8,128)(2,1)S(1)}, u32[]{:S(2)}, u32[]{:S(2)}) collective-permute-start(bf16[264,128]{1,0:T(8,128)(2,1)S(1)} %get-tuple-element.43), channel_id=1, source_target_pairs={{0,12},{4,0},{8,4},{12,8},{1,13},{5,1},{9,5},{13,9},{2,14},{6,2},{... | collective-permute-start | bytes 202760 | tf_op jit(solution)/shard_map/ppermute | solution.py:606
  29.7 6.1 %collective-permute-start.10 = (bf16[264,128]{1,0:T(8,128)(2,1)S(1)}, bf16[264,128]{1,0:T(8,128)(2,1)S(1)}, u32[]{:S(2)}, u32[]{:S(2)}) collective-permute-start(bf16[264,128]{1,0:T(8,128)(2,1)S(1)} %get-tuple-element.45), channel_id=1, source_target_pairs={{0,4},{4,8},{8,12},{12,0},{1,5},{5,9},{9,13},{13,1},{2,6},{6,10},{... | collective-permute-start | bytes 202760 | tf_op jit(solution)/shard_map/ppermute | solution.py:606

commit v6 on v5

--- a/solution.py
+++ b/solution.py
@@ -149,8 +149,8 @@
 SHARD = SCORE_ROW + 2 * PAD
 AHEAD = 4
 HEAD = 6
-SPARE = 16
-JOINED_SPARE = 48
+SPARE = 0
+JOINED_SPARE = 64
 BF = jnp.bfloat16
 F32 = jnp.float32
 
@@ -201,9 +201,7 @@
                 (c_hbm, c_ref),
                 (off_hbm, off_ref),
                 (score_hbm, score_ref),
-                (w_hbm, mw1.at[0:SCORE_ROW]),
                 (w_hbm, mw2.at[0:SCORE_ROW]),
-                (w_hbm, mw3.at[0:SCORE_ROW]),
             )
         )
     ]
@@ -248,8 +246,9 @@
             moved = pltpu.roll(c_ref[0, 0:PAD, before].astype(F32), HEAD, 0)
             head = jnp.where(tile_row < HEAD, x_ref[0, 0:PAD, before].astype(F32), moved)
             mw3[appended(half, j), :] = head.astype(BF)
-    for copy in copies[4:]:
-        copy.wait()
+    copies[4].wait()
+    for ref in (mw1, mw3):
+        ref[0:SCORE_ROW, :] = mw2[0:SCORE_ROW, :]
 
 
 def join_kernel(w0, w1, w2, w3, joined, halo_own, halo_flip):
@@ -366,7 +365,14 @@
     return jnp.concatenate(inner + logit, axis=0)
 
 
-def hidden_kernel(files, mine_ref, other_ref, wm_ref, wt_ref, h_out, l_out, r_out):
+def own_window_kernel(files, message, out_ref):
+    since, _ = row_info(message, files, 0, message_rows(message))
+    none = jnp.zeros((PAD, GROUP_WIDTH), F32)
+    for j in range(SLOTS):
+        out_ref[j] = jnp.concatenate(windows_of(message, none, j, since), axis=1)
+
+
+def hidden_kernel(files, own_win, mine_ref, other_ref, wm_ref, wt_ref, h_out, l_out, r_out):
     messages = (mine_ref, other_ref)
     rows = h_out.shape[1]
     pairs = rows // 2
@@ -380,7 +386,10 @@
         score = jnp.where(row == AHEAD, jnp.broadcast_to(score[0:1], row.shape), 0.0)
         for stream in range(2):
             since, valid = infos[stream]
-            win = jnp.concatenate(windows_of(messages[stream], none, j, since), axis=1)
+            if stream == 0:
+                win = own_win[j]
+            else:
+                win = jnp.concatenate(windows_of(messages[stream], none, j, since), axis=1)
             hidden = jnp.dot(win, kernel, preferred_element_type=F32)
             h_out[stream, :, lanes(j)] = hidden * valid
             cot = messages[stream][rows : rows + pairs, lanes(j)]
@@ -571,11 +580,14 @@
     return copies
 
 
-def finish_kernel(kept_ref, got_ref, z1, z2, z3, x_got_ref, x_hbm,
-                  x_out, grad_out, score_out, grad_ref, score_ref, sems):
+def place_kernel(x_got_ref, x_hbm, x_out, sems):
     del x_hbm
+    for copy in half_copies(x_got_ref, x_out, 1 - lax.axis_index("dp"), sems):
+        copy.wait()
+
+
+def finish_kernel(kept_ref, got_ref, z1, z2, z3, grad_out, score_out, grad_ref, score_ref, sems):
     f = lax.axis_index("fsdp")
-    copies = half_copies(x_got_ref, x_out, 1 - lax.axis_index("dp"), sems)
     total = kept_ref[0 : SCORE_ROW + PAD, :] + got_ref[0 : SCORE_ROW + PAD, :]
     grad, score = total[0:SCORE_ROW], total[SCORE_ROW:]
     for ref in (z1, z2, z3):
@@ -583,15 +595,15 @@
         pair = ref[SCORE_ROW:HALO_ROW, :].astype(F32)
         score = score + jnp.sum(pair, axis=0, keepdims=True)
     grad_ref[...] = grad
-    copy_grad = pltpu.make_async_copy(grad_ref, grad_out, sems.at[SLOTS])
+    copy_grad = pltpu.make_async_copy(grad_ref, grad_out, sems.at[0])
     copy_grad.start()
     half = GROUP_WIDTH // 2
     score_ref[...] = jnp.where(
         jnp.full((1, half), f, jnp.int32) == 0, score[0:1, :half], score[0:1, half:]
     )
-    copy_score = pltpu.make_async_copy(score_ref, score_out, sems.at[SLOTS + 1])
+    copy_score = pltpu.make_async_copy(score_ref, score_out, sems.at[1])
     copy_score.start()
-    for copy in copies + [copy_grad, copy_score]:
+    for copy in (copy_grad, copy_score):
         copy.wait()
 
 
@@ -620,7 +632,7 @@
             pltpu.VMEM(inputs.shape, BF),
             pltpu.VMEM(cotangent.shape, BF),
             pltpu.VMEM((1, score_weight.shape[0]), BF),
-            pltpu.SemaphoreType.DMA((7,)),
+            pltpu.SemaphoreType.DMA((5,)),
         ),
         hbm=5,
     )(*(pltpu.with_memory_space_constraint(v, pltpu.HBM) for v in (offsets, inputs, cotangent, conv_weight, score_weight.reshape(1, -1))), lengths.reshape(1, 1))
@@ -631,11 +643,15 @@
     )(mw2, cycle(mw1, 1), cycle(mw2, 2), cycle(mw3, 3))
     halo_other = flip(halo_other, "dp")
     shards = (kernel_mine, flip(kernel_mine, "fsdp"))
+    own_windows = call(
+        functools.partial(own_window_kernel, files),
+        shape((SLOTS, rows, KERNEL * GROUP_WIDTH), BF),
+    )(mine)
     left = shape((2, pairs + PAD, HALF), BF)
     sums = shape((2, 16, GROUP_WIDTH), F32)
     hidden, left_main, partial = call(
         functools.partial(hidden_kernel, files), (shape((2, rows, HALF), F32), left, sums)
-    )(mine, other, *shards)
+    )(own_windows, mine, other, *shards)
     edge_hidden, left, partial = call(
         functools.partial(edge_hidden_kernel, files),
         (shape((2, 2 * PAD, HALF), F32), left, sums),
@@ -676,23 +692,30 @@
         compiler_params=params,
         cost_estimate=pl.CostEstimate(flops=0, transcendentals=0, bytes_accessed=4 * 1024 * 1024),
     )(hg, hg_ahead, mine, *shards)
-    input_grad, kernel_grad, score_grad = pl.pallas_call(
+    input_grad = pl.pallas_call(
+        place_kernel,
+        out_shape=shape(inputs.shape, BF),
+        in_specs=[vmem, hbm],
+        out_specs=hbm,
+        scratch_shapes=[pltpu.SemaphoreType.DMA((SLOTS,))],
+        input_output_aliases={1: 0},
+        compiler_params=params,
+    )(x_got, input_grad)
+    kernel_grad, score_grad = pl.pallas_call(
         finish_kernel,
         out_shape=(
-            shape(inputs.shape, BF),
             shape((SCORE_ROW, GROUP_WIDTH), F32),
             shape((1, GROUP_WIDTH // 2), F32),
         ),
-        in_specs=[vmem] * 6 + [hbm],
-        out_specs=(hbm, hbm, hbm),
+        in_specs=[vmem] * 5,
+        out_specs=(hbm, hbm),
         scratch_shapes=[
             pltpu.VMEM((SCORE_ROW, GROUP_WIDTH), F32),
             pltpu.VMEM((1, GROUP_WIDTH // 2), F32),
-            pltpu.SemaphoreType.DMA((SLOTS + 2,)),
+            pltpu.SemaphoreType.DMA((2,)),
         ],
-        input_output_aliases={6: 0},
         compiler_params=params,
-    )(kept, got, *final, x_got, input_grad)
+    )(kept, got, *final)
     return (input_grad, kernel_grad, score_grad.reshape(-1))
 
 

time: 36.8 us -> 36.5 us (level)
  waiting for transfers between devices: 13 us -> 10.5 us
  starting transfers between devices: 13.9 us -> 15.4 us
  Pallas kernels: 8.47 us -> 9.15 us
    ppermute x6, starting transfers between devices: 4.6 us -> 6.46 us  [flip(): return lax.ppermute(value, axis, [(0, 1), (1, 0)])]
    ppermute x6, waiting for transfers between devices: 6.83 us -> 5.41 us  [cycle(): lax.ppermute(value, 'seq', [(i, (i + by) % SLOTS) for i in range(SLOTS)])]
    ppermute x6, waiting for transfers between devices: 6.17 us -> 5.09 us  [flip(): return lax.ppermute(value, axis, [(0, 1), (1, 0)])]
    pallas_call x1 -> x2, Pallas kernels: 0.81 us -> 1.44 us  [the longest x1 0.72 us: per_device_paired(): pl.pallas_call(finish_kernel, out_shape=(shape((SCORE_ROW, GROUP_WIDTH),...]
    pallas_call x8 -> x9, Pallas kernels: 6.23 us -> 6.29 us  [run(): pl.pallas_call(body, out_shape=out_shape, in_specs=specs, out_specs=jax.t...]
  transfers between devices with their start and end apart: 12 -> 12, of which waited for: 7 -> 5; matrix products, arithmetic and copies ran while one was open for 0% -> 0% of each run, Pallas kernels for 12% -> 14%
where the time goes in v6:
time: 36.5 us; the launch traced here: 36.4 us
  starting transfers between devices  15.4 us (42%)
  waiting for transfers between devices  10.5 us (29%)
  Pallas kernels  9.15 us (25%)
  between operations  1.39 us (4%)
    ppermute x6, starting transfers between devices, cycle(): lax.ppermute(value, 'seq', [(i, (i + by) % SLOTS) for i in range(SLOTS)])  8.9 us
    ppermute x6, starting transfers between devices, flip(): return lax.ppermute(value, axis, [(0, 1), (1, 0)])  6.46 us
    pallas_call x9, Pallas kernels, run(): pl.pallas_call(body, out_shape=out_shape, in_specs=specs, out_specs=jax.t...  6.29 us
    ppermute x6, waiting for transfers between devices, cycle(): lax.ppermute(value, 'seq', [(i, (i + by) % SLOTS) for i in range(SLOTS)])  5.41 us
    ppermute x6, waiting for transfers between devices, flip(): return lax.ppermute(value, axis, [(0, 1), (1, 0)])  5.09 us
    pallas_call x1, Pallas kernels, per_device_paired(): pl.pallas_call(functools.partial(own_kernel, files), out_shape=shape(inpu...  1.41 us
  transfers between devices with their start and end apart: 12, of which 5 were waited for; matrix products, arithmetic and copies ran while one was open for 0% of the time, Pallas kernels for 14%

profile of v6, /device:TPU:0, one launch (start us, length us, event | category | flops | bytes accessed | tf_op | source)
XLA Modules:
  0.0 36.4 jit_solution(6391578910111060844)
XLA Ops:
  1.3 1.3 %shard_map.85 = (bf16[368,512]{1,0:T(8,128)(2,1)S(1)}, bf16[368,512]{1,0:T(8,128)(2,1)S(1)}, bf16[328,128]{1,0:T(8,128)(2,1)S(1)}, bf16[264,128]{1,0:T(8,128)(2,1)S(1)}, bf16[328,128]{1,0:T(8,128)(2,1)S(1)}) custom-call(s32[1,16]{1,0:T(1,128)} %off_hbm.1, bf16[1,240,1024]{2,1,0:T(8,128)(2,1)} %x_hbm.1, bf16[1,120,1024]{2,1,0:T(8,128)(2,1)} %c_hbm.1, ...), custom_call_target="tpu_custom_call" | custom-call | tf_op jit(solution)/shard_map/pallas_call | solution.py:174
  2.6 3.1 %collective-permute-start.1 = (bf16[328,128]{1,0:T(8,128)(2,1)S(1)}, bf16[328,128]{1,0:T(8,128)(2,1)S(1)}, u32[]{:S(2)}, u32[]{:S(2)}) collective-permute-start(bf16[328,128]{1,0:T(8,128)(2,1)S(1)} %get-tuple-element.29), channel_id=1, source_target_pairs={{0,4},{4,8},{8,12},{12,0},{1,5},{5,9},{9,13},{13,1},{2,6},{6,10},{... | collective-permute-start | bytes 251912 | tf_op jit(solution)/shard_map/ppermute | solution.py:618
  5.7 2.1 %collective-permute-start.3 = (bf16[328,128]{1,0:T(8,128)(2,1)S(1)}, bf16[328,128]{1,0:T(8,128)(2,1)S(1)}, u32[]{:S(2)}, u32[]{:S(2)}) collective-permute-start(bf16[328,128]{1,0:T(8,128)(2,1)S(1)} %get-tuple-element.30), channel_id=1, source_target_pairs={{0,12},{4,0},{8,4},{12,8},{1,13},{5,1},{9,5},{13,9},{2,14},{6,2},{... | collective-permute-start | bytes 251912 | tf_op jit(solution)/shard_map/ppermute | solution.py:618
  7.8 1.6 %collective-permute-start = (bf16[368,512]{1,0:T(8,128)(2,1)S(1)}, bf16[368,512]{1,0:T(8,128)(2,1)S(1)}, u32[]{:S(2)}, u32[]{:S(2)}) collective-permute-start(bf16[368,512]{1,0:T(8,128)(2,1)S(1)} %get-tuple-element.27), channel_id=1, source_target_pairs={{0,2},{2,0},{1,3},{3,1},{4,6},{6,4},{5,7},{7,5},{8,10},{10,8},{9,1... | collective-permute-start | bytes 1130504 | tf_op jit(solution)/shard_map/ppermute | solution.py:615
  9.4 0.8 %collective-permute-start.2 = (bf16[264,128]{1,0:T(8,128)(2,1)S(1)}, bf16[264,128]{1,0:T(8,128)(2,1)S(1)}, u32[]{:S(2)}, u32[]{:S(2)}) collective-permute-start(bf16[264,128]{1,0:T(8,128)(2,1)S(1)} %get-tuple-element.28.w0), channel_id=1, source_target_pairs={{0,8},{4,12},{8,0},{12,4},{1,9},{5,13},{9,1},{13,5},{2,10},{6,14},... | collective-permute-start | bytes 202760 | tf_op jit(solution)/shard_map/ppermute | solution.py:618
  10.2 4.7 %collective-permute-done.2.w2 = bf16[264,128]{1,0:T(8,128)(2,1)S(1)} collective-permute-done((bf16[264,128]{1,0:T(8,128)(2,1)S(1)}, bf16[264,128]{1,0:T(8,128)(2,1)S(1)}, u32[]{:S(2)}, u32[]{:S(2)}) %collective-permute-start.2) | collective-permute-done | bytes 67616 | tf_op jit(solution)/shard_map/ppermute | solution.py:618
  15.0 1.6 %collective-permute-start.4 = (bf16[16,512]{1,0:T(8,128)(2,1)S(1)}, bf16[16,512]{1,0:T(8,128)(2,1)S(1)}, u32[]{:S(2)}, u32[]{:S(2)}) collective-permute-start(bf16[16,512]{1,0:T(8,128)(2,1)S(1)} %get-tuple-element.32), channel_id=1, source_target_pairs={{0,2},{2,0},{1,3},{3,1},{4,6},{6,4},{5,7},{7,5},{8,10},{10,8},{9,1... | collective-permute-start | bytes 49160 | tf_op jit(solution)/shard_map/ppermute | solution.py:615
  16.8 1.2 %collective-permute-done.other_ref = bf16[368,512]{1,0:T(8,128)(2,1)S(1)} collective-permute-done((bf16[368,512]{1,0:T(8,128)(2,1)S(1)}, bf16[368,512]{1,0:T(8,128)(2,1)S(1)}, u32[]{:S(2)}, u32[]{:S(2)}) %collective-permute-start) | collective-permute-done | bytes 376864 | tf_op jit(solution)/shard_map/ppermute | solution.py:615
  18.0 1.3 %shard_map.88 = (f32[2,240,512]{2,1,0:T(8,128)S(1)}, bf16[2,128,512]{2,1,0:T(8,128)(2,1)S(1)}, f32[2,16,128]{2,1,0:T(8,128)S(1)}) custom-call(bf16[4,240,512]{2,1,0:T(8,128)(2,1)S(1)} %shard_map.87.own_win, bf16[368,512]{1,0:T(8,128)(2,1)S(1)} %get-tuple-element.26.message.mine_ref, bf16[368,512]{1,0:T(8,128)(2,1)S(1)} %collective-permute-done.other_ref, ...), custom_call_target="tpu_custom_call" | custom-call | tf_op jit(solution)/shard_map/pallas_call | solution.py:174
  19.3 0.5 %shard_map.89 = (f32[2,16,512]{2,1,0:T(8,128)S(1)}, bf16[2,128,512]{2,1,0:T(8,128)(2,1)S(1)}, f32[2,16,128]{2,1,0:T(8,128)S(1)}) custom-call(bf16[368,512]{1,0:T(8,128)(2,1)S(1)} %get-tuple-element.26.message.mine_ref, bf16[368,512]{1,0:T(8,128)(2,1)S(1)} %collective-permute-done.other_ref, bf16[16,512]{1,0:T(8,128)(2,1)S(1)} %get-tuple-element.31.own_halo, ...), custom_call_target="tpu_custom_call" | custom-call | tf_op jit(solution)/shard_map/pallas_call | solution.py:174
  19.9 1.6 %collective-permute-start.6 = (f32[2,16,128]{2,1,0:T(8,128)S(1)}, f32[2,16,128]{2,1,0:T(8,128)S(1)}, u32[]{:S(2)}, u32[]{:S(2)}) collective-permute-start(f32[2,16,128]{2,1,0:T(8,128)S(1)} %get-tuple-element.36.after_ref.r_ref), channel_id=1, source_target_pairs={{0,2},{2,0},{1,3},{3,1},{4,6},{6,4},{5,7},{7,5},{8,10},{10,8},{9,1... | collective-permute-start | bytes 49160 | tf_op jit(solution)/shard_map/ppermute | solution.py:615
  21.4 0.8 %shard_map.90.win_ref = bf16[4,512,512]{2,1,0:T(8,128)(2,1)S(1)} custom-call(bf16[368,512]{1,0:T(8,128)(2,1)S(1)} %get-tuple-element.26.message.mine_ref, bf16[368,512]{1,0:T(8,128)(2,1)S(1)} %collective-permute-done.other_ref, bf16[16,512]{1,0:T(8,128)(2,1)S(1)} %get-tuple-element.31.own_halo, bf16[16,512]{1,0:T(8,128)(2,1)S(1)} %collective-permute-done.4.other_halo, ...), custom_call_target="tpu_custom_call" | custom-call | bytes 2097152 | tf_op jit(solution)/shard_map/pallas_call | solution.py:174
  22.2 1.5 %collective-permute-done.6.rr_ref = f32[2,16,128]{2,1,0:T(8,128)S(1)} collective-permute-done((f32[2,16,128]{2,1,0:T(8,128)S(1)}, f32[2,16,128]{2,1,0:T(8,128)S(1)}, u32[]{:S(2)}, u32[]{:S(2)}) %collective-permute-start.6) | collective-permute-done | bytes 16416 | tf_op jit(solution)/shard_map/ppermute | solution.py:615
  23.7 1.3 %shard_map.91 = (bf16[2,240,512]{2,1,0:T(8,128)(2,1)S(1)}, bf16[2,16,512]{2,1,0:T(8,128)(2,1)S(1)}, f32[1056,128]{1,0:T(8,128)S(1)}, f32[1056,128]{1,0:T(8,128)S(1)}) custom-call(bf16[368,512]{1,0:T(8,128)(2,1)S(1)} %get-tuple-element.26.message.mine_ref, bf16[368,512]{1,0:T(8,128)(2,1)S(1)} %collective-permute-done.other_ref, ...), custom_call_target="tpu_custom_call" | custom-call | tf_op jit(solution)/shard_map/pallas_call | solution.py:174
  25.1 0.7 %shard_map.92 = bf16[240,512]{1,0:T(8,128)(2,1)S(1)} custom-call(bf16[2,240,512]{2,1,0:T(8,128)(2,1)S(1)} %get-tuple-element.40.hg_ref, bf16[2,16,512]{2,1,0:T(8,128)(2,1)S(1)} %get-tuple-element.41.hx_ref, bf16[368,512]{1,0:T(8,128)(2,1)S(1)} %collective-permute-done.other_ref, bf16[1152,128]{1,0:T(8,128)(2,1)S(1)} %get-tuple-element.33.wm_ref, ...), custom_call_target="tpu_custom_call" | custom-call | tf_op jit(solution)/shard_map/pallas_call | solution.py:174
  25.8 1.6 %collective-permute-start.7 = (bf16[240,512]{1,0:T(8,128)(2,1)S(1)}, bf16[240,512]{1,0:T(8,128)(2,1)S(1)}, u32[]{:S(2)}, u32[]{:S(2)}) collective-permute-start(bf16[240,512]{1,0:T(8,128)(2,1)S(1)} %shard_map.92), channel_id=1, source_target_pairs={{0,2},{2,0},{1,3},{3,1},{4,6},{6,4},{5,7},{7,5},{8,10},{10,8},{9,1... | collective-permute-start | bytes 737288 | tf_op jit(solution)/shard_map/ppermute | solution.py:615
  27.4 0.9 %collective-permute-start.10 = (bf16[272,128]{1,0:T(8,128)(2,1)S(1)}, bf16[272,128]{1,0:T(8,128)(2,1)S(1)}, u32[]{:S(2)}, u32[]{:S(2)}) collective-permute-start(bf16[272,128]{1,0:T(8,128)(2,1)S(1)} %get-tuple-element.45), channel_id=1, source_target_pairs={{0,8},{4,12},{8,0},{12,4},{1,9},{5,13},{9,1},{13,5},{2,10},{6,14},... | collective-permute-start | bytes 208904 | tf_op jit(solution)/shard_map/ppermute | solution.py:618
  28.3 1.2 %collective-permute-start.9 = (bf16[264,128]{1,0:T(8,128)(2,1)S(1)}, bf16[264,128]{1,0:T(8,128)(2,1)S(1)}, u32[]{:S(2)}, u32[]{:S(2)}) collective-permute-start(bf16[264,128]{1,0:T(8,128)(2,1)S(1)} %get-tuple-element.44), channel_id=1, source_target_pairs={{0,12},{4,0},{8,4},{12,8},{1,13},{5,1},{9,5},{13,9},{2,14},{6,2},{... | collective-permute-start | bytes 202760 | tf_op jit(solution)/shard_map/ppermute | solution.py:618
  29.5 0.9 %collective-permute-start.11 = (bf16[264,128]{1,0:T(8,128)(2,1)S(1)}, bf16[264,128]{1,0:T(8,128)(2,1)S(1)}, u32[]{:S(2)}, u32[]{:S(2)}) collective-permute-start(bf16[264,128]{1,0:T(8,128)(2,1)S(1)} %get-tuple-element.46), channel_id=1, source_target_pairs={{0,4},{4,8},{8,12},{12,0},{1,5},{5,9},{9,13},{13,1},{2,6},{6,10},{... | collective-permute-start | bytes 202760 | tf_op jit(solution)/shard_map/ppermute | solution.py:618
  30.3 1.4 %shard_map.93.x_hbm = bf16[1,240,1024]{2,1,0:T(8,128)(2,1)} custom-call(bf16[2,240,512]{2,1,0:T(8,128)(2,1)S(1)} %get-tuple-element.40.hg_ref, bf16[2,16,512]{2,1,0:T(8,128)(2,1)S(1)} %get-tuple-element.41.hx_ref, bf16[368,512]{1,0:T(8,128)(2,1)S(1)} %get-tuple-element.26.message.mine_ref, bf16[1152,128]{1,0:T(8,128)(2,1)S(1)} %get-tuple-element.33.wm_ref, ...), custom_call_target="tpu_custom_call" | custom-call | bytes 4194304 | tf_op jit(solution)/shard_map/pallas_call | solution.py:686
  31.7 2.5 %collective-permute-done.7.x_got_ref = bf16[240,512]{1,0:T(8,128)(2,1)S(1)} collective-permute-done((bf16[240,512]{1,0:T(8,128)(2,1)S(1)}, bf16[240,512]{1,0:T(8,128)(2,1)S(1)}, u32[]{:S(2)}, u32[]{:S(2)}) %collective-permute-start.7) | collective-permute-done | bytes 245792 | tf_op jit(solution)/shard_map/ppermute | solution.py:615
  34.2 0.7 %shard_map.94 = bf16[1,240,1024]{2,1,0:T(8,128)(2,1)} custom-call(bf16[240,512]{1,0:T(8,128)(2,1)S(1)} %collective-permute-done.7.x_got_ref, bf16[1,240,1024]{2,1,0:T(8,128)(2,1)} %shard_map.93.x_hbm), custom_call_target="tpu_custom_call", output_to_operand_aliasing={{}: (1, {})} | custom-call | tf_op jit(solution)/shard_map/pallas_call | solution.py:695
  34.9 0.7 %collective-permute-done.11.z3 = bf16[264,128]{1,0:T(8,128)(2,1)S(1)} collective-permute-done((bf16[264,128]{1,0:T(8,128)(2,1)S(1)}, bf16[264,128]{1,0:T(8,128)(2,1)S(1)}, u32[]{:S(2)}, u32[]{:S(2)}) %collective-permute-start.11) | collective-permute-done | bytes 67616 | tf_op jit(solution)/shard_map/ppermute | solution.py:618
  35.7 0.7 %shard_map.96 = (f32[256,128]{1,0:T(8,128)}, f32[1,64]{1,0:T(1,128)}) custom-call(f32[1056,128]{1,0:T(8,128)S(1)} %get-tuple-element.42.kept_ref, f32[1056,128]{1,0:T(8,128)S(1)} %collective-permute-done.8.got_ref, bf16[264,128]{1,0:T(8,128)(2,1)S(1)} %collective-permute-done.9.z1, bf16[272,128]{1,0:T(8,128)(2,1)S(1)} %collective-permute-done.10.z2, ...), custom_call_target="tpu_custom_call" | custom-call | tf_op jit(solution)/shard_map/pallas_call | solution.py:704
  (12 shorter events, 0.5 us)
Async XLA Ops:
  2.6 12.3 %collective-permute-start.1 = (bf16[328,128]{1,0:T(8,128)(2,1)S(1)}, bf16[328,128]{1,0:T(8,128)(2,1)S(1)}, u32[]{:S(2)}, u32[]{:S(2)}) collective-permute-start(bf16[328,128]{1,0:T(8,128)(2,1)S(1)} %get-tuple-element.29), channel_id=1, source_target_pairs={{0,4},{4,8},{8,12},{12,0},{1,5},{5,9},{9,13},{13,1},{2,6},{6,10},{... | collective-permute-start | bytes 251912 | tf_op jit(solution)/shard_map/ppermute | solution.py:618
  5.7 9.2 %collective-permute-start.3 = (bf16[328,128]{1,0:T(8,128)(2,1)S(1)}, bf16[328,128]{1,0:T(8,128)(2,1)S(1)}, u32[]{:S(2)}, u32[]{:S(2)}) collective-permute-start(bf16[328,128]{1,0:T(8,128)(2,1)S(1)} %get-tuple-element.30), channel_id=1, source_target_pairs={{0,12},{4,0},{8,4},{12,8},{1,13},{5,1},{9,5},{13,9},{2,14},{6,2},{... | collective-permute-start | bytes 251912 | tf_op jit(solution)/shard_map/ppermute | solution.py:618
  7.8 10.2 %collective-permute-start = (bf16[368,512]{1,0:T(8,128)(2,1)S(1)}, bf16[368,512]{1,0:T(8,128)(2,1)S(1)}, u32[]{:S(2)}, u32[]{:S(2)}) collective-permute-start(bf16[368,512]{1,0:T(8,128)(2,1)S(1)} %get-tuple-element.27), channel_id=1, source_target_pairs={{0,2},{2,0},{1,3},{3,1},{4,6},{6,4},{5,7},{7,5},{8,10},{10,8},{9,1... | collective-permute-start | bytes 1130504 | tf_op jit(solution)/shard_map/ppermute | solution.py:615
  9.4 5.5 %collective-permute-start.2 = (bf16[264,128]{1,0:T(8,128)(2,1)S(1)}, bf16[264,128]{1,0:T(8,128)(2,1)S(1)}, u32[]{:S(2)}, u32[]{:S(2)}) collective-permute-start(bf16[264,128]{1,0:T(8,128)(2,1)S(1)} %get-tuple-element.28.w0), channel_id=1, source_target_pairs={{0,8},{4,12},{8,0},{12,4},{1,9},{5,13},{9,1},{13,5},{2,10},{6,14},... | collective-permute-start | bytes 202760 | tf_op jit(solution)/shard_map/ppermute | solution.py:618
  14.9 3.1 %collective-permute-start.5 = (bf16[1152,128]{1,0:T(8,128)(2,1)S(1)}, bf16[1152,128]{1,0:T(8,128)(2,1)S(1)}, u32[]{:S(2)}, u32[]{:S(2)}) collective-permute-start(bf16[1152,128]{1,0:T(8,128)(2,1)S(1)} %get-tuple-element.33.wm_ref), channel_id=1, source_target_pairs={{0,1},{1,0},{2,3},{3,2},{4,5},{5,4},{6,7},{7,6},{8,9},{9,8},{10,11... | collective-permute-start | bytes 884744 | tf_op jit(solution)/shard_map/ppermute | solution.py:615
  15.0 4.3 %collective-permute-start.4 = (bf16[16,512]{1,0:T(8,128)(2,1)S(1)}, bf16[16,512]{1,0:T(8,128)(2,1)S(1)}, u32[]{:S(2)}, u32[]{:S(2)}) collective-permute-start(bf16[16,512]{1,0:T(8,128)(2,1)S(1)} %get-tuple-element.32), channel_id=1, source_target_pairs={{0,2},{2,0},{1,3},{3,1},{4,6},{6,4},{5,7},{7,5},{8,10},{10,8},{9,1... | collective-permute-start | bytes 49160 | tf_op jit(solution)/shard_map/ppermute | solution.py:615
  19.9 3.8 %collective-permute-start.6 = (f32[2,16,128]{2,1,0:T(8,128)S(1)}, f32[2,16,128]{2,1,0:T(8,128)S(1)}, u32[]{:S(2)}, u32[]{:S(2)}) collective-permute-start(f32[2,16,128]{2,1,0:T(8,128)S(1)} %get-tuple-element.36.after_ref.r_ref), channel_id=1, source_target_pairs={{0,2},{2,0},{1,3},{3,1},{4,6},{6,4},{5,7},{7,5},{8,10},{10,8},{9,1... | collective-permute-start | bytes 49160 | tf_op jit(solution)/shard_map/ppermute | solution.py:615
  25.0 2.3 %collective-permute-start.8 = (f32[1056,128]{1,0:T(8,128)S(1)}, f32[1056,128]{1,0:T(8,128)S(1)}, u32[]{:S(2)}, u32[]{:S(2)}) collective-permute-start(f32[1056,128]{1,0:T(8,128)S(1)} %get-tuple-element.43), channel_id=1, source_target_pairs={{0,1},{1,0},{2,3},{3,2},{4,5},{5,4},{6,7},{7,6},{8,9},{9,8},{10,11... | collective-permute-start | bytes 1622024 | tf_op jit(solution)/shard_map/ppermute | solution.py:615
  25.8 8.4 %collective-permute-start.7 = (bf16[240,512]{1,0:T(8,128)(2,1)S(1)}, bf16[240,512]{1,0:T(8,128)(2,1)S(1)}, u32[]{:S(2)}, u32[]{:S(2)}) collective-permute-start(bf16[240,512]{1,0:T(8,128)(2,1)S(1)} %shard_map.92), channel_id=1, source_target_pairs={{0,2},{2,0},{1,3},{3,1},{4,6},{6,4},{5,7},{7,5},{8,10},{10,8},{9,1... | collective-permute-start | bytes 737288 | tf_op jit(solution)/shard_map/ppermute | solution.py:615
  27.4 8.3 %collective-permute-start.10 = (bf16[272,128]{1,0:T(8,128)(2,1)S(1)}, bf16[272,128]{1,0:T(8,128)(2,1)S(1)}, u32[]{:S(2)}, u32[]{:S(2)}) collective-permute-start(bf16[272,128]{1,0:T(8,128)(2,1)S(1)} %get-tuple-element.45), channel_id=1, source_target_pairs={{0,8},{4,12},{8,0},{12,4},{1,9},{5,13},{9,1},{13,5},{2,10},{6,14},... | collective-permute-start | bytes 208904 | tf_op jit(solution)/shard_map/ppermute | solution.py:618
  28.3 6.6 %collective-permute-start.9 = (bf16[264,128]{1,0:T(8,128)(2,1)S(1)}, bf16[264,128]{1,0:T(8,128)(2,1)S(1)}, u32[]{:S(2)}, u32[]{:S(2)}) collective-permute-start(bf16[264,128]{1,0:T(8,128)(2,1)S(1)} %get-tuple-element.44), channel_id=1, source_target_pairs={{0,12},{4,0},{8,4},{12,8},{1,13},{5,1},{9,5},{13,9},{2,14},{6,2},{... | collective-permute-start | bytes 202760 | tf_op jit(solution)/shard_map/ppermute | solution.py:618
  29.5 6.2 %collective-permute-start.11 = (bf16[264,128]{1,0:T(8,128)(2,1)S(1)}, bf16[264,128]{1,0:T(8,128)(2,1)S(1)}, u32[]{:S(2)}, u32[]{:S(2)}) collective-permute-start(bf16[264,128]{1,0:T(8,128)(2,1)S(1)} %get-tuple-element.46), channel_id=1, source_target_pairs={{0,4},{4,8},{8,12},{12,0},{1,5},{5,9},{9,13},{13,1},{2,6},{6,10},{... | collective-permute-start | bytes 202760 | tf_op jit(solution)/shard_map/ppermute | solution.py:618
